TPU v7x, 256 devices: a whole 4x4x8 slice. The times are simulated.
256 devices in a mesh: tm: 64 (over z, x, y_lo), gz: 4 (over y_hi, core).
Axes of the slice: x: 4, y: 4 (y_hi: 2, y_lo: 2; y = y_hi * 2 + y_lo), z: 8, core: 2. Of those that a mesh axis runs over, the one named last changes fastest.
Arguments:
- source: float32 [128, 32, 32, 512], P('tm', None, None, 'gz'), may hold values from -8 to 8
- initial_guess: float32 [128, 32, 32, 512], P('tm', None, None, 'gz'), may hold values from -8 to 8
- diffusivity: float32 [32, 32, 512], P(None, None, 'gz'), may hold values from 0.25 to 2.5
Outputs:
- solution: float32 [128, 32, 32, 512], P('tm', None, None, 'gz')
- residual: float32 [128, 32, 32, 512], P('tm', None, None, 'gz')
All inputs are finite; a program needn't handle non-finite values.
Results may differ from a plain program's by a relative error of at most 0.00002.
Values sent between devices are 32-bit elements; how exact they have to be, the bound alone decides.
No kernel may reach another device: no remote copies, remote signals or barrier semaphores. Data moves between devices by JAX's collectives and lax.ppermute only.
A program may use at most 128 MiB of HBM per device.

v0:
```python
import jax
import jax.numpy as jnp
from jax import lax
from jax.sharding import PartitionSpec as P

LEVELS = 5
SWEEPS = 2
CSWEEPS = 4


damping = 0.8
base_coef = 8.0


def passed_along(block, axis, distance):
    devices = range(lax.axis_size(axis))
    route = [(i - distance, i) for i in devices if i - distance in devices]
    return lax.ppermute(block, axis, route)


def padded_2(block, sides, width):
    for axis, dim in sides:
        count = lax.axis_size(axis)
        forward = [(i, i + 1) for i in range(count - 1)]
        backward = [(target, source) for source, target in forward]
        low = lax.ppermute(
            lax.slice_in_dim(block, block.shape[dim] - width, None, axis=dim), axis, forward
        )
        high = lax.ppermute(lax.slice_in_dim(block, 0, width, axis=dim), axis, backward)
        block = jnp.concatenate([low, block, high], axis=dim)
    return block


def partner(block, axis, distance):
    count = lax.axis_size(axis)
    route = []
    for low in range(count):
        high = low | 1 << distance
        if high != low and high < count:
            route += [(low, high), (high, low)]
    return lax.ppermute(block, axis, route)


def neighbours(padded):
    beside = padded[:, 2:, 1:-1, 1:-1] + padded[:, :-2, 1:-1, 1:-1]
    beside = beside + padded[:, 1:-1, 2:, 1:-1] + padded[:, 1:-1, :-2, 1:-1]
    beside = beside + padded[:, 1:-1, 1:-1, 2:] + padded[:, 1:-1, 1:-1, :-2]
    return beside


def operate(values, diffusivity, time_coef, stride):
    earlier = passed_along(values[-1:], "tm", stride)
    before = jnp.concatenate([earlier, values[:-1]], axis=0)
    padded = padded_2(values, (("gz", 3),), 1)
    padded = jnp.pad(padded, ((0, 0), (1, 1), (1, 1), (0, 0)))
    return time_coef * (values - before) + diffusivity * (6.0 * values - neighbours(padded))


def smooth_single(values, target, diffusivity, time_coef, stride, sweep_count):
    scaled = damping / (time_coef + 6.0 * diffusivity)
    for sweep_num in range(sweep_count):
        values = values + scaled * (target - operate(values, diffusivity, time_coef, stride))
    return values


def smooth(values, target, diffusivity, time_coef, stride, sweep_count):
    return smooth_single(values, target, diffusivity, time_coef, stride, sweep_count)


def cycle(level_num, values, target, diffusivity, coeff_wide, stride):
    time_coef = base_coef / 2.0**level_num
    if level_num == LEVELS - 1:
        return smooth(values, target, diffusivity, time_coef, stride, CSWEEPS)
    values = smooth(values, target, diffusivity, time_coef, stride, SWEEPS)
    leftover = target - operate(values, diffusivity, time_coef, stride)
    if values.shape[0] > 1:
        coarse_res = (leftover[0::2] + leftover[1::2]) * 0.5
        correction = cycle(
            level_num + 1, jnp.zeros_like(coarse_res), coarse_res, diffusivity, coeff_wide, stride
        )
        values = values + jnp.repeat(correction, 2, axis=0)
    else:
        other_res = partner(leftover, "tm", stride.bit_length() - 1)
        coarse_res = (leftover + other_res) * 0.5
        correction = cycle(
            level_num + 1,
            jnp.zeros_like(coarse_res),
            coarse_res,
            diffusivity,
            coeff_wide,
            2 * stride,
        )
        values = values + correction
    return smooth(values, target, diffusivity, time_coef, stride, SWEEPS)


def body(source, initial_guess, diffusivity):
    solution = cycle(0, initial_guess, source, diffusivity, diffusivity, 1)
    residual = source - operate(solution, diffusivity, base_coef, 1)
    return (solution, residual)


def solution(mesh):
    placed = (P("tm", None, None, "gz"), P("tm", None, None, "gz"), P(None, None, "gz"))
    return jax.shard_map(
        body,
        mesh=mesh,
        in_specs=placed,
        out_specs=(P("tm", None, None, "gz"), P("tm", None, None, "gz")),
        check_vma=False,
    )
```

profile of v0, /device:TPU:3, one launch (start us, length us, event | category | flops | bytes accessed | tf_op | source)
XLA Modules:
  0.0 542.4 jit_solution(7175983873636543249)
XLA Ops:
  5.3 5.4 collective-permute-start.1
  21.8 5.9 %collective-permute-done = f32[1,32,32,128]{3,2,1,0:T(8,128)} collective-permute-done((f32[1,32,32,128]{3,2,1,0:T(8,128)}, f32[1,32,32,128]{3,2,1,0:T(8,128)}, u32[]{:S(2)}, u32[]{:S(2)}) %collective-permute-start) | collective-permute-done | bytes 524320 | tf_op jit(solution)/shard_map/ppermute | solution.py:18
  37.6 5.7 %collective-permute-start.4 = (f32[2,32,32,1]{2,1,3,0:T(8,128)S(1)}, f32[2,32,32,1]{2,1,3,0:T(8,128)S(1)}, u32[]{:S(2)}, u32[]{:S(2)}) collective-permute-start(f32[2,32,32,1]{2,1,3,0:T(8,128)S(1)} %copy.32), channel_id=1, source_target_pairs={{0,1},{1,2},{2,3},{4,5},{5,6},{6,7},{8,9},{9,10},{10,11},{12,13},{... | collective-permute-start | bytes 24584 | tf_op jit(solution)/shard_map/ppermute | solution.py:26
  46.6 5.1 collective-permute-start.10
  70.1 6.0 %collective-permute-start.7 = (f32[2,32,32,1]{2,1,3,0:T(8,128)S(1)}, f32[2,32,32,1]{2,1,3,0:T(8,128)S(1)}, u32[]{:S(2)}, u32[]{:S(2)}) collective-permute-start(f32[2,32,32,1]{2,1,3,0:T(8,128)S(1)} %copy.38), channel_id=1, source_target_pairs={{0,1},{1,2},{2,3},{4,5},{5,6},{6,7},{8,9},{9,10},{10,11},{12,13},{... | collective-permute-start | bytes 24584 | tf_op jit(solution)/shard_map/ppermute | solution.py:26
  99.0 6.4 %collective-permute-start.13 = (f32[1,32,32,1]{3,2,1,0:T(8,128)S(1)}, f32[1,32,32,1]{3,2,1,0:T(8,128)S(1)}, u32[]{:S(2)}, u32[]{:S(2)}) collective-permute-start(f32[1,32,32,1]{3,2,1,0:T(8,128)S(1)} %get-tuple-element.66), channel_id=1, source_target_pairs={{0,1},{1,2},{2,3},{4,5},{5,6},{6,7},{8,9},{9,10},{10,11},{12,13},{... | collective-permute-start | bytes 12296 | tf_op jit(solution)/shard_map/ppermute | solution.py:26
  107.3 6.6 %collective-permute-done.13 = f32[1,32,32,1]{3,2,1,0:T(8,128)S(1)} collective-permute-done((f32[1,32,32,1]{3,2,1,0:T(8,128)S(1)}, f32[1,32,32,1]{3,2,1,0:T(8,128)S(1)}, u32[]{:S(2)}, u32[]{:S(2)}) %collective-permute-start.13) | collective-permute-done | bytes 4128 | tf_op jit(solution)/shard_map/ppermute | solution.py:26
  113.9 4.9 collective-permute-done.14
  120.5 7.8 %collective-permute-start.15 = (f32[1,32,32,128]{3,2,1,0:T(8,128)S(1)}, f32[1,32,32,128]{3,2,1,0:T(8,128)S(1)}, u32[]{:S(2)}, u32[]{:S(2)}) collective-permute-start(f32[1,32,32,128]{3,2,1,0:T(8,128)S(1)} %fusion.176), channel_id=1, source_target_pairs={{0,4},{4,8},{8,12},{12,16},{16,20},{20,24},{24,28},{28,32},{32,36}... | collective-permute-start | bytes 1572872 | tf_op jit(solution)/shard_map/ppermute | solution.py:18
  133.1 5.6 %collective-permute-start.19 = (f32[1,32,32,128]{3,2,1,0:T(8,128)}, f32[1,32,32,128]{3,2,1,0:T(8,128)S(1)}, u32[]{:S(2)}, u32[]{:S(2)}) collective-permute-start(f32[1,32,32,128]{3,2,1,0:T(8,128)} %broadcast.101), channel_id=1, source_target_pairs={{0,8},{4,12},{8,16},{12,20},{16,24},{20,28},{24,32},{28,36},{32,40... | collective-permute-start | bytes 1572872 | tf_op jit(solution)/shard_map/ppermute | solution.py:18
  154.9 8.3 %collective-permute-start.20 = (f32[1,32,32,128]{3,2,1,0:T(8,128)S(1)}, f32[1,32,32,128]{3,2,1,0:T(8,128)S(1)}, u32[]{:S(2)}, u32[]{:S(2)}) collective-permute-start(f32[1,32,32,128]{3,2,1,0:T(8,128)S(1)} %get-tuple-element.8), channel_id=1, source_target_pairs={{0,8},{4,12},{8,16},{12,20},{16,24},{20,28},{24,32},{28,36},{32,40... | collective-permute-start | bytes 1572872 | tf_op jit(solution)/shard_map/ppermute | solution.py:18
  172.4 5.9 %collective-permute-done.22 = f32[1,32,32,1]{3,2,1,0:T(8,128)S(1)} collective-permute-done((f32[1,32,32,1]{3,2,1,0:T(8,128)S(1)}, f32[1,32,32,1]{3,2,1,0:T(8,128)S(1)}, u32[]{:S(2)}, u32[]{:S(2)}) %collective-permute-start.22) | collective-permute-done | bytes 4128 | tf_op jit(solution)/shard_map/ppermute | solution.py:29
  186.5 6.7 %collective-permute-start.27 = (f32[1,32,32,128]{3,2,1,0:T(8,128)}, f32[1,32,32,128]{3,2,1,0:T(8,128)S(1)}, u32[]{:S(2)}, u32[]{:S(2)}) collective-permute-start(f32[1,32,32,128]{3,2,1,0:T(8,128)} %broadcast.101), channel_id=1, source_target_pairs={{0,16},{4,20},{8,24},{12,28},{16,32},{20,36},{24,40},{28,44},{32,4... | collective-permute-start | bytes 1572872 | tf_op jit(solution)/shard_map/ppermute | solution.py:18
  199.4 5.9 %collective-permute-done.27 = f32[1,32,32,128]{3,2,1,0:T(8,128)S(1)} collective-permute-done((f32[1,32,32,128]{3,2,1,0:T(8,128)}, f32[1,32,32,128]{3,2,1,0:T(8,128)S(1)}, u32[]{:S(2)}, u32[]{:S(2)}) %collective-permute-start.27) | collective-permute-done | bytes 524320 | tf_op jit(solution)/shard_map/ppermute | solution.py:18
  205.3 13.6 %collective-permute-done.26 = f32[1,32,32,128]{3,2,1,0:T(8,128)S(1)} collective-permute-done((f32[1,32,32,128]{3,2,1,0:T(8,128)S(1)}, f32[1,32,32,128]{3,2,1,0:T(8,128)S(1)}, u32[]{:S(2)}, u32[]{:S(2)}) %collective-permute-start.26) | collective-permute-done | bytes 524320 | tf_op jit(solution)/shard_map/ppermute | solution.py:41
  230.6 5.9 %collective-permute-done.30 = f32[1,32,32,1]{3,2,1,0:T(8,128)S(1)} collective-permute-done((f32[1,32,32,1]{3,2,1,0:T(8,128)S(1)}, f32[1,32,32,1]{3,2,1,0:T(8,128)S(1)}, u32[]{:S(2)}, u32[]{:S(2)}) %collective-permute-start.30) | collective-permute-done | bytes 4128 | tf_op jit(solution)/shard_map/ppermute | solution.py:29
  238.2 5.6 %collective-permute-start.31 = (f32[1,32,32,128]{3,2,1,0:T(8,128)S(1)}, f32[1,32,32,128]{3,2,1,0:T(8,128)S(1)}, u32[]{:S(2)}, u32[]{:S(2)}) collective-permute-start(f32[1,32,32,128]{3,2,1,0:T(8,128)S(1)} %fusion.148), channel_id=1, source_target_pairs={{0,16},{4,20},{8,24},{12,28},{16,32},{20,36},{24,40},{28,44},{32,4... | collective-permute-start | bytes 1572872 | tf_op jit(solution)/shard_map/ppermute | solution.py:18
  252.1 5.9 %collective-permute-done.33 = f32[1,32,32,1]{3,2,1,0:T(8,128)S(1)} collective-permute-done((f32[1,32,32,1]{3,2,1,0:T(8,128)S(1)}, f32[1,32,32,1]{3,2,1,0:T(8,128)S(1)}, u32[]{:S(2)}, u32[]{:S(2)}) %collective-permute-start.33) | collective-permute-done | bytes 4128 | tf_op jit(solution)/shard_map/ppermute | solution.py:29
  263.8 7.5 %collective-permute-done.34 = f32[1,32,32,128]{3,2,1,0:T(8,128)S(1)} collective-permute-done((f32[1,32,32,128]{3,2,1,0:T(8,128)S(1)}, f32[1,32,32,128]{3,2,1,0:T(8,128)S(1)}, u32[]{:S(2)}, u32[]{:S(2)}) %collective-permute-start.34) | collective-permute-done | bytes 524320 | tf_op jit(solution)/shard_map/ppermute | solution.py:41
  271.6 7.3 %collective-permute-start.36 = (f32[1,32,32,128]{3,2,1,0:T(8,128)S(1)}, f32[1,32,32,128]{3,2,1,0:T(8,128)S(1)}, u32[]{:S(2)}, u32[]{:S(2)}) collective-permute-start(f32[1,32,32,128]{3,2,1,0:T(8,128)S(1)} %get-tuple-element.4), channel_id=1, source_target_pairs={{0,32},{4,36},{8,40},{12,44},{16,48},{20,52},{24,56},{28,60},{32,6... | collective-permute-start | bytes 1572872 | tf_op jit(solution)/shard_map/ppermute | solution.py:18
  287.1 5.9 %collective-permute-done.38 = f32[1,32,32,1]{3,2,1,0:T(8,128)S(1)} collective-permute-done((f32[1,32,32,1]{3,2,1,0:T(8,128)S(1)}, f32[1,32,32,1]{3,2,1,0:T(8,128)S(1)}, u32[]{:S(2)}, u32[]{:S(2)}) %collective-permute-start.38) | collective-permute-done | bytes 4128 | tf_op jit(solution)/shard_map/ppermute | solution.py:29
  305.5 5.9 %collective-permute-done.41 = f32[1,32,32,1]{3,2,1,0:T(8,128)S(1)} collective-permute-done((f32[1,32,32,1]{3,2,1,0:T(8,128)S(1)}, f32[1,32,32,1]{3,2,1,0:T(8,128)S(1)}, u32[]{:S(2)}, u32[]{:S(2)}) %collective-permute-start.41) | collective-permute-done | bytes 4128 | tf_op jit(solution)/shard_map/ppermute | solution.py:29
  324.8 5.9 %collective-permute-done.44 = f32[1,32,32,1]{3,2,1,0:T(8,128)S(1)} collective-permute-done((f32[1,32,32,1]{3,2,1,0:T(8,128)S(1)}, f32[1,32,32,1]{3,2,1,0:T(8,128)S(1)}, u32[]{:S(2)}, u32[]{:S(2)}) %collective-permute-start.44) | collective-permute-done | bytes 4128 | tf_op jit(solution)/shard_map/ppermute | solution.py:29
  345.4 5.9 %collective-permute-done.47 = f32[1,32,32,1]{3,2,1,0:T(8,128)S(1)} collective-permute-done((f32[1,32,32,1]{3,2,1,0:T(8,128)S(1)}, f32[1,32,32,1]{3,2,1,0:T(8,128)S(1)}, u32[]{:S(2)}, u32[]{:S(2)}) %collective-permute-start.47) | collective-permute-done | bytes 4128 | tf_op jit(solution)/shard_map/ppermute | solution.py:29
  363.2 5.9 %collective-permute-done.50 = f32[1,32,32,1]{3,2,1,0:T(8,128)S(1)} collective-permute-done((f32[1,32,32,1]{3,2,1,0:T(8,128)S(1)}, f32[1,32,32,1]{3,2,1,0:T(8,128)S(1)}, u32[]{:S(2)}, u32[]{:S(2)}) %collective-permute-start.50) | collective-permute-done | bytes 4128 | tf_op jit(solution)/shard_map/ppermute | solution.py:29
  383.3 5.9 %collective-permute-done.53 = f32[1,32,32,1]{3,2,1,0:T(8,128)S(1)} collective-permute-done((f32[1,32,32,1]{3,2,1,0:T(8,128)S(1)}, f32[1,32,32,1]{3,2,1,0:T(8,128)S(1)}, u32[]{:S(2)}, u32[]{:S(2)}) %collective-permute-start.53) | collective-permute-done | bytes 4128 | tf_op jit(solution)/shard_map/ppermute | solution.py:29
  401.9 9.6 %collective-permute-done.56 = f32[1,32,32,1]{3,2,1,0:T(8,128)S(1)} collective-permute-done((f32[1,32,32,1]{3,2,1,0:T(8,128)S(1)}, f32[1,32,32,1]{3,2,1,0:T(8,128)S(1)}, u32[]{:S(2)}, u32[]{:S(2)}) %collective-permute-start.56) | collective-permute-done | bytes 4128 | tf_op jit(solution)/shard_map/ppermute | solution.py:29
  421.3 7.6 %collective-permute-done.58 = f32[1,32,32,1]{3,2,1,0:T(8,128)S(1)} collective-permute-done((f32[1,32,32,1]{3,2,1,0:T(8,128)S(1)}, f32[1,32,32,1]{3,2,1,0:T(8,128)S(1)}, u32[]{:S(2)}, u32[]{:S(2)}) %collective-permute-start.58) | collective-permute-done | bytes 4128 | tf_op jit(solution)/shard_map/ppermute | solution.py:26
  428.9 6.3 %collective-permute-done.59 = f32[1,32,32,1]{3,2,1,0:T(8,128)S(1)} collective-permute-done((f32[1,32,32,1]{3,2,1,0:T(8,128)S(1)}, f32[1,32,32,1]{3,2,1,0:T(8,128)S(1)}, u32[]{:S(2)}, u32[]{:S(2)}) %collective-permute-start.59) | collective-permute-done | bytes 4128 | tf_op jit(solution)/shard_map/ppermute | solution.py:29
  444.7 6.9 %collective-permute-done.61 = f32[1,32,32,1]{3,2,1,0:T(8,128)S(1)} collective-permute-done((f32[1,32,32,1]{3,2,1,0:T(8,128)S(1)}, f32[1,32,32,1]{3,2,1,0:T(8,128)S(1)}, u32[]{:S(2)}, u32[]{:S(2)}) %collective-permute-start.61) | collective-permute-done | bytes 4128 | tf_op jit(solution)/shard_map/ppermute | solution.py:26
  457.9 9.3 %collective-permute-start.63 = (f32[1,32,32,128]{3,2,1,0:T(8,128)}, f32[1,32,32,128]{3,2,1,0:T(8,128)}, u32[]{:S(2)}, u32[]{:S(2)}) collective-permute-start(f32[1,32,32,128]{3,2,1,0:T(8,128)} %get-tuple-element.21), channel_id=1, source_target_pairs={{0,4},{4,8},{8,12},{12,16},{16,20},{20,24},{24,28},{28,32},{32,36}... | collective-permute-start | bytes 1572872 | tf_op jit(solution)/shard_map/ppermute | solution.py:18
  519.4 5.8 %collective-permute-start.70 = (f32[2,32,32,1]{2,1,3,0:T(8,128)S(1)}, f32[2,32,32,1]{2,1,3,0:T(8,128)S(1)}, u32[]{:S(2)}, u32[]{:S(2)}) collective-permute-start(f32[2,32,32,1]{2,1,3,0:T(8,128)S(1)} %copy.56), channel_id=1, source_target_pairs={{0,1},{1,2},{2,3},{4,5},{5,6},{6,7},{8,9},{9,10},{10,11},{12,13},{... | collective-permute-start | bytes 24584 | tf_op jit(solution)/shard_map/ppermute | solution.py:26
  (266 shorter events, 327.0 us)
Async XLA Ops:
  14.2 13.6 %collective-permute-start = (f32[1,32,32,128]{3,2,1,0:T(8,128)}, f32[1,32,32,128]{3,2,1,0:T(8,128)}, u32[]{:S(2)}, u32[]{:S(2)}) collective-permute-start(f32[1,32,32,128]{3,2,1,0:T(8,128)} %get-tuple-element.33), channel_id=1, source_target_pairs={{0,4},{4,8},{8,12},{12,16},{16,20},{20,24},{24,28},{28,32},{32,36}... | collective-permute-start | bytes 1572872 | tf_op jit(solution)/shard_map/ppermute | solution.py:18
  32.3 30.2 %collective-permute-start.3 = (f32[1,32,32,128]{3,2,1,0:T(8,128)}, f32[1,32,32,128]{3,2,1,0:T(8,128)}, u32[]{:S(2)}, u32[]{:S(2)}) collective-permute-start(f32[1,32,32,128]{3,2,1,0:T(8,128)} %get-tuple-element.29), channel_id=1, source_target_pairs={{0,4},{4,8},{8,12},{12,16},{16,20},{20,24},{24,28},{28,32},{32,36}... | collective-permute-start | bytes 1572872 | tf_op jit(solution)/shard_map/ppermute | solution.py:18
  37.6 16.0 %collective-permute-start.4 = (f32[2,32,32,1]{2,1,3,0:T(8,128)S(1)}, f32[2,32,32,1]{2,1,3,0:T(8,128)S(1)}, u32[]{:S(2)}, u32[]{:S(2)}) collective-permute-start(f32[2,32,32,1]{2,1,3,0:T(8,128)S(1)} %copy.32), channel_id=1, source_target_pairs={{0,1},{1,2},{2,3},{4,5},{5,6},{6,7},{8,9},{9,10},{10,11},{12,13},{... | collective-permute-start | bytes 24584 | tf_op jit(solution)/shard_map/ppermute | solution.py:26
  43.8 14.8 %collective-permute-start.5 = (f32[2,32,32,1]{2,1,3,0:T(8,128)S(1)}, f32[2,32,32,1]{2,1,3,0:T(8,128)S(1)}, u32[]{:S(2)}, u32[]{:S(2)}) collective-permute-start(f32[2,32,32,1]{2,1,3,0:T(8,128)S(1)} %copy.33), channel_id=1, source_target_pairs={{1,0},{2,1},{3,2},{5,4},{6,5},{7,6},{9,8},{10,9},{11,10},{13,12},{... | collective-permute-start | bytes 24584 | tf_op jit(solution)/shard_map/ppermute | solution.py:29
  46.6 31.9 %collective-permute-start.10 = (f32[1,32,32,1]{3,2,1,0:T(8,128)}, f32[1,32,32,1]{3,2,1,0:T(8,128)}, u32[]{:S(2)}, u32[]{:S(2)}) collective-permute-start(f32[1,32,32,1]{3,2,1,0:T(8,128)} %broadcast.103), channel_id=1, source_target_pairs={{0,1},{1,2},{2,3},{4,5},{5,6},{6,7},{8,9},{9,10},{10,11},{12,13},{... | collective-permute-start | bytes 12296 | tf_op jit(solution)/shard_map/ppermute | solution.py:26
  51.7 28.9 %collective-permute-start.11 = (f32[1,32,32,1]{3,2,1,0:T(8,128)}, f32[1,32,32,1]{3,2,1,0:T(8,128)}, u32[]{:S(2)}, u32[]{:S(2)}) collective-permute-start(f32[1,32,32,1]{3,2,1,0:T(8,128)} %broadcast.103), channel_id=1, source_target_pairs={{1,0},{2,1},{3,2},{5,4},{6,5},{7,6},{9,8},{10,9},{11,10},{13,12},{... | collective-permute-start | bytes 12296 | tf_op jit(solution)/shard_map/ppermute | solution.py:29
  54.5 40.1 %collective-permute-start.9 = (f32[1,32,32,128]{3,2,1,0:T(8,128)}, f32[1,32,32,128]{3,2,1,0:T(8,128)}, u32[]{:S(2)}, u32[]{:S(2)}) collective-permute-start(f32[1,32,32,128]{3,2,1,0:T(8,128)} %broadcast.101), channel_id=1, source_target_pairs={{0,4},{4,8},{8,12},{12,16},{16,20},{20,24},{24,28},{28,32},{32,36}... | collective-permute-start | bytes 1572872 | tf_op jit(solution)/shard_map/ppermute | solution.py:18
  96.8 22.6 %collective-permute-start.12 = (f32[1,32,32,128]{3,2,1,0:T(8,128)S(1)}, f32[1,32,32,128]{3,2,1,0:T(8,128)S(1)}, u32[]{:S(2)}, u32[]{:S(2)}) collective-permute-start(f32[1,32,32,128]{3,2,1,0:T(8,128)S(1)} %get-tuple-element.10), channel_id=1, source_target_pairs={{0,4},{4,8},{8,12},{12,16},{16,20},{20,24},{24,28},{28,32},{32,36}... | collective-permute-start | bytes 1572872 | tf_op jit(solution)/shard_map/ppermute | solution.py:18
  99.0 14.9 %collective-permute-start.13 = (f32[1,32,32,1]{3,2,1,0:T(8,128)S(1)}, f32[1,32,32,1]{3,2,1,0:T(8,128)S(1)}, u32[]{:S(2)}, u32[]{:S(2)}) collective-permute-start(f32[1,32,32,1]{3,2,1,0:T(8,128)S(1)} %get-tuple-element.66), channel_id=1, source_target_pairs={{0,1},{1,2},{2,3},{4,5},{5,6},{6,7},{8,9},{9,10},{10,11},{12,13},{... | collective-permute-start | bytes 12296 | tf_op jit(solution)/shard_map/ppermute | solution.py:26
  120.5 24.9 %collective-permute-start.15 = (f32[1,32,32,128]{3,2,1,0:T(8,128)S(1)}, f32[1,32,32,128]{3,2,1,0:T(8,128)S(1)}, u32[]{:S(2)}, u32[]{:S(2)}) collective-permute-start(f32[1,32,32,128]{3,2,1,0:T(8,128)S(1)} %fusion.176), channel_id=1, source_target_pairs={{0,4},{4,8},{8,12},{12,16},{16,20},{20,24},{24,28},{28,32},{32,36}... | collective-permute-start | bytes 1572872 | tf_op jit(solution)/shard_map/ppermute | solution.py:18
  133.1 17.3 %collective-permute-start.19 = (f32[1,32,32,128]{3,2,1,0:T(8,128)}, f32[1,32,32,128]{3,2,1,0:T(8,128)S(1)}, u32[]{:S(2)}, u32[]{:S(2)}) collective-permute-start(f32[1,32,32,128]{3,2,1,0:T(8,128)} %broadcast.101), channel_id=1, source_target_pairs={{0,8},{4,12},{8,16},{12,20},{16,24},{20,28},{24,32},{28,36},{32,40... | collective-permute-start | bytes 1572872 | tf_op jit(solution)/shard_map/ppermute | solution.py:18
  154.9 24.0 %collective-permute-start.20 = (f32[1,32,32,128]{3,2,1,0:T(8,128)S(1)}, f32[1,32,32,128]{3,2,1,0:T(8,128)S(1)}, u32[]{:S(2)}, u32[]{:S(2)}) collective-permute-start(f32[1,32,32,128]{3,2,1,0:T(8,128)S(1)} %get-tuple-element.8), channel_id=1, source_target_pairs={{0,8},{4,12},{8,16},{12,20},{16,24},{20,28},{24,32},{28,36},{32,40... | collective-permute-start | bytes 1572872 | tf_op jit(solution)/shard_map/ppermute | solution.py:18
  180.0 16.7 %collective-permute-start.23 = (f32[1,32,32,128]{3,2,1,0:T(8,128)S(1)}, f32[1,32,32,128]{3,2,1,0:T(8,128)S(1)}, u32[]{:S(2)}, u32[]{:S(2)}) collective-permute-start(f32[1,32,32,128]{3,2,1,0:T(8,128)S(1)} %fusion.162), channel_id=1, source_target_pairs={{0,8},{4,12},{8,16},{12,20},{16,24},{20,28},{24,32},{28,36},{32,40... | collective-permute-start | bytes 1572872 | tf_op jit(solution)/shard_map/ppermute | solution.py:18
  186.5 18.8 %collective-permute-start.27 = (f32[1,32,32,128]{3,2,1,0:T(8,128)}, f32[1,32,32,128]{3,2,1,0:T(8,128)S(1)}, u32[]{:S(2)}, u32[]{:S(2)}) collective-permute-start(f32[1,32,32,128]{3,2,1,0:T(8,128)} %broadcast.101), channel_id=1, source_target_pairs={{0,16},{4,20},{8,24},{12,28},{16,32},{20,36},{24,40},{28,44},{32,4... | collective-permute-start | bytes 1572872 | tf_op jit(solution)/shard_map/ppermute | solution.py:18
  197.7 21.2 %collective-permute-start.26 = (f32[1,32,32,128]{3,2,1,0:T(8,128)S(1)}, f32[1,32,32,128]{3,2,1,0:T(8,128)S(1)}, u32[]{:S(2)}, u32[]{:S(2)}) collective-permute-start(f32[1,32,32,128]{3,2,1,0:T(8,128)S(1)} %fusion.154), channel_id=1, source_target_pairs={{0,8},{8,0},{4,12},{12,4},{16,24},{24,16},{20,28},{28,20},{32,40},... | collective-permute-start | bytes 1572872 | tf_op jit(solution)/shard_map/ppermute | solution.py:41
  219.2 18.0 %collective-permute-start.28 = (f32[1,32,32,128]{3,2,1,0:T(8,128)S(1)}, f32[1,32,32,128]{3,2,1,0:T(8,128)S(1)}, u32[]{:S(2)}, u32[]{:S(2)}) collective-permute-start(f32[1,32,32,128]{3,2,1,0:T(8,128)S(1)} %get-tuple-element.6), channel_id=1, source_target_pairs={{0,16},{4,20},{8,24},{12,28},{16,32},{20,36},{24,40},{28,44},{32,4... | collective-permute-start | bytes 1572872 | tf_op jit(solution)/shard_map/ppermute | solution.py:18
  238.2 20.4 %collective-permute-start.31 = (f32[1,32,32,128]{3,2,1,0:T(8,128)S(1)}, f32[1,32,32,128]{3,2,1,0:T(8,128)S(1)}, u32[]{:S(2)}, u32[]{:S(2)}) collective-permute-start(f32[1,32,32,128]{3,2,1,0:T(8,128)S(1)} %fusion.148), channel_id=1, source_target_pairs={{0,16},{4,20},{8,24},{12,28},{16,32},{20,36},{24,40},{28,44},{32,4... | collective-permute-start | bytes 1572872 | tf_op jit(solution)/shard_map/ppermute | solution.py:18
  248.4 15.4 %collective-permute-start.35 = (f32[1,32,32,128]{3,2,1,0:T(8,128)}, f32[1,32,32,128]{3,2,1,0:T(8,128)S(1)}, u32[]{:S(2)}, u32[]{:S(2)}) collective-permute-start(f32[1,32,32,128]{3,2,1,0:T(8,128)} %broadcast.101), channel_id=1, source_target_pairs={{0,32},{4,36},{8,40},{12,44},{16,48},{20,52},{24,56},{28,60},{32,6... | collective-permute-start | bytes 1572872 | tf_op jit(solution)/shard_map/ppermute | solution.py:18
  271.6 22.0 %collective-permute-start.36 = (f32[1,32,32,128]{3,2,1,0:T(8,128)S(1)}, f32[1,32,32,128]{3,2,1,0:T(8,128)S(1)}, u32[]{:S(2)}, u32[]{:S(2)}) collective-permute-start(f32[1,32,32,128]{3,2,1,0:T(8,128)S(1)} %get-tuple-element.4), channel_id=1, source_target_pairs={{0,32},{4,36},{8,40},{12,44},{16,48},{20,52},{24,56},{28,60},{32,6... | collective-permute-start | bytes 1572872 | tf_op jit(solution)/shard_map/ppermute | solution.py:18
  294.7 17.4 %collective-permute-start.39 = (f32[1,32,32,128]{3,2,1,0:T(8,128)S(1)}, f32[1,32,32,128]{3,2,1,0:T(8,128)S(1)}, u32[]{:S(2)}, u32[]{:S(2)}) collective-permute-start(f32[1,32,32,128]{3,2,1,0:T(8,128)S(1)} %fusion.134), channel_id=1, source_target_pairs={{0,32},{4,36},{8,40},{12,44},{16,48},{20,52},{24,56},{28,60},{32,6... | collective-permute-start | bytes 1572872 | tf_op jit(solution)/shard_map/ppermute | solution.py:18
  313.1 18.2 %collective-permute-start.42 = (f32[1,32,32,128]{3,2,1,0:T(8,128)S(1)}, f32[1,32,32,128]{3,2,1,0:T(8,128)S(1)}, u32[]{:S(2)}, u32[]{:S(2)}) collective-permute-start(f32[1,32,32,128]{3,2,1,0:T(8,128)S(1)} %fusion.126), channel_id=1, source_target_pairs={{0,32},{4,36},{8,40},{12,44},{16,48},{20,52},{24,56},{28,60},{32,6... | collective-permute-start | bytes 1572872 | tf_op jit(solution)/shard_map/ppermute | solution.py:18
  332.4 19.5 %collective-permute-start.45 = (f32[1,32,32,128]{3,2,1,0:T(8,128)S(1)}, f32[1,32,32,128]{3,2,1,0:T(8,128)S(1)}, u32[]{:S(2)}, u32[]{:S(2)}) collective-permute-start(f32[1,32,32,128]{3,2,1,0:T(8,128)S(1)} %fusion.118), channel_id=1, source_target_pairs={{0,16},{4,20},{8,24},{12,28},{16,32},{20,36},{24,40},{28,44},{32,4... | collective-permute-start | bytes 1572872 | tf_op jit(solution)/shard_map/ppermute | solution.py:18
  353.0 16.7 %collective-permute-start.48 = (f32[1,32,32,128]{3,2,1,0:T(8,128)S(1)}, f32[1,32,32,128]{3,2,1,0:T(8,128)S(1)}, u32[]{:S(2)}, u32[]{:S(2)}) collective-permute-start(f32[1,32,32,128]{3,2,1,0:T(8,128)S(1)} %fusion.109), channel_id=1, source_target_pairs={{0,16},{4,20},{8,24},{12,28},{16,32},{20,36},{24,40},{28,44},{32,4... | collective-permute-start | bytes 1572872 | tf_op jit(solution)/shard_map/ppermute | solution.py:18
  370.8 19.1 %collective-permute-start.51 = (f32[1,32,32,128]{3,2,1,0:T(8,128)S(1)}, f32[1,32,32,128]{3,2,1,0:T(8,128)S(1)}, u32[]{:S(2)}, u32[]{:S(2)}) collective-permute-start(f32[1,32,32,128]{3,2,1,0:T(8,128)S(1)} %fusion.101), channel_id=1, source_target_pairs={{0,8},{4,12},{8,16},{12,20},{16,24},{20,28},{24,32},{28,36},{32,40... | collective-permute-start | bytes 1572872 | tf_op jit(solution)/shard_map/ppermute | solution.py:18
  390.9 21.1 %collective-permute-start.54 = (f32[1,32,32,128]{3,2,1,0:T(8,128)S(1)}, f32[1,32,32,128]{3,2,1,0:T(8,128)S(1)}, u32[]{:S(2)}, u32[]{:S(2)}) collective-permute-start(f32[1,32,32,128]{3,2,1,0:T(8,128)S(1)} %fusion.92), channel_id=1, source_target_pairs={{0,8},{4,12},{8,16},{12,20},{16,24},{20,28},{24,32},{28,36},{32,40... | collective-permute-start | bytes 1572872 | tf_op jit(solution)/shard_map/ppermute | solution.py:18
  395.8 15.7 %collective-permute-start.56 = (f32[1,32,32,1]{3,2,1,0:T(8,128)S(1)}, f32[1,32,32,1]{3,2,1,0:T(8,128)S(1)}, u32[]{:S(2)}, u32[]{:S(2)}) collective-permute-start(f32[1,32,32,1]{3,2,1,0:T(8,128)S(1)} %get-tuple-element.41), channel_id=1, source_target_pairs={{1,0},{2,1},{3,2},{5,4},{6,5},{7,6},{9,8},{10,9},{11,10},{13,12},{... | collective-permute-start | bytes 12296 | tf_op jit(solution)/shard_map/ppermute | solution.py:29
  413.1 22.7 %collective-permute-start.57 = (f32[1,32,32,128]{3,2,1,0:T(8,128)S(1)}, f32[1,32,32,128]{3,2,1,0:T(8,128)S(1)}, u32[]{:S(2)}, u32[]{:S(2)}) collective-permute-start(f32[1,32,32,128]{3,2,1,0:T(8,128)S(1)} %fusion.84), channel_id=1, source_target_pairs={{0,4},{4,8},{8,12},{12,16},{16,20},{20,24},{24,28},{28,32},{32,36}... | collective-permute-start | bytes 1572872 | tf_op jit(solution)/shard_map/ppermute | solution.py:18
  419.4 15.8 %collective-permute-start.59 = (f32[1,32,32,1]{3,2,1,0:T(8,128)S(1)}, f32[1,32,32,1]{3,2,1,0:T(8,128)S(1)}, u32[]{:S(2)}, u32[]{:S(2)}) collective-permute-start(f32[1,32,32,1]{3,2,1,0:T(8,128)S(1)} %get-tuple-element.39), channel_id=1, source_target_pairs={{1,0},{2,1},{3,2},{5,4},{6,5},{7,6},{9,8},{10,9},{11,10},{13,12},{... | collective-permute-start | bytes 12296 | tf_op jit(solution)/shard_map/ppermute | solution.py:29
  436.9 18.7 %collective-permute-start.60 = (f32[1,32,32,128]{3,2,1,0:T(8,128)S(1)}, f32[1,32,32,128]{3,2,1,0:T(8,128)S(1)}, u32[]{:S(2)}, u32[]{:S(2)}) collective-permute-start(f32[1,32,32,128]{3,2,1,0:T(8,128)S(1)} %fusion.75), channel_id=1, source_target_pairs={{0,4},{4,8},{8,12},{12,16},{16,20},{20,24},{24,28},{28,32},{32,36}... | collective-permute-start | bytes 1572872 | tf_op jit(solution)/shard_map/ppermute | solution.py:18
  457.9 26.1 %collective-permute-start.63 = (f32[1,32,32,128]{3,2,1,0:T(8,128)}, f32[1,32,32,128]{3,2,1,0:T(8,128)}, u32[]{:S(2)}, u32[]{:S(2)}) collective-permute-start(f32[1,32,32,128]{3,2,1,0:T(8,128)} %get-tuple-element.21), channel_id=1, source_target_pairs={{0,4},{4,8},{8,12},{12,16},{16,20},{20,24},{24,28},{28,32},{32,36}... | collective-permute-start | bytes 1572872 | tf_op jit(solution)/shard_map/ppermute | solution.py:18
  488.6 18.5 %collective-permute-start.66 = (f32[1,32,32,128]{3,2,1,0:T(8,128)}, f32[1,32,32,128]{3,2,1,0:T(8,128)}, u32[]{:S(2)}, u32[]{:S(2)}) collective-permute-start(f32[1,32,32,128]{3,2,1,0:T(8,128)} %get-tuple-element.17), channel_id=1, source_target_pairs={{0,4},{4,8},{8,12},{12,16},{16,20},{20,24},{24,28},{28,32},{32,36}... | collective-permute-start | bytes 1572872 | tf_op jit(solution)/shard_map/ppermute | solution.py:18
  512.5 25.3 %collective-permute-start.69 = (f32[1,32,32,128]{3,2,1,0:T(8,128)}, f32[1,32,32,128]{3,2,1,0:T(8,128)}, u32[]{:S(2)}, u32[]{:S(2)}) collective-permute-start(f32[1,32,32,128]{3,2,1,0:T(8,128)} %get-tuple-element.13), channel_id=1, source_target_pairs={{0,4},{4,8},{8,12},{12,16},{16,20},{20,24},{24,28},{28,32},{32,36}... | collective-permute-start | bytes 1572872 | tf_op jit(solution)/shard_map/ppermute | solution.py:18
  (66 other events, 556.3 us)
where the time goes:
time: 553 us; the launch traced here: 542 us
  starting transfers between devices  222 us (40%)
  waiting for transfers between devices  201 us (36%)
  other arithmetic  68.7 us (12%)
  local copies, waits for them, and re-layouts  48.5 us (9%)
    ppermute x25, starting transfers between devices, passed_along(): return lax.ppermute(block, axis, route)  100 us
    ppermute x22, waiting for transfers between devices, padded_2(): lax.ppermute(lax.slice_in_dim(block, 0, width, axis=dim), axis, backward)  94.9 us
    ppermute x22, starting transfers between devices, padded_2(): lax.ppermute(lax.slice_in_dim(block, block.shape[dim] - width, None, axis...  71.8 us
    ppermute x22, waiting for transfers between devices, padded_2(): lax.ppermute(lax.slice_in_dim(block, block.shape[dim] - width, None, axis...  57.6 us
    ppermute x22, starting transfers between devices, padded_2(): lax.ppermute(lax.slice_in_dim(block, 0, width, axis=dim), axis, backward)  47.8 us
    concatenate x22, other arithmetic, padded_2(): block = jnp.concatenate([low, block, high], axis=dim)  27.7 us
    ppermute x3, waiting for transfers between devices, partner(): return lax.ppermute(block, axis, route)  25.2 us
    add x13, other arithmetic, smooth_single(): values + scaled * (target - operate(values, diffusivity, time_coef, stride))  24.2 us
  transfers between devices with their start and end apart: 72, of which 42 were waited for; matrix products, arithmetic and copies ran while one was open for 14% of the time, Pallas kernels for 0%

commit v1 on v0

v1 whole, which is shorter than its diff:
```python
import functools
import math
import jax
import jax.numpy as jnp
from jax import lax
from jax.experimental import pallas as pl
from jax.experimental.pallas import tpu as pltpu
from jax.sharding import PartitionSpec as P

damping = 0.8
keep = 1.0 - 0.8
base_coef = 8.0

SIDE = 32
OWN = 128
HALO = 22
EXT = OWN + 2 * HALO
GROUP = 8
PIECE = 17
WIDE = PIECE + 30
COARSE = GROUP * PIECE + 30
LOW = HALO - 19
F32 = jnp.float32

VM = pl.BlockSpec(memory_space=pltpu.VMEM)
SM = pl.BlockSpec(memory_space=pltpu.SMEM)


def call(body, outs, args, scratch=(), n_scalar=0):
    single = isinstance(outs, tuple)
    shapes = [outs] if single else list(outs)
    held = shapes + list(scratch) + [a.shape for a in args[n_scalar:]]
    need = sum(4 * math.prod(s) for s in held)
    result = pl.pallas_call(
        body,
        out_shape=[jax.ShapeDtypeStruct(s, F32) for s in shapes],
        in_specs=[SM] * n_scalar + [VM] * (len(args) - n_scalar),
        out_specs=[VM] * len(shapes),
        scratch_shapes=[pltpu.VMEM(s, F32) for s in scratch],
        compiler_params=pltpu.CompilerParams(vmem_limit_bytes=need + (2 << 20)),
    )(*args)
    return result[0] if single else result


def planes(low, high, width, fn):
    width = min(width, high - low)

    def step(i, carry):
        fn(pl.ds(jnp.minimum(low + i * width, high - width), width))
        return carry

    lax.fori_loop(0, -(-(high - low) // width), step, 0)


def width(steps):
    return max(1, 16 // steps)


def moved(at, by):
    return pl.ds(at.start + by, at.size)


def masks():
    lane = lax.broadcasted_iota(jnp.int32, (8, 128), 1)
    row = lax.broadcasted_iota(jnp.int32, (8, 128), 0)
    y = lane % SIDE
    return y != SIDE - 1, y != 0, lane < 96, lane >= 32, row < 7, row > 0


def beside(p, m):
    shape = p.shape
    p = p.reshape((-1,) + shape[-2:])
    y_up, y_down, x_in, x_out, row_up, row_down = [jnp.broadcast_to(a[None], p.shape) for a in m]
    zero = jnp.zeros_like(p)
    up = pltpu.roll(p, 96, 2)
    down = pltpu.roll(p, 32, 2)
    total = jnp.where(y_up, pltpu.roll(p, 127, 2), zero) + jnp.where(y_down, pltpu.roll(p, 1, 2), zero)
    total = total + jnp.where(x_in, up, jnp.where(row_up, pltpu.roll(up, 7, 1), zero))
    total = total + jnp.where(x_out, down, jnp.where(row_down, pltpu.roll(down, 1, 1), zero))
    return total.reshape(shape)


def spread(ref, t0, t1, z, m):
    p = ref[t0:t1, z]
    return p, beside(p, m) + ref[t0:t1, moved(z, -1)] + ref[t0:t1, moved(z, 1)]


def transposed_in(flag, v_ref, g_ref, d_ref, out, tail, edge_a, edge_b):
    for t in range(5):
        ref = v_ref if t < 2 else g_ref
        for s in range(8):
            rows = slice(s * 128, (s + 1) * 128)
            block = d_ref[rows, :] if t == 4 else ref[t % 2, rows, :]
            out[t, :, s, :] = block.T
            if t == 1:
                tail[0, :, s, :] = block.T
    odd = flag[0]
    far = OWN - HALO
    start_a = far * (1 - odd)
    start_b = far * odd

    def edge(z):
        edge_a[:, z] = out[:, moved(z, start_a)]
        edge_b[:, z] = out[:, moved(z, start_b)]

    planes(0, HALO, 2, edge)


def first_level(flag, own, edge_a, edge_b, back, back_edge, ext, v1, tail, prev):
    odd = flag[0]
    end = OWN + HALO
    at_a = end * (1 - odd)
    at_b = end * odd

    def centre(z):
        ext[0:5, moved(z, HALO)] = own[:, z]
        prev[0, moved(z, HALO)] = back[0, z]

    def edge(z):
        ext[0:5, moved(z, at_a)] = edge_a[:, z]
        ext[0:5, moved(z, at_b)] = edge_b[:, z]
        prev[0, moved(z, at_a)] = back_edge[0, z]
        prev[0, moved(z, at_b)] = back_edge[1, z]

    planes(0, OWN, 4, centre)
    planes(0, HALO, 2, edge)

    def scale(z):
        ext[5, z] = damping / (base_coef + 6.0 * ext[4, z])

    planes(0, EXT, 8, scale)
    pair_sweep(ext, ext, 0, prev, 0, v1, tail, 1, 1, EXT - 1)


def pair_sweep(ext, src, off, prev, off_prev, dst, tail, off_dst, low, high):
    m = masks()

    def fn(z):
        p, near = spread(src, 0, 2, moved(z, -off), m)
        before = jnp.concatenate([prev[0:1, moved(z, -off_prev)], p[0:1]], axis=0)
        value = keep * p + ext[5, z] * (ext[2:4, z] + base_coef * before + ext[4, z] * near)
        dst[:, moved(z, -off_dst)] = value
        tail[:, moved(z, -off_dst)] = value[1:2]

    planes(low, high, 8, fn)


def pair_left(ext, src, off, prev, off_prev, low, high, store):
    m = masks()

    def fn(z):
        p, near = spread(src, 0, 2, moved(z, -off), m)
        d = ext[4, z]
        before = jnp.concatenate([prev[0:1, moved(z, -off_prev)], p[0:1]], axis=0)
        store(z, ext[2:4, z] + base_coef * before + d * near - (base_coef + 6.0 * d) * p)

    planes(low, high, 8, fn)


def second_sweep(ext, v1, prev, v2, tail):
    pair_sweep(ext, v1, 1, prev, 1, v2, tail, 2, 2, EXT - 2)


def restrict_left(ext, v2, prev, out):
    def store(z, r):
        out[:, moved(z, -LOW)] = 0.5 * (r[0:1] + r[1:2])

    pair_left(ext, v2, 2, prev, 2, LOW, LOW + COARSE, store)


FIN = OWN + 2
FIRST = HALO - 1
E_LOW = HALO - 4


def third_sweep(ext, v2, prev, e0, e1, v3, tail, va, vp):
    def add(z):
        here = moved(z, -2)
        there = moved(z, -E_LOW)
        va[:, moved(z, -FIRST + 2)] = v2[:, here] + e0[:, there]
        vp[:, moved(z, -FIRST + 2)] = prev[:, here] + e1[:, there]

    planes(FIRST - 2, FIRST + FIN + 2, 8, add)
    pair_sweep(ext, va, FIRST - 2, vp, FIRST - 2, v3, tail, FIRST - 1, FIRST - 1, FIRST + FIN + 1)


def fourth_sweep(ext, v3, prev, v4, tail):
    pair_sweep(ext, v3, FIRST - 1, prev, FIRST - 1, v4, tail, FIRST, FIRST, FIRST + FIN)


def finish(ext, v4, prev, sol_out, res_out, res):
    def store(z, r):
        res[:, moved(z, -HALO)] = r

    for t in range(2):
        for s in range(8):
            sol_out[t, s * 128 : (s + 1) * 128, :] = v4[t, 1 : OWN + 1, s, :].T
    pair_left(ext, v4, FIRST, prev, FIRST, HALO, HALO + OWN, store)
    for t in range(2):
        for s in range(8):
            res_out[t, s * 128 : (s + 1) * 128, :] = res[t, :, s, :].T


def step_down(flag, d_ref, *refs, counts, own, c, low, last, tail_steps):
    history = refs[: len(counts)]
    g_own = refs[len(counts)]
    rest = refs[len(counts) + 1 :]
    past = sum(counts)
    total = past + own
    high = WIDE - low
    q = flag[0]
    if last:
        v_above, e_ref, tail, s_ref, g_ref, va, vb = rest
    elif tail_steps:
        v2, below, tail, s_ref, g_ref, va = rest
    else:
        v2, below, s_ref, g_ref, va = rest

    def gather(z):
        s = damping / (c + 6.0 * d_ref[z])
        s_ref[z] = s
        at = 0
        for i, (ref, n) in enumerate(zip(history, counts)):
            known = jnp.where(q > len(counts) - 1 - i, 1.0, 0.0).astype(F32)
            g = known * ref[:, moved(z, -low)]
            g_ref[at : at + n, z] = g
            va[at : at + n, z] = s * g
            at += n
        g = g_own[:, moved(z, -low)]
        g_ref[at:, z] = g
        va[at:, z] = s * g

    planes(low, high, width(total), gather)
    m = masks()

    def sweep(src, start, margin, store):
        def fn(z):
            p, near = spread(src, start, total, z, m)
            value = keep * p + s_ref[z] * (
                g_ref[start:total, z] + c * src[start - 1 : total - 1, z] + d_ref[z] * near
            )
            store(z, value)

        planes(low + margin, high - margin, width(total - start), fn)

    if last:

        def keep_b(z, value):
            vb[1:total, z] = value

        def keep_a(z, value):
            va[2:total, z] = value

        def keep_e(z, value):
            e_ref[:, moved(z, -low - 3)] = value
            tail[:, moved(z, -low - 3)] = v_above[v_above.shape[0] - 2 :, moved(z, 1 - low)] + value

        sweep(va, 1, 1, keep_b)
        sweep(vb, 2, 2, keep_a)
        sweep(va, 3, 3, keep_e)
        return

    def keep_v(z, value):
        v2[:, moved(z, -low - 1)] = value

    sweep(va, 1, 1, keep_v)

    def left(z):
        zz = moved(z, -low - 1)
        p, near = spread(v2, past - 1, total - 1, zz, m)
        d = d_ref[z]
        r = g_ref[past:total, z] + c * v2[past - 2 : total - 2, zz] + d * near - (c + 6.0 * d) * p
        for j in range(own // 2):
            value = 0.5 * (r[2 * j] + r[2 * j + 1])
            below[j, moved(z, -low - 2)] = value
            if tail_steps and j >= own // 2 - tail_steps:
                tail[j - own // 2 + tail_steps, moved(z, -low - 2)] = value

    planes(low + 2, high - 2, width(own), left)


def step_up(flag, d_ref, v2, g_last, g_own, v_last, e_own, *rest, own, c, low, e_low, top):
    if top:
        out, s_ref, va, vb = rest
    else:
        v_above, out, tail, s_ref, va, vb = rest
    q = flag[0]
    known = jnp.where(q > 0, 1.0, 0.0).astype(F32)
    n = own + 2
    last = g_last.shape[0] - 1

    def correct(z):
        s_ref[z] = damping / (c + 6.0 * d_ref[z])
        zz = moved(z, -low - 1)
        here = moved(z, -e_low)
        va[0:2, z] = known * v_last[:, here]
        for j in range(own // 2):
            e = e_own[j, here]
            va[2 + 2 * j, z] = v2[1 + 2 * j, zz] + e
            va[3 + 2 * j, z] = v2[2 + 2 * j, zz] + e

    planes(e_low, WIDE - e_low, width(n), correct)
    m = masks()

    def sweep1(z):
        p, near = spread(va, 1, n, z, m)
        g0 = known * g_last[last : last + 1, moved(z, -low)]
        g = jnp.concatenate([g0, g_own[:, moved(z, -low)]], axis=0)
        vb[:, z] = keep * p + s_ref[z] * (g + c * va[0 : n - 1, z] + d_ref[z] * near)

    planes(e_low + 1, WIDE - e_low - 1, width(n - 1), sweep1)

    def sweep2(z):
        p, near = spread(vb, 1, n - 1, z, m)
        value = keep * p + s_ref[z] * (
            g_own[:, moved(z, -low)] + c * vb[0 : n - 2, z] + d_ref[z] * near
        )
        here = moved(z, -e_low - 2)
        out[:, here] = value
        if not top:
            tail[:, here] = v_above[v_above.shape[0] - 2 :, moved(z, 1 - low)] + value[own - 1 :]

    planes(e_low + 2, WIDE - e_low - 2, width(own), sweep2)


def later(block, distance):
    count = lax.axis_size("tm")
    return lax.ppermute(block, "tm", [(i, i + distance) for i in range(count - distance)])


def around(block, distance):
    count = lax.axis_size("tm")
    return lax.ppermute(block, "tm", [(i, (i + distance) % count) for i in range(count)])


def body(source, initial_guess, diffusivity):
    T = (8, 128)
    slabs = lax.axis_size("gz")
    count = lax.axis_size("tm")
    odd = (lax.axis_index("gz") % 2).astype(jnp.int32).reshape(1)
    me = lax.axis_index("tm")
    q = (me // GROUP).astype(jnp.int32).reshape(1)
    piece = me % GROUP

    flat = lambda a: a.reshape(a.shape[:-3] + (SIDE * SIDE, OWN))
    own, tail, edge_a, edge_b = call(
        transposed_in,
        [(5, OWN) + T, (1, OWN) + T, (5, HALO) + T, (5, HALO) + T],
        (odd, flat(initial_guess), flat(source), flat(diffusivity)),
        n_scalar=1,
    )
    edge_a = lax.ppermute(edge_a, "gz", [(i, i ^ 1) for i in range(slabs)])
    pairs = [(i, i + 1) for i in range(1, slabs - 1, 2)]
    edge_b = lax.ppermute(edge_b, "gz", pairs + [(b, a) for a, b in pairs])
    prev = later(tail, 1)
    prev_edge = later(jnp.stack([edge_a[1], edge_b[1]]), 1)
    ext, v1, tail = call(
        first_level,
        [(6, EXT) + T, (2, EXT - 2) + T, (1, EXT - 2) + T],
        (odd, own, edge_a, edge_b, prev, prev_edge),
        scratch=[(1, EXT) + T],
        n_scalar=1,
    )
    v2, tail = call(second_sweep, [(2, EXT - 4) + T, (1, EXT - 4) + T], (ext, v1, later(tail, 1)))
    v2_prev = later(tail, 1)
    g1 = call(restrict_left, (1, COARSE) + T, (ext, v2, v2_prev))[0]

    groups = [list(range(a, a + GROUP)) for a in range(0, count, GROUP)]
    pieces = jnp.stack([g1[PIECE * b : PIECE * b + WIDE] for b in range(GROUP)])
    g = lax.all_to_all(pieces, "tm", 0, 0, axis_index_groups=groups, tiled=True)
    d = lax.dynamic_slice_in_dim(ext[4], LOW + PIECE * piece, WIDE, axis=0)

    saved = []
    own_steps = GROUP
    c = base_coef / 2.0
    low = 0
    g_tail = g[-2:]
    for level in range(1, 4):
        history = around(g_tail, GROUP)
        total = own_steps + 2
        wide = WIDE - 2 * low
        tail_steps = 2 if own_steps > 4 else 0
        v, g_below, *g_tail = call(
            functools.partial(
                step_down, counts=[2], own=own_steps, c=c, low=low, last=False, tail_steps=tail_steps
            ),
            [(total - 1, wide - 2) + T, (own_steps // 2, wide - 4) + T]
            + [(tail_steps, wide - 4) + T] * (tail_steps > 0),
            (q, d, history, g),
            scratch=[(WIDE,) + T, (total, WIDE) + T, (total, WIDE) + T],
            n_scalar=1,
        )
        g_tail = g_tail[0] if g_tail else g_below
        saved.append((v, history, g, own_steps, c, low))
        g = g_below
        own_steps //= 2
        c /= 2.0
        low += 2
    history = [around(g, i * GROUP) for i in (3, 2, 1)]
    wide = WIDE - 2 * low
    e, tail = call(
        functools.partial(
            step_down, counts=[1] * 3, own=1, c=c, low=low, last=True, tail_steps=0
        ),
        [(1, wide - 6) + T, (2, wide - 6) + T],
        (q, d, *history, g, saved[-1][0]),
        scratch=[(WIDE,) + T] + [(4, WIDE) + T] * 3,
        n_scalar=1,
    )
    e_low = low + 3
    while saved:
        v, g_last, g, own_steps, c, low = saved.pop()
        v_last = around(tail, GROUP)
        top = not saved
        narrow = WIDE - 2 * e_low - 4
        e = call(
            functools.partial(step_up, own=own_steps, c=c, low=low, e_low=e_low, top=top),
            [(own_steps, narrow) + T] + [(2, narrow) + T] * (not top),
            (q, d, v, g_last, g, v_last, e) + (() if top else (saved[-1][0],)),
            scratch=[(WIDE,) + T, (own_steps + 2, WIDE) + T, (own_steps + 1, WIDE) + T],
            n_scalar=1,
        )
        tail = e[-1]
        e = e[0]
        e_low += 2
    e0 = lax.all_to_all(e, "tm", 0, 0, axis_index_groups=groups, tiled=True)
    e0 = e0.reshape((1, GROUP * PIECE) + T)
    v3, tail = call(
        third_sweep,
        [(2, FIN + 2) + T, (1, FIN + 2) + T],
        (ext, v2, v2_prev, e0, later(e0, 1)),
        scratch=[(2, FIN + 4) + T, (1, FIN + 4) + T],
    )
    v4, tail = call(fourth_sweep, [(2, FIN) + T, (1, FIN) + T], (ext, v3, later(tail, 1)))
    sol, res = call(
        finish,
        [(2, SIDE * SIDE, OWN)] * 2,
        (ext, v4, later(tail, 1)),
        scratch=[(2, OWN) + T],
    )
    return sol.reshape(source.shape), res.reshape(source.shape)


def solution(mesh):
    placed = (P("tm", None, None, "gz"), P("tm", None, None, "gz"), P(None, None, "gz"))
    return jax.shard_map(
        body,
        mesh=mesh,
        in_specs=placed,
        out_specs=(P("tm", None, None, "gz"), P("tm", None, None, "gz")),
        check_vma=False,
    )
```

time: 553 us -> 283 us (0.51)
  the two profiles are of different devices: /device:TPU:3 before, /device:TPU:144 now
where the time goes in v1:
time: 283 us
  waiting for transfers between devices  143 us (51%)
  starting transfers between devices  47.7 us (17%)
  Pallas kernels  46.7 us (17%)
  blocking collectives  38.3 us (14%)
  local copies, waits for them, and re-layouts  6.42 us (2%)
    ppermute x7, waiting for transfers between devices, later(): lax.ppermute(block, 'tm', [(i, i + distance) for i in range(count - dista...  79.5 us
    ppermute x9, waiting for transfers between devices, around(): lax.ppermute(block, 'tm', [(i, (i + distance) % count) for i in range(cou...  53.6 us
    pallas_call x14, Pallas kernels, call(): pl.pallas_call(body, out_shape=[jax.ShapeDtypeStruct(s, F32) for s in sha...  46.7 us
    ppermute x7, starting transfers between devices, later(): lax.ppermute(block, 'tm', [(i, i + distance) for i in range(count - dista...  27.7 us
    all_to_all x1, blocking collectives, body(): e0 = lax.all_to_all(e, 'tm', 0, 0, axis_index_groups=groups, tiled=True)  20.3 us
    all_to_all x1, blocking collectives, body(): g = lax.all_to_all(pieces, 'tm', 0, 0, axis_index_groups=groups, tiled=True)  18 us
    ppermute x9, starting transfers between devices, around(): lax.ppermute(block, 'tm', [(i, (i + distance) % count) for i in range(cou...  17.7 us
    ppermute x1, waiting for transfers between devices, body(): edge_b = lax.ppermute(edge_b, 'gz', pairs + [(b, a) for a, b in pairs])  9.48 us
  transfers between devices with their start and end apart: 18, of which 15 were waited for; matrix products, arithmetic and copies ran while one was open for 0% of the time, Pallas kernels for 0%

profile of v1, /device:TPU:144, one launch (start us, length us, event | category | flops | bytes accessed | tf_op | source)
XLA Modules:
  0.0 282.8 jit_solution(10613970166812862306)
XLA Ops:
  8.5 4.1 %collective-permute-start.2 = (f32[1,128,8,128]{3,2,1,0:T(8,128)S(1)}, f32[1,128,8,128]{3,2,1,0:T(8,128)S(1)}, u32[]{:S(2)}, u32[]{:S(2)}) collective-permute-start(f32[1,128,8,128]{3,2,1,0:T(8,128)S(1)} %get-tuple-element.33), channel_id=1, source_target_pairs={{0,4},{4,8},{8,12},{12,16},{16,20},{20,24},{24,28},{28,32},{32,36}... | collective-permute-start | bytes 1572872 | tf_op jit(solution)/shard_map/ppermute | solution.py:328
  12.6 9.5 %collective-permute-done.1.edge_b = f32[5,22,8,128]{3,2,1,0:T(8,128)S(1)} collective-permute-done((f32[5,22,8,128]{3,2,1,0:T(8,128)S(1)}, f32[5,22,8,128]{3,2,1,0:T(8,128)S(1)}, u32[]{:S(2)}, u32[]{:S(2)}) %collective-permute-start.1) | collective-permute-done | bytes 450592 | tf_op jit(solution)/shard_map/ppermute | solution.py:354
  22.1 11.6 %collective-permute-start.3 = (f32[2,22,8,128]{3,2,1,0:T(8,128)S(1)}, f32[2,22,8,128]{3,2,1,0:T(8,128)S(1)}, u32[]{:S(2)}, u32[]{:S(2)}) collective-permute-start(f32[2,22,8,128]{3,2,1,0:T(8,128)S(1)} %pad_maximum_fusion), channel_id=1, source_target_pairs={{0,4},{4,8},{8,12},{12,16},{16,20},{20,24},{24,28},{28,32},{32,36}... | collective-permute-start | bytes 540680 | tf_op jit(solution)/shard_map/ppermute | solution.py:328
  33.7 5.2 %collective-permute-done.3.back_edge = f32[2,22,8,128]{3,2,1,0:T(8,128)S(1)} collective-permute-done((f32[2,22,8,128]{3,2,1,0:T(8,128)S(1)}, f32[2,22,8,128]{3,2,1,0:T(8,128)S(1)}, u32[]{:S(2)}, u32[]{:S(2)}) %collective-permute-start.3) | collective-permute-done | bytes 180256 | tf_op jit(solution)/shard_map/ppermute | solution.py:328
  38.9 4.1 %shard_map.51 = (f32[6,172,8,128]{3,2,1,0:T(8,128)S(1)}, f32[2,170,8,128]{3,2,1,0:T(8,128)S(1)}, f32[1,170,8,128]{3,2,1,0:T(8,128)S(1)}) custom-call(s32[1]{0:T(128)} %bitcast.flag, f32[5,128,8,128]{3,2,1,0:T(8,128)S(1)} %get-tuple-element.30.own, f32[5,22,8,128]{3,2,1,0:T(8,128)S(1)} %collective-permute-done.edge_a, ...), custom_call_target="tpu_custom_call" | custom-call | tf_op jit(solution)/shard_map/pallas_call | solution.py:34
  43.0 3.5 %collective-permute-start.4 = (f32[1,170,8,128]{3,2,1,0:T(8,128)S(1)}, f32[1,170,8,128]{3,2,1,0:T(8,128)S(1)}, u32[]{:S(2)}, u32[]{:S(2)}) collective-permute-start(f32[1,170,8,128]{3,2,1,0:T(8,128)S(1)} %get-tuple-element.36), channel_id=1, source_target_pairs={{0,4},{4,8},{8,12},{12,16},{16,20},{20,24},{24,28},{28,32},{32,36}... | collective-permute-start | bytes 2088968 | tf_op jit(solution)/shard_map/ppermute | solution.py:328
  46.6 13.6 %collective-permute-done.4.prev = f32[1,170,8,128]{3,2,1,0:T(8,128)S(1)} collective-permute-done((f32[1,170,8,128]{3,2,1,0:T(8,128)S(1)}, f32[1,170,8,128]{3,2,1,0:T(8,128)S(1)}, u32[]{:S(2)}, u32[]{:S(2)}) %collective-permute-start.4) | collective-permute-done | bytes 696352 | tf_op jit(solution)/shard_map/ppermute | solution.py:328
  60.2 3.1 %shard_map.52 = (f32[2,168,8,128]{3,2,1,0:T(8,128)S(1)}, f32[1,168,8,128]{3,2,1,0:T(8,128)S(1)}) custom-call(f32[6,172,8,128]{3,2,1,0:T(8,128)S(1)} %get-tuple-element.34.ext, f32[2,170,8,128]{3,2,1,0:T(8,128)S(1)} %get-tuple-element.35.v1, f32[1,170,8,128]{3,2,1,0:T(8,128)S(1)} %collective-permute-done.4.prev), custom_call_target="tpu_custom_call" | custom-call | tf_op jit(solution)/shard_map/pallas_call | solution.py:34
  65.5 15.5 %collective-permute-done.5.prev = f32[1,168,8,128]{3,2,1,0:T(8,128)S(1)} collective-permute-done((f32[1,168,8,128]{3,2,1,0:T(8,128)S(1)}, f32[1,168,8,128]{3,2,1,0:T(8,128)S(1)}, u32[]{:S(2)}, u32[]{:S(2)}) %collective-permute-start.5) | collective-permute-done | bytes 688160 | tf_op jit(solution)/shard_map/ppermute | solution.py:328
  81.0 3.1 %shard_map.53 = f32[1,166,8,128]{3,2,1,0:T(8,128)S(1)} custom-call(f32[6,172,8,128]{3,2,1,0:T(8,128)S(1)} %get-tuple-element.34.ext, f32[2,168,8,128]{3,2,1,0:T(8,128)S(1)} %get-tuple-element.37.v2, f32[1,168,8,128]{3,2,1,0:T(8,128)S(1)} %collective-permute-done.5.prev), custom_call_target="tpu_custom_call" | custom-call | tf_op jit(solution)/shard_map/pallas_call | solution.py:34
  85.1 18.0 %all_to_all.10.refs_1_.g_own = f32[8,47,8,128]{3,2,1,0:T(8,128)S(1)} all-to-all(f32[8,47,8,128]{3,2,1,0:T(8,128)S(1)} %slice_dynamic-update-slice_fusion), channel_id=1, replica_groups={{0,4,8,12,16,20,24,28},{32,36,40,44,48,52,56,60},{64,68,72,76,80,84,88,..., dimensions={0} | all-to-all | bytes 3080192 | tf_op jit(solution)/shard_map/all_to_all | solution.py:370
  103.9 4.9 %collective-permute-start.6 = (f32[2,47,8,128]{3,2,1,0:T(8,128)}, f32[2,47,8,128]{3,2,1,0:T(8,128)S(1)}, u32[]{:S(2)}, u32[]{:S(2)}) collective-permute-start(f32[2,47,8,128]{3,2,1,0:T(8,128)} %slice.66), channel_id=1, source_target_pairs={{0,32},{4,36},{8,40},{12,44},{16,48},{20,52},{24,56},{28,60},{32,6... | collective-permute-start | bytes 1155080 | tf_op jit(solution)/shard_map/ppermute | solution.py:333
  109.9 8.1 %collective-permute-done.6.refs_0_.g_last = f32[2,47,8,128]{3,2,1,0:T(8,128)S(1)} collective-permute-done((f32[2,47,8,128]{3,2,1,0:T(8,128)}, f32[2,47,8,128]{3,2,1,0:T(8,128)S(1)}, u32[]{:S(2)}, u32[]{:S(2)}) %collective-permute-start.6) | collective-permute-done | bytes 385056 | tf_op jit(solution)/shard_map/ppermute | solution.py:333
  118.1 9.2 %shard_map.54 = (f32[9,45,8,128]{3,2,1,0:T(8,128)S(1)}, f32[4,43,8,128]{3,2,1,0:T(8,128)S(1)}, f32[2,43,8,128]{3,2,1,0:T(8,128)S(1)}) custom-call(s32[1]{0:T(128)} %bitcast.4.flag, f32[47,8,128]{2,1,0:T(8,128)S(1)} %dynamic-slice_bitcast_fusion.d_ref, f32[2,47,8,128]{3,2,1,0:T(8,128)S(1)} %collective-permute-done.6.refs_0_.g_last, ...), custom_call_target="tpu_custom_call" | custom-call | tf_op jit(solution)/shard_map/pallas_call | solution.py:34
  127.5 10.7 %collective-permute-done.7.refs_0_.g_last = f32[2,43,8,128]{3,2,1,0:T(8,128)S(1)} collective-permute-done((f32[2,43,8,128]{3,2,1,0:T(8,128)S(1)}, f32[2,43,8,128]{3,2,1,0:T(8,128)S(1)}, u32[]{:S(2)}, u32[]{:S(2)}) %collective-permute-start.7) | collective-permute-done | bytes 352288 | tf_op jit(solution)/shard_map/ppermute | solution.py:333
  138.2 3.8 %shard_map.55 = (f32[5,41,8,128]{3,2,1,0:T(8,128)S(1)}, f32[2,39,8,128]{3,2,1,0:T(8,128)S(1)}) custom-call(s32[1]{0:T(128)} %bitcast.4.flag, f32[47,8,128]{2,1,0:T(8,128)S(1)} %dynamic-slice_bitcast_fusion.d_ref, f32[2,43,8,128]{3,2,1,0:T(8,128)S(1)} %collective-permute-done.7.refs_0_.g_last, f32[4,43,8,128]{3,2,1,0:T(8,128)S(1)} %get-tuple-element.41.refs_1_.g_own), custom_call_target="tpu_custom_call" | custom-call | tf_op jit(solution)/shard_map/pallas_call | solution.py:34
  142.9 9.2 %collective-permute-done.8.refs_0_.g_last = f32[2,39,8,128]{3,2,1,0:T(8,128)S(1)} collective-permute-done((f32[2,39,8,128]{3,2,1,0:T(8,128)S(1)}, f32[2,39,8,128]{3,2,1,0:T(8,128)S(1)}, u32[]{:S(2)}, u32[]{:S(2)}) %collective-permute-start.8) | collective-permute-done | bytes 319520 | tf_op jit(solution)/shard_map/ppermute | solution.py:333
  154.3 3.2 %collective-permute-start.10 = (f32[1,35,8,128]{3,2,1,0:T(8,128)S(1)}, f32[1,35,8,128]{3,2,1,0:T(8,128)S(1)}, u32[]{:S(2)}, u32[]{:S(2)}) collective-permute-start(f32[1,35,8,128]{3,2,1,0:T(8,128)S(1)} %get-tuple-element.45.refs_3_), channel_id=1, source_target_pairs={{0,64},{4,68},{8,72},{12,76},{16,80},{20,84},{24,88},{28,92},{32,9... | collective-permute-start | bytes 430088 | tf_op jit(solution)/shard_map/ppermute | solution.py:333
  157.5 3.1 %collective-permute-start.9 = (f32[1,35,8,128]{3,2,1,0:T(8,128)S(1)}, f32[1,35,8,128]{3,2,1,0:T(8,128)S(1)}, u32[]{:S(2)}, u32[]{:S(2)}) collective-permute-start(f32[1,35,8,128]{3,2,1,0:T(8,128)S(1)} %get-tuple-element.45.refs_3_), channel_id=1, source_target_pairs={{0,96},{4,100},{8,104},{12,108},{16,112},{20,116},{24,120},{28,124... | collective-permute-start | bytes 430088 | tf_op jit(solution)/shard_map/ppermute | solution.py:333
  160.6 2.8 collective-permute-done.11.refs_2_
  163.4 6.9 %collective-permute-done.9.refs_0_ = f32[1,35,8,128]{3,2,1,0:T(8,128)S(1)} collective-permute-done((f32[1,35,8,128]{3,2,1,0:T(8,128)S(1)}, f32[1,35,8,128]{3,2,1,0:T(8,128)S(1)}, u32[]{:S(2)}, u32[]{:S(2)}) %collective-permute-start.9) | collective-permute-done | bytes 143392 | tf_op jit(solution)/shard_map/ppermute | solution.py:333
  172.4 3.0 %collective-permute-start.12 = (f32[2,29,8,128]{3,2,1,0:T(8,128)S(1)}, f32[2,29,8,128]{3,2,1,0:T(8,128)S(1)}, u32[]{:S(2)}, u32[]{:S(2)}) collective-permute-start(f32[2,29,8,128]{3,2,1,0:T(8,128)S(1)} %get-tuple-element.46), channel_id=1, source_target_pairs={{0,32},{4,36},{8,40},{12,44},{16,48},{20,52},{24,56},{28,60},{32,6... | collective-permute-start | bytes 712712 | tf_op jit(solution)/shard_map/ppermute | solution.py:333
  175.3 4.4 %collective-permute-done.12.v_last = f32[2,29,8,128]{3,2,1,0:T(8,128)S(1)} collective-permute-done((f32[2,29,8,128]{3,2,1,0:T(8,128)S(1)}, f32[2,29,8,128]{3,2,1,0:T(8,128)S(1)}, u32[]{:S(2)}, u32[]{:S(2)}) %collective-permute-start.12) | collective-permute-done | bytes 237600 | tf_op jit(solution)/shard_map/ppermute | solution.py:333
  183.1 5.3 %collective-permute-done.13.v_last = f32[2,25,8,128]{3,2,1,0:T(8,128)S(1)} collective-permute-done((f32[2,25,8,128]{3,2,1,0:T(8,128)S(1)}, f32[2,25,8,128]{3,2,1,0:T(8,128)S(1)}, u32[]{:S(2)}, u32[]{:S(2)}) %collective-permute-start.13) | collective-permute-done | bytes 204832 | tf_op jit(solution)/shard_map/ppermute | solution.py:333
  191.1 6.2 %collective-permute-done.14.v_last = f32[2,21,8,128]{3,2,1,0:T(8,128)S(1)} collective-permute-done((f32[2,21,8,128]{3,2,1,0:T(8,128)S(1)}, f32[2,21,8,128]{3,2,1,0:T(8,128)S(1)}, u32[]{:S(2)}, u32[]{:S(2)}) %collective-permute-start.14) | collective-permute-done | bytes 172064 | tf_op jit(solution)/shard_map/ppermute | solution.py:333
  197.3 3.8 %shard_map.60 = f32[8,17,8,128]{3,2,1,0:T(8,128)S(1)} custom-call(s32[1]{0:T(128)} %bitcast.4.flag, f32[47,8,128]{2,1,0:T(8,128)S(1)} %dynamic-slice_bitcast_fusion.d_ref, f32[9,45,8,128]{3,2,1,0:T(8,128)S(1)} %get-tuple-element.39.rest_0_.v2, f32[2,47,8,128]{3,2,1,0:T(8,128)S(1)} %collective-permute-done.6.refs_0_.g_last, ...), custom_call_target="tpu_custom_call" | custom-call | tf_op jit(solution)/shard_map/pallas_call | solution.py:34
  201.1 20.3 %all_to_all.11 = f32[8,17,8,128]{3,2,1,0:T(8,128)S(1)} all-to-all(f32[8,17,8,128]{3,2,1,0:T(8,128)S(1)} %shard_map.60), channel_id=1, replica_groups={{0,4,8,12,16,20,24,28},{32,36,40,44,48,52,56,60},{64,68,72,76,80,84,88,..., dimensions={0} | all-to-all | bytes 1114112 | tf_op jit(solution)/shard_map/all_to_all | solution.py:426
  223.8 18.2 %collective-permute-done.15.e1 = f32[1,136,8,128]{3,2,1,0:T(8,128)S(1)} collective-permute-done((f32[1,136,8,128]{3,2,1,0:T(8,128)S(1)}, f32[1,136,8,128]{3,2,1,0:T(8,128)S(1)}, u32[]{:S(2)}, u32[]{:S(2)}) %collective-permute-start.15) | collective-permute-done | bytes 557088 | tf_op jit(solution)/shard_map/ppermute | solution.py:328
  242.1 2.8 shard_map.61
  246.8 13.5 %collective-permute-done.16.prev = f32[1,132,8,128]{3,2,1,0:T(8,128)S(1)} collective-permute-done((f32[1,132,8,128]{3,2,1,0:T(8,128)S(1)}, f32[1,132,8,128]{3,2,1,0:T(8,128)S(1)}, u32[]{:S(2)}, u32[]{:S(2)}) %collective-permute-start.16) | collective-permute-done | bytes 540704 | tf_op jit(solution)/shard_map/ppermute | solution.py:328
  264.8 13.5 %collective-permute-done.17.prev = f32[1,130,8,128]{3,2,1,0:T(8,128)S(1)} collective-permute-done((f32[1,130,8,128]{3,2,1,0:T(8,128)S(1)}, f32[1,130,8,128]{3,2,1,0:T(8,128)S(1)}, u32[]{:S(2)}, u32[]{:S(2)}) %collective-permute-start.17) | collective-permute-done | bytes 532512 | tf_op jit(solution)/shard_map/ppermute | solution.py:328
  278.2 4.5 %shard_map.63 = (f32[2,1024,128]{2,1,0:T(8,128)}, f32[2,1024,128]{2,1,0:T(8,128)}) custom-call(f32[6,172,8,128]{3,2,1,0:T(8,128)S(1)} %bitcast.11, f32[2,130,8,128]{3,2,1,0:T(8,128)S(1)} %get-tuple-element.54.v4, f32[1,130,8,128]{3,2,1,0:T(8,128)S(1)} %collective-permute-done.17.prev), custom_call_target="tpu_custom_call" | custom-call | tf_op jit(solution)/shard_map/pallas_call | solution.py:34
  (51 shorter events, 33.1 us)
Async XLA Ops:
  0.6 1.2 copy-start.3
  1.9 1.2 copy-start.4
  3.1 1.0 copy-start.5
  6.0 6.5 %collective-permute-start = (f32[5,22,8,128]{3,2,1,0:T(8,128)S(1)}, f32[5,22,8,128]{3,2,1,0:T(8,128)S(1)}, u32[]{:S(2)}, u32[]{:S(2)}) collective-permute-start(f32[5,22,8,128]{3,2,1,0:T(8,128)S(1)} %get-tuple-element.31), channel_id=1, source_target_pairs={{0,1},{1,0},{2,3},{3,2},{4,5},{5,4},{6,7},{7,6},{8,9},{9,8},{10,11... | collective-permute-start | bytes 1351688 | tf_op jit(solution)/shard_map/ppermute | solution.py:352
  6.1 15.9 %collective-permute-start.1 = (f32[5,22,8,128]{3,2,1,0:T(8,128)S(1)}, f32[5,22,8,128]{3,2,1,0:T(8,128)S(1)}, u32[]{:S(2)}, u32[]{:S(2)}) collective-permute-start(f32[5,22,8,128]{3,2,1,0:T(8,128)S(1)} %get-tuple-element.32), channel_id=1, source_target_pairs={{1,2},{2,1},{5,6},{6,5},{9,10},{10,9},{13,14},{14,13},{17,18},{18,... | collective-permute-start | bytes 1351688 | tf_op jit(solution)/shard_map/ppermute | solution.py:354
  8.5 25.3 %collective-permute-start.2 = (f32[1,128,8,128]{3,2,1,0:T(8,128)S(1)}, f32[1,128,8,128]{3,2,1,0:T(8,128)S(1)}, u32[]{:S(2)}, u32[]{:S(2)}) collective-permute-start(f32[1,128,8,128]{3,2,1,0:T(8,128)S(1)} %get-tuple-element.33), channel_id=1, source_target_pairs={{0,4},{4,8},{8,12},{12,16},{16,20},{20,24},{24,28},{28,32},{32,36}... | collective-permute-start | bytes 1572872 | tf_op jit(solution)/shard_map/ppermute | solution.py:328
  22.1 16.8 %collective-permute-start.3 = (f32[2,22,8,128]{3,2,1,0:T(8,128)S(1)}, f32[2,22,8,128]{3,2,1,0:T(8,128)S(1)}, u32[]{:S(2)}, u32[]{:S(2)}) collective-permute-start(f32[2,22,8,128]{3,2,1,0:T(8,128)S(1)} %pad_maximum_fusion), channel_id=1, source_target_pairs={{0,4},{4,8},{8,12},{12,16},{16,20},{20,24},{24,28},{28,32},{32,36}... | collective-permute-start | bytes 540680 | tf_op jit(solution)/shard_map/ppermute | solution.py:328
  43.0 37.9 %copy-start = (f32[6,172,8,128]{3,2,1,0:T(8,128)}, f32[6,172,8,128]{3,2,1,0:T(8,128)S(1)}, u32[]{:S(2)}) copy-start(f32[6,172,8,128]{3,2,1,0:T(8,128)S(1)} %get-tuple-element.34.ext) | copy-start | bytes 12681220
  43.0 17.1 %collective-permute-start.4 = (f32[1,170,8,128]{3,2,1,0:T(8,128)S(1)}, f32[1,170,8,128]{3,2,1,0:T(8,128)S(1)}, u32[]{:S(2)}, u32[]{:S(2)}) collective-permute-start(f32[1,170,8,128]{3,2,1,0:T(8,128)S(1)} %get-tuple-element.36), channel_id=1, source_target_pairs={{0,4},{4,8},{8,12},{12,16},{16,20},{20,24},{24,28},{28,32},{32,36}... | collective-permute-start | bytes 2088968 | tf_op jit(solution)/shard_map/ppermute | solution.py:328
  63.3 17.7 %collective-permute-start.5 = (f32[1,168,8,128]{3,2,1,0:T(8,128)S(1)}, f32[1,168,8,128]{3,2,1,0:T(8,128)S(1)}, u32[]{:S(2)}, u32[]{:S(2)}) collective-permute-start(f32[1,168,8,128]{3,2,1,0:T(8,128)S(1)} %get-tuple-element.38), channel_id=1, source_target_pairs={{0,4},{4,8},{8,12},{12,16},{16,20},{20,24},{24,28},{28,32},{32,36}... | collective-permute-start | bytes 2064392 | tf_op jit(solution)/shard_map/ppermute | solution.py:328
  84.1 0.8 copy-start.1
  103.9 14.2 %collective-permute-start.6 = (f32[2,47,8,128]{3,2,1,0:T(8,128)}, f32[2,47,8,128]{3,2,1,0:T(8,128)S(1)}, u32[]{:S(2)}, u32[]{:S(2)}) collective-permute-start(f32[2,47,8,128]{3,2,1,0:T(8,128)} %slice.66), channel_id=1, source_target_pairs={{0,32},{4,36},{8,40},{12,44},{16,48},{20,52},{24,56},{28,60},{32,6... | collective-permute-start | bytes 1155080 | tf_op jit(solution)/shard_map/ppermute | solution.py:333
  127.3 10.9 %collective-permute-start.7 = (f32[2,43,8,128]{3,2,1,0:T(8,128)S(1)}, f32[2,43,8,128]{3,2,1,0:T(8,128)S(1)}, u32[]{:S(2)}, u32[]{:S(2)}) collective-permute-start(f32[2,43,8,128]{3,2,1,0:T(8,128)S(1)} %get-tuple-element.40), channel_id=1, source_target_pairs={{0,32},{4,36},{8,40},{12,44},{16,48},{20,52},{24,56},{28,60},{32,6... | collective-permute-start | bytes 1056776 | tf_op jit(solution)/shard_map/ppermute | solution.py:333
  142.0 10.1 %collective-permute-start.8 = (f32[2,39,8,128]{3,2,1,0:T(8,128)S(1)}, f32[2,39,8,128]{3,2,1,0:T(8,128)S(1)}, u32[]{:S(2)}, u32[]{:S(2)}) collective-permute-start(f32[2,39,8,128]{3,2,1,0:T(8,128)S(1)} %get-tuple-element.43.refs_1_.g_own), channel_id=1, source_target_pairs={{0,32},{4,36},{8,40},{12,44},{16,48},{20,52},{24,56},{28,60},{32,6... | collective-permute-start | bytes 958472 | tf_op jit(solution)/shard_map/ppermute | solution.py:333
  154.2 9.2 %collective-permute-start.11 = (f32[1,35,8,128]{3,2,1,0:T(8,128)S(1)}, f32[1,35,8,128]{3,2,1,0:T(8,128)S(1)}, u32[]{:S(2)}, u32[]{:S(2)}) collective-permute-start(f32[1,35,8,128]{3,2,1,0:T(8,128)S(1)} %get-tuple-element.45.refs_3_), channel_id=1, source_target_pairs={{0,32},{4,36},{8,40},{12,44},{16,48},{20,52},{24,56},{28,60},{32,6... | collective-permute-start | bytes 430088 | tf_op jit(solution)/shard_map/ppermute | solution.py:333
  154.3 9.1 %collective-permute-start.10 = (f32[1,35,8,128]{3,2,1,0:T(8,128)S(1)}, f32[1,35,8,128]{3,2,1,0:T(8,128)S(1)}, u32[]{:S(2)}, u32[]{:S(2)}) collective-permute-start(f32[1,35,8,128]{3,2,1,0:T(8,128)S(1)} %get-tuple-element.45.refs_3_), channel_id=1, source_target_pairs={{0,64},{4,68},{8,72},{12,76},{16,80},{20,84},{24,88},{28,92},{32,9... | collective-permute-start | bytes 430088 | tf_op jit(solution)/shard_map/ppermute | solution.py:333
  157.5 12.8 %collective-permute-start.9 = (f32[1,35,8,128]{3,2,1,0:T(8,128)S(1)}, f32[1,35,8,128]{3,2,1,0:T(8,128)S(1)}, u32[]{:S(2)}, u32[]{:S(2)}) collective-permute-start(f32[1,35,8,128]{3,2,1,0:T(8,128)S(1)} %get-tuple-element.45.refs_3_), channel_id=1, source_target_pairs={{0,96},{4,100},{8,104},{12,108},{16,112},{20,116},{24,120},{28,124... | collective-permute-start | bytes 430088 | tf_op jit(solution)/shard_map/ppermute | solution.py:333
  172.4 7.4 %collective-permute-start.12 = (f32[2,29,8,128]{3,2,1,0:T(8,128)S(1)}, f32[2,29,8,128]{3,2,1,0:T(8,128)S(1)}, u32[]{:S(2)}, u32[]{:S(2)}) collective-permute-start(f32[2,29,8,128]{3,2,1,0:T(8,128)S(1)} %get-tuple-element.46), channel_id=1, source_target_pairs={{0,32},{4,36},{8,40},{12,44},{16,48},{20,52},{24,56},{28,60},{32,6... | collective-permute-start | bytes 712712 | tf_op jit(solution)/shard_map/ppermute | solution.py:333
  179.8 62.3 %slice-start = ((s8[4227072]{0:T(1024)(128)(4,1)}), s8[4194304]{0:T(1024)(128)(4,1)S(1)}, s32[]{:S(2)}) async-start(s8[4227072]{0:T(1024)(128)(4,1)} %bitcast.10), calls=%async_computation.2 | async-start | bytes 8388608
  181.3 7.0 %collective-permute-start.13 = (f32[2,25,8,128]{3,2,1,0:T(8,128)S(1)}, f32[2,25,8,128]{3,2,1,0:T(8,128)S(1)}, u32[]{:S(2)}, u32[]{:S(2)}) collective-permute-start(f32[2,25,8,128]{3,2,1,0:T(8,128)S(1)} %get-tuple-element.48), channel_id=1, source_target_pairs={{0,32},{4,36},{8,40},{12,44},{16,48},{20,52},{24,56},{28,60},{32,6... | collective-permute-start | bytes 614408 | tf_op jit(solution)/shard_map/ppermute | solution.py:333
  188.4 53.7 %slice-start.1 = ((s8[4227072]{0:T(1024)(128)(4,1)}), s8[32768]{0:T(1024)(128)(4,1)S(1)}, s32[]{:S(2)}) async-start(s8[4227072]{0:T(1024)(128)(4,1)} %bitcast.10), calls=%async_computation.3 | async-start | bytes 65536
  190.6 6.7 %collective-permute-start.14 = (f32[2,21,8,128]{3,2,1,0:T(8,128)S(1)}, f32[2,21,8,128]{3,2,1,0:T(8,128)S(1)}, u32[]{:S(2)}, u32[]{:S(2)}) collective-permute-start(f32[2,21,8,128]{3,2,1,0:T(8,128)S(1)} %get-tuple-element.50), channel_id=1, source_target_pairs={{0,32},{4,36},{8,40},{12,44},{16,48},{20,52},{24,56},{28,60},{32,6... | collective-permute-start | bytes 516104 | tf_op jit(solution)/shard_map/ppermute | solution.py:333
  201.1 41.0 %copy-start.2 = (f32[1,168,8,128]{3,2,1,0:T(8,128)S(1)}, f32[1,168,8,128]{3,2,1,0:T(8,128)}, u32[]{:S(2)}) copy-start(f32[1,168,8,128]{3,2,1,0:T(8,128)} %copy-done.1) | copy-start | bytes 2064388
  221.4 20.7 %collective-permute-start.15 = (f32[1,136,8,128]{3,2,1,0:T(8,128)S(1)}, f32[1,136,8,128]{3,2,1,0:T(8,128)S(1)}, u32[]{:S(2)}, u32[]{:S(2)}) collective-permute-start(f32[1,136,8,128]{3,2,1,0:T(8,128)S(1)} %bitcast.12), channel_id=1, source_target_pairs={{0,4},{4,8},{8,12},{12,16},{16,20},{20,24},{24,28},{28,32},{32,36}... | collective-permute-start | bytes 1671176 | tf_op jit(solution)/shard_map/ppermute | solution.py:328
  244.9 15.5 %collective-permute-start.16 = (f32[1,132,8,128]{3,2,1,0:T(8,128)S(1)}, f32[1,132,8,128]{3,2,1,0:T(8,128)S(1)}, u32[]{:S(2)}, u32[]{:S(2)}) collective-permute-start(f32[1,132,8,128]{3,2,1,0:T(8,128)S(1)} %get-tuple-element.53), channel_id=1, source_target_pairs={{0,4},{4,8},{8,12},{12,16},{16,20},{20,24},{24,28},{28,32},{32,36}... | collective-permute-start | bytes 1622024 | tf_op jit(solution)/shard_map/ppermute | solution.py:328
  262.9 15.4 %collective-permute-start.17 = (f32[1,130,8,128]{3,2,1,0:T(8,128)S(1)}, f32[1,130,8,128]{3,2,1,0:T(8,128)S(1)}, u32[]{:S(2)}, u32[]{:S(2)}) collective-permute-start(f32[1,130,8,128]{3,2,1,0:T(8,128)S(1)} %get-tuple-element.55), channel_id=1, source_target_pairs={{0,4},{4,8},{8,12},{12,16},{16,20},{20,24},{24,28},{28,32},{32,36}... | collective-permute-start | bytes 1597448 | tf_op jit(solution)/shard_map/ppermute | solution.py:328

commit v2 on v1

--- a/solution.py
+++ b/solution.py
@@ -13,13 +13,10 @@
 
 SIDE = 32
 OWN = 128
-HALO = 22
-EXT = OWN + 2 * HALO
 GROUP = 8
-PIECE = 17
-WIDE = PIECE + 30
-COARSE = GROUP * PIECE + 30
-LOW = HALO - 19
+PIECE = OWN // GROUP
+HALO = 15
+WIDE = PIECE + 2 * HALO
 F32 = jnp.float32
 
 VM = pl.BlockSpec(memory_space=pltpu.VMEM)
@@ -53,7 +50,7 @@
 
 
 def width(steps):
-    return max(1, 16 // steps)
+    return max(1, 24 // steps)
 
 
 def moved(at, by):
@@ -85,120 +82,182 @@
     return p, beside(p, m) + ref[t0:t1, moved(z, -1)] + ref[t0:t1, moved(z, 1)]
 
 
-def transposed_in(flag, v_ref, g_ref, d_ref, out, tail, edge_a, edge_b):
-    for t in range(5):
-        ref = v_ref if t < 2 else g_ref
-        for s in range(8):
-            rows = slice(s * 128, (s + 1) * 128)
-            block = d_ref[rows, :] if t == 4 else ref[t % 2, rows, :]
-            out[t, :, s, :] = block.T
-            if t == 1:
-                tail[0, :, s, :] = block.T
+def turn_in(ref, store):
+    for s in range(8):
+        store(s, ref[s * 128 : (s + 1) * 128, :].T)
+
+
+def turn_out(ref, out):
+    for s in range(8):
+        out[s * 128 : (s + 1) * 128, :] = ref[:, s, :].T
+
+
+def share_edges(odd, ref, edge_a, edge_b):
+    n = edge_a.shape[1]
+    far = OWN - n
+    edge_a[...] = ref[:, pl.ds(far * (1 - odd), n)]
+    edge_b[...] = ref[:, pl.ds(far * odd, n)]
+
+
+def step_over(odd, src, row, edge_a, edge_b, edge_row, fn):
+    m = masks()
+    t = slice(row, row + 1)
+    a = edge_a[edge_row : edge_row + 1]
+    b = edge_b[edge_row : edge_row + 1]
+    low = jnp.where(odd > 0, a, b)
+    high = jnp.where(odd > 0, b, a)
+    p = src[t, 0:1]
+    fn(pl.ds(0, 1), p, beside(p, m) + low + src[t, 1:2])
+    p = src[t, OWN - 1 : OWN]
+    fn(pl.ds(OWN - 1, 1), p, beside(p, m) + high + src[t, OWN - 2 : OWN - 1])
+    planes(1, OWN - 1, 18, lambda z: fn(z, *spread(src, row, row + 1, z, m)))
+
+
+def swept(fixed, step, z, p, near, before):
+    g = fixed[step : step + 1, z]
+    return keep * p + fixed[3, z] * (g + base_coef * before[0:1, z] + fixed[2, z] * near)
+
+
+def left(fixed, step, z, p, near, before):
+    d = fixed[2, z]
+    known = fixed[step : step + 1, z] + base_coef * before[0:1, z] + d * near
+    return known - (base_coef + 6.0 * d) * p
+
+
+def sweep_late(flag, fixed, x, x_a, x_b, y1, out_a, out_b):
     odd = flag[0]
-    far = OWN - HALO
-    start_a = far * (1 - odd)
-    start_b = far * odd
-
-    def edge(z):
-        edge_a[:, z] = out[:, moved(z, start_a)]
-        edge_b[:, z] = out[:, moved(z, start_b)]
-
-    planes(0, HALO, 2, edge)
-
-
-def first_level(flag, own, edge_a, edge_b, back, back_edge, ext, v1, tail, prev):
+
+    def fn(z, p, near):
+        y1[:, z] = swept(fixed, 1, z, p, near, x)
+
+    step_over(odd, x, 1, x_a, x_b, 1, fn)
+    share_edges(odd, y1, out_a, out_b)
+
+
+def sweep_both(flag, fixed, x, x_a, x_b, prev, y1, y1_a, y1_b, y0, z1, out_a, out_b):
+    odd = flag[0]
+
+    def early(z, p, near):
+        y0[:, z] = swept(fixed, 0, z, p, near, prev)
+
+    step_over(odd, x, 0, x_a, x_b, 0, early)
+
+    def late(z, p, near):
+        z1[:, z] = swept(fixed, 1, z, p, near, y0)
+
+    step_over(odd, y1, 0, y1_a, y1_b, 0, late)
+    share_edges(odd, y0, out_a.at[0:1], out_b.at[0:1])
+    share_edges(odd, z1, out_a.at[1:2], out_b.at[1:2])
+
+
+def sweep_both_raw(flag, fixed, x, x_a, x_b, back, y1, y1_a, y1_b, y0, z1, out_a, out_b, prev):
+    def store(s, block):
+        prev[0, :, s, :] = block
+
+    turn_in(back.at[0], store)
+    sweep_both(flag, fixed, x, x_a, x_b, prev, y1, y1_a, y1_b, y0, z1, out_a, out_b)
+
+
+def sweep_early(flag, fixed, y0, y_a, y_b, prev, z0, out_a, out_b):
+    odd = flag[0]
+
+    def fn(z, p, near):
+        z0[:, z] = swept(fixed, 0, z, p, near, prev)
+
+    step_over(odd, y0, 0, y_a, y_b, 0, fn)
+    share_edges(odd, z0, out_a, out_b)
+
+
+def turned(flag, v_ref, g_ref, d_ref, v0, fixed, edge_a, edge_b):
+    def into(ref, row):
+        def store(s, block):
+            ref[row, :, s, :] = block
+
+        return store
+
+    for t in range(2):
+        turn_in(v_ref.at[t], into(v0, t))
+    share_edges(flag[0], v0, edge_a, edge_b)
+    for t in range(2):
+        turn_in(g_ref.at[t], into(fixed, t))
+    turn_in(d_ref, into(fixed, 2))
+
+    def scale(z):
+        fixed[3, z] = damping / (base_coef + 6.0 * fixed[2, z])
+
+    planes(0, OWN, 8, scale)
+
+
+def restrict_left(flag, fixed, z0, z1, e0a, e0b, e1a, e1b, prev, out, out_a, out_b):
+    odd = flag[0]
+
+    def early(z, p, near):
+        out[0:1, z] = 0.5 * left(fixed, 0, z, p, near, prev)
+        out[1:2, z] = fixed[2:3, z]
+
+    def late(z, p, near):
+        out[0:1, z] += 0.5 * left(fixed, 1, z, p, near, z0)
+
+    step_over(odd, z0, 0, e0a, e0b, 0, early)
+    step_over(odd, z1, 0, e1a, e1b, 1, late)
+    share_edges(odd, out, out_a, out_b)
+
+
+def cut(flag, own, edge_a, edge_b, pieces, d_piece, tall):
     odd = flag[0]
     end = OWN + HALO
-    at_a = end * (1 - odd)
-    at_b = end * odd
-
-    def centre(z):
-        ext[0:5, moved(z, HALO)] = own[:, z]
-        prev[0, moved(z, HALO)] = back[0, z]
-
-    def edge(z):
-        ext[0:5, moved(z, at_a)] = edge_a[:, z]
-        ext[0:5, moved(z, at_b)] = edge_b[:, z]
-        prev[0, moved(z, at_a)] = back_edge[0, z]
-        prev[0, moved(z, at_b)] = back_edge[1, z]
-
-    planes(0, OWN, 4, centre)
-    planes(0, HALO, 2, edge)
-
-    def scale(z):
-        ext[5, z] = damping / (base_coef + 6.0 * ext[4, z])
-
-    planes(0, EXT, 8, scale)
-    pair_sweep(ext, ext, 0, prev, 0, v1, tail, 1, 1, EXT - 1)
-
-
-def pair_sweep(ext, src, off, prev, off_prev, dst, tail, off_dst, low, high):
-    m = masks()
-
-    def fn(z):
-        p, near = spread(src, 0, 2, moved(z, -off), m)
-        before = jnp.concatenate([prev[0:1, moved(z, -off_prev)], p[0:1]], axis=0)
-        value = keep * p + ext[5, z] * (ext[2:4, z] + base_coef * before + ext[4, z] * near)
-        dst[:, moved(z, -off_dst)] = value
-        tail[:, moved(z, -off_dst)] = value[1:2]
-
-    planes(low, high, 8, fn)
-
-
-def pair_left(ext, src, off, prev, off_prev, low, high, store):
-    m = masks()
-
-    def fn(z):
-        p, near = spread(src, 0, 2, moved(z, -off), m)
-        d = ext[4, z]
-        before = jnp.concatenate([prev[0:1, moved(z, -off_prev)], p[0:1]], axis=0)
-        store(z, ext[2:4, z] + base_coef * before + d * near - (base_coef + 6.0 * d) * p)
-
-    planes(low, high, 8, fn)
-
-
-def second_sweep(ext, v1, prev, v2, tail):
-    pair_sweep(ext, v1, 1, prev, 1, v2, tail, 2, 2, EXT - 2)
-
-
-def restrict_left(ext, v2, prev, out):
-    def store(z, r):
-        out[:, moved(z, -LOW)] = 0.5 * (r[0:1] + r[1:2])
-
-    pair_left(ext, v2, 2, prev, 2, LOW, LOW + COARSE, store)
-
-
-FIN = OWN + 2
-FIRST = HALO - 1
-E_LOW = HALO - 4
-
-
-def third_sweep(ext, v2, prev, e0, e1, v3, tail, va, vp):
+    tall[:, pl.ds(end * (1 - odd), HALO)] = edge_a[...]
+    tall[:, pl.ds(end * odd, HALO)] = edge_b[...]
+
+    def copy(z):
+        tall[:, moved(z, HALO)] = own[:, z]
+
+    planes(0, OWN, 8, copy)
+    for i in range(GROUP):
+        pieces[i] = tall[0, i * PIECE : i * PIECE + WIDE]
+    d_piece[...] = tall[1, pl.ds(flag[1], WIDE)]
+
+
+def corrected_late(
+    flag, fixed, z0, z1, e0a, e0b, e1a, e1b, e, e_a, e_b, x, x_a, x_b, y1, out_a, out_b
+):
     def add(z):
-        here = moved(z, -2)
-        there = moved(z, -E_LOW)
-        va[:, moved(z, -FIRST + 2)] = v2[:, here] + e0[:, there]
-        vp[:, moved(z, -FIRST + 2)] = prev[:, here] + e1[:, there]
-
-    planes(FIRST - 2, FIRST + FIN + 2, 8, add)
-    pair_sweep(ext, va, FIRST - 2, vp, FIRST - 2, v3, tail, FIRST - 1, FIRST - 1, FIRST + FIN + 1)
-
-
-def fourth_sweep(ext, v3, prev, v4, tail):
-    pair_sweep(ext, v3, FIRST - 1, prev, FIRST - 1, v4, tail, FIRST, FIRST, FIRST + FIN)
-
-
-def finish(ext, v4, prev, sol_out, res_out, res):
-    def store(z, r):
-        res[:, moved(z, -HALO)] = r
-
-    for t in range(2):
-        for s in range(8):
-            sol_out[t, s * 128 : (s + 1) * 128, :] = v4[t, 1 : OWN + 1, s, :].T
-    pair_left(ext, v4, FIRST, prev, FIRST, HALO, HALO + OWN, store)
-    for t in range(2):
-        for s in range(8):
-            res_out[t, s * 128 : (s + 1) * 128, :] = res[t, :, s, :].T
+        x[0:1, z] = z0[:, z] + e[:, z]
+        x[1:2, z] = z1[:, z] + e[:, z]
+
+    planes(0, OWN, 8, add)
+    x_a[0:1] = e0a[...] + e_a[...]
+    x_b[0:1] = e0b[...] + e_b[...]
+    x_a[1:2] = e1a[1:2] + e_a[...]
+    x_b[1:2] = e1b[1:2] + e_b[...]
+    sweep_late(flag, fixed, x, x_a, x_b, y1, out_a, out_b)
+
+
+def corrected_both(
+    flag, fixed, x, x_a, x_b, prev, e_prev, y1, y1_a, y1_b, y0, z1, out_a, out_b, total
+):
+    def add(z):
+        total[:, z] = prev[:, z] + e_prev[:, z]
+
+    planes(0, OWN, 8, add)
+    sweep_both(flag, fixed, x, x_a, x_b, total, y1, y1_a, y1_b, y0, z1, out_a, out_b)
+
+
+def finish(flag, fixed, z0, z1, e0a, e0b, e1a, e1b, prev, sol_out, res_out, res):
+    odd = flag[0]
+    turn_out(z0.at[0], sol_out.at[0])
+    turn_out(z1.at[0], sol_out.at[1])
+
+    def late(z, p, near):
+        res[1:2, z] = left(fixed, 1, z, p, near, z0)
+
+    def early(z, p, near):
+        res[0:1, z] = left(fixed, 0, z, p, near, prev)
+
+    step_over(odd, z1, 0, e1a, e1b, 1, late)
+    turn_out(res.at[1], res_out.at[1])
+    step_over(odd, z0, 0, e0a, e0b, 0, early)
+    turn_out(res.at[0], res_out.at[0])
 
 
 def step_down(flag, d_ref, *refs, counts, own, c, low, last, tail_steps):
@@ -338,37 +397,55 @@
     slabs = lax.axis_size("gz")
     count = lax.axis_size("tm")
     odd = (lax.axis_index("gz") % 2).astype(jnp.int32).reshape(1)
-    me = lax.axis_index("tm")
-    q = (me // GROUP).astype(jnp.int32).reshape(1)
-    piece = me % GROUP
+    me = lax.axis_index("tm").astype(jnp.int32)
+    q = (me // GROUP).reshape(1)
+    piece = jnp.concatenate([odd, (me % GROUP * PIECE).reshape(1)])
+    pairs = [(i, i + 1) for i in range(1, slabs - 1, 2)]
+    pairs = pairs + [(b, a) for a, b in pairs]
+
+    def swapped(edge_a, edge_b):
+        return (
+            lax.ppermute(edge_a, "gz", [(i, i ^ 1) for i in range(slabs)]),
+            lax.ppermute(edge_b, "gz", pairs),
+        )
 
     flat = lambda a: a.reshape(a.shape[:-3] + (SIDE * SIDE, OWN))
-    own, tail, edge_a, edge_b = call(
-        transposed_in,
-        [(5, OWN) + T, (1, OWN) + T, (5, HALO) + T, (5, HALO) + T],
-        (odd, flat(initial_guess), flat(source), flat(diffusivity)),
+    guess = flat(initial_guess)
+    prev = later(guess[1:2], 1)
+    plane = (1, OWN) + T
+    edge = [(1, 1) + T] * 2
+    edges = [(2, 1) + T] * 2
+    run = functools.partial(call, n_scalar=1)
+    x, fixed, *ends = run(
+        turned,
+        [(2, OWN) + T, (4, OWN) + T] + edges,
+        (odd, guess, flat(source), flat(diffusivity)),
+    )
+    x = (x, *swapped(*ends))
+    y1, *ends = run(sweep_late, [plane] + edge, (odd, fixed, *x))
+    y1_prev = later(y1, 1)
+    y0, z1, *ends = run(
+        sweep_both_raw,
+        [plane, plane] + edges,
+        (odd, fixed, *x, prev, y1, *swapped(*ends)),
+        scratch=[plane],
+    )
+    v2_prev = later(z1, 1)
+    late_ends = swapped(*ends)
+    z0, *ends = run(sweep_early, [plane] + edge, (odd, fixed, y0, *late_ends, y1_prev))
+    v2 = (z0, z1, *swapped(*ends), *late_ends)
+    g1, *ends = run(
+        restrict_left, [(2, OWN) + T] + [(2, HALO) + T] * 2, (odd, fixed, *v2, v2_prev)
+    )
+    pieces, d = call(
+        cut,
+        [(GROUP, WIDE) + T, (WIDE,) + T],
+        (piece, g1, *swapped(*ends)),
+        scratch=[(2, OWN + 2 * HALO) + T],
         n_scalar=1,
     )
-    edge_a = lax.ppermute(edge_a, "gz", [(i, i ^ 1) for i in range(slabs)])
-    pairs = [(i, i + 1) for i in range(1, slabs - 1, 2)]
-    edge_b = lax.ppermute(edge_b, "gz", pairs + [(b, a) for a, b in pairs])
-    prev = later(tail, 1)
-    prev_edge = later(jnp.stack([edge_a[1], edge_b[1]]), 1)
-    ext, v1, tail = call(
-        first_level,
-        [(6, EXT) + T, (2, EXT - 2) + T, (1, EXT - 2) + T],
-        (odd, own, edge_a, edge_b, prev, prev_edge),
-        scratch=[(1, EXT) + T],
-        n_scalar=1,
-    )
-    v2, tail = call(second_sweep, [(2, EXT - 4) + T, (1, EXT - 4) + T], (ext, v1, later(tail, 1)))
-    v2_prev = later(tail, 1)
-    g1 = call(restrict_left, (1, COARSE) + T, (ext, v2, v2_prev))[0]
-
     groups = [list(range(a, a + GROUP)) for a in range(0, count, GROUP)]
-    pieces = jnp.stack([g1[PIECE * b : PIECE * b + WIDE] for b in range(GROUP)])
     g = lax.all_to_all(pieces, "tm", 0, 0, axis_index_groups=groups, tiled=True)
-    d = lax.dynamic_slice_in_dim(ext[4], LOW + PIECE * piece, WIDE, axis=0)
 
     saved = []
     own_steps = GROUP
@@ -424,18 +501,30 @@
         e = e[0]
         e_low += 2
     e0 = lax.all_to_all(e, "tm", 0, 0, axis_index_groups=groups, tiled=True)
-    e0 = e0.reshape((1, GROUP * PIECE) + T)
-    v3, tail = call(
-        third_sweep,
-        [(2, FIN + 2) + T, (1, FIN + 2) + T],
-        (ext, v2, v2_prev, e0, later(e0, 1)),
-        scratch=[(2, FIN + 4) + T, (1, FIN + 4) + T],
-    )
-    v4, tail = call(fourth_sweep, [(2, FIN) + T, (1, FIN) + T], (ext, v3, later(tail, 1)))
-    sol, res = call(
+    e0 = e0.reshape((1, OWN) + T)
+    e_prev = later(e0, 1)
+    side = (OWN - 1) * (1 - odd[0])
+    e_a = lax.dynamic_slice_in_dim(e0, side, 1, axis=1)
+    e_b = lax.dynamic_slice_in_dim(e0, OWN - 1 - side, 1, axis=1)
+    *x, y1, out_a, out_b = run(
+        corrected_late,
+        [(2, OWN) + T] + edges + [plane] + edge,
+        (odd, fixed, *v2, e0, *swapped(e_a, e_b)),
+    )
+    y1_prev = later(y1, 1)
+    y0, z1, *ends = run(
+        corrected_both,
+        [plane, plane] + edges,
+        (odd, fixed, *x, v2_prev, e_prev, y1, *swapped(out_a, out_b)),
+        scratch=[plane],
+    )
+    prev = later(z1, 1)
+    late_ends = swapped(*ends)
+    z0, *ends = run(sweep_early, [plane] + edge, (odd, fixed, y0, *late_ends, y1_prev))
+    sol, res = run(
         finish,
         [(2, SIDE * SIDE, OWN)] * 2,
-        (ext, v4, later(tail, 1)),
+        (odd, fixed, z0, z1, *swapped(*ends), *late_ends, prev),
         scratch=[(2, OWN) + T],
     )
     return sol.reshape(source.shape), res.reshape(source.shape)

time: 283 us -> 254 us (0.90)
  the two profiles are of different devices: /device:TPU:144 before, /device:TPU:3 now
where the time goes in v2:
time: 254 us; the launch traced here: 253 us
  waiting for transfers between devices  98 us (39%)
  starting transfers between devices  72.3 us (28%)
  Pallas kernels  40.9 us (16%)
  blocking collectives  28.6 us (11%)
  local copies, waits for them, and re-layouts  11.8 us (5%)
    ppermute x9, waiting for transfers between devices, around(): lax.ppermute(block, 'tm', [(i, (i + distance) % count) for i in range(cou...  53.9 us
    ppermute x9, waiting for transfers between devices, swapped(): lax.ppermute(edge_b, 'gz', pairs)  44.1 us
    pallas_call x17, Pallas kernels, call(): pl.pallas_call(body, out_shape=[jax.ShapeDtypeStruct(s, F32) for s in sha...  40.9 us
    ppermute x9, starting transfers between devices, swapped(): lax.ppermute(edge_b, 'gz', pairs)  38.9 us
    all_to_all x1, blocking collectives, body(): g = lax.all_to_all(pieces, 'tm', 0, 0, axis_index_groups=groups, tiled=True)  18.1 us
    ppermute x6, starting transfers between devices, later(): lax.ppermute(block, 'tm', [(i, i + distance) for i in range(count - dista...  16 us
    ppermute x9, starting transfers between devices, around(): lax.ppermute(block, 'tm', [(i, (i + distance) % count) for i in range(cou...  11.7 us
    all_to_all x1, blocking collectives, body(): e0 = lax.all_to_all(e, 'tm', 0, 0, axis_index_groups=groups, tiled=True)  10.5 us
  transfers between devices with their start and end apart: 33, of which 18 were waited for; matrix products, arithmetic and copies ran while one was open for 0% of the time, Pallas kernels for 6%

profile of v2, /device:TPU:3, one launch (start us, length us, event | category | flops | bytes accessed | tf_op | source)
XLA Modules:
  0.0 252.8 jit_solution(9449581817942305132)
XLA Ops:
  2.6 3.2 %collective-permute-start.2 = (f32[1,1024,128]{2,1,0:T(8,128)}, f32[1,1024,128]{2,1,0:T(8,128)}, u32[]{:S(2)}, u32[]{:S(2)}) collective-permute-start(f32[1,1024,128]{2,1,0:T(8,128)} %bitcast.4), channel_id=1, source_target_pairs={{0,4},{4,8},{8,12},{12,16},{16,20},{20,24},{24,28},{28,32},{32,36}... | collective-permute-start | bytes 1572872 | tf_op jit(solution)/shard_map/ppermute | solution.py:387
  10.9 4.4 %collective-permute-start.1 = (f32[2,1,8,128]{3,2,1,0:T(8,128)S(1)}, f32[2,1,8,128]{3,2,1,0:T(8,128)S(1)}, u32[]{:S(2)}, u32[]{:S(2)}) collective-permute-start(f32[2,1,8,128]{3,2,1,0:T(8,128)S(1)} %get-tuple-element.52), channel_id=1, source_target_pairs={{1,2},{2,1},{5,6},{6,5},{9,10},{10,9},{13,14},{14,13},{17,18},{18,... | collective-permute-start | bytes 24584 | tf_op jit(solution)/shard_map/ppermute | solution.py:409
  15.3 6.6 %collective-permute-done.1.x_b = f32[2,1,8,128]{3,2,1,0:T(8,128)S(1)} collective-permute-done((f32[2,1,8,128]{3,2,1,0:T(8,128)S(1)}, f32[2,1,8,128]{3,2,1,0:T(8,128)S(1)}, u32[]{:S(2)}, u32[]{:S(2)}) %collective-permute-start.1) | collective-permute-done | bytes 8224 | tf_op jit(solution)/shard_map/ppermute | solution.py:409
  27.5 4.9 %collective-permute-done.4.y1_b = f32[1,1,8,128]{3,2,1,0:T(8,128)S(1)} collective-permute-done((f32[1,1,8,128]{3,2,1,0:T(8,128)S(1)}, f32[1,1,8,128]{3,2,1,0:T(8,128)S(1)}, u32[]{:S(2)}, u32[]{:S(2)}) %collective-permute-start.4) | collective-permute-done | bytes 4128 | tf_op jit(solution)/shard_map/ppermute | solution.py:409
  32.4 3.7 %shard_map.52 = (f32[1,128,8,128]{3,2,1,0:T(8,128)S(1)}, f32[1,128,8,128]{3,2,1,0:T(8,128)S(1)}, f32[2,1,8,128]{3,2,1,0:T(8,128)S(1)}, f32[2,1,8,128]{3,2,1,0:T(8,128)S(1)}) custom-call(s32[1]{0:T(128)} %bitcast.flag, f32[4,128,8,128]{3,2,1,0:T(8,128)S(1)} %get-tuple-element.49.fixed, f32[2,128,8,128]{3,2,1,0:T(8,128)S(1)} %get-tuple-element.50.x, ...), custom_call_target="tpu_custom_call" | custom-call | tf_op jit(solution)/shard_map/pallas_call | solution.py:31
  36.1 3.7 %collective-permute-start.10 = (f32[1,128,8,128]{3,2,1,0:T(8,128)S(1)}, f32[1,128,8,128]{3,2,1,0:T(8,128)S(1)}, u32[]{:S(2)}, u32[]{:S(2)}) collective-permute-start(f32[1,128,8,128]{3,2,1,0:T(8,128)S(1)} %get-tuple-element.60.z1), channel_id=1, source_target_pairs={{0,4},{4,8},{8,12},{12,16},{16,20},{20,24},{24,28},{28,32},{32,36}... | collective-permute-start | bytes 1572872 | tf_op jit(solution)/shard_map/ppermute | solution.py:387
  39.9 3.2 %collective-permute-start.6 = (f32[2,1,8,128]{3,2,1,0:T(8,128)S(1)}, f32[2,1,8,128]{3,2,1,0:T(8,128)S(1)}, u32[]{:S(2)}, u32[]{:S(2)}) collective-permute-start(f32[2,1,8,128]{3,2,1,0:T(8,128)S(1)} %get-tuple-element.58), channel_id=1, source_target_pairs={{1,2},{2,1},{5,6},{6,5},{9,10},{10,9},{13,14},{14,13},{17,18},{18,... | collective-permute-start | bytes 24584 | tf_op jit(solution)/shard_map/ppermute | solution.py:409
  43.1 4.9 %collective-permute-done.6.y_b.e1b = f32[2,1,8,128]{3,2,1,0:T(8,128)S(1)} collective-permute-done((f32[2,1,8,128]{3,2,1,0:T(8,128)S(1)}, f32[2,1,8,128]{3,2,1,0:T(8,128)S(1)}, u32[]{:S(2)}, u32[]{:S(2)}) %collective-permute-start.6) | collective-permute-done | bytes 8224 | tf_op jit(solution)/shard_map/ppermute | solution.py:409
  49.4 4.8 %collective-permute-start.9 = (f32[1,1,8,128]{3,2,1,0:T(8,128)S(1)}, f32[1,1,8,128]{3,2,1,0:T(8,128)S(1)}, u32[]{:S(2)}, u32[]{:S(2)}) collective-permute-start(f32[1,1,8,128]{3,2,1,0:T(8,128)S(1)} %get-tuple-element.62), channel_id=1, source_target_pairs={{1,2},{2,1},{5,6},{6,5},{9,10},{10,9},{13,14},{14,13},{17,18},{18,... | collective-permute-start | bytes 12296 | tf_op jit(solution)/shard_map/ppermute | solution.py:409
  59.2 4.8 %collective-permute-start.12 = (f32[2,15,8,128]{3,2,1,0:T(8,128)S(1)}, f32[2,15,8,128]{3,2,1,0:T(8,128)S(1)}, u32[]{:S(2)}, u32[]{:S(2)}) collective-permute-start(f32[2,15,8,128]{3,2,1,0:T(8,128)S(1)} %get-tuple-element.65), channel_id=1, source_target_pairs={{1,2},{2,1},{5,6},{6,5},{9,10},{10,9},{13,14},{14,13},{17,18},{18,... | collective-permute-start | bytes 368648 | tf_op jit(solution)/shard_map/ppermute | solution.py:409
  68.9 18.1 %all_to_all.10.refs_1_.g_own = f32[8,46,8,128]{3,2,1,0:T(8,128)S(1)} all-to-all(f32[8,46,8,128]{3,2,1,0:T(8,128)S(1)} %get-tuple-element.67), channel_id=1, replica_groups={{0,4,8,12,16,20,24,28},{32,36,40,44,48,52,56,60},{64,68,72,76,80,84,88,..., dimensions={0} | all-to-all | bytes 3014656 | tf_op jit(solution)/shard_map/all_to_all | solution.py:448
  90.5 8.9 %collective-permute-done.13.refs_0_.g_last = f32[2,46,8,128]{3,2,1,0:T(8,128)S(1)} collective-permute-done((f32[2,46,8,128]{3,2,1,0:T(8,128)}, f32[2,46,8,128]{3,2,1,0:T(8,128)S(1)}, u32[]{:S(2)}, u32[]{:S(2)}) %collective-permute-start.13) | collective-permute-done | bytes 376864 | tf_op jit(solution)/shard_map/ppermute | solution.py:392
  100.8 6.6 %shard_map.56 = (f32[9,44,8,128]{3,2,1,0:T(8,128)S(1)}, f32[4,42,8,128]{3,2,1,0:T(8,128)S(1)}, f32[2,42,8,128]{3,2,1,0:T(8,128)S(1)}) custom-call(s32[1]{0:T(128)} %bitcast.5.flag, f32[46,8,128]{2,1,0:T(8,128)S(1)} %get-tuple-element.66.d_ref, f32[2,46,8,128]{3,2,1,0:T(8,128)S(1)} %collective-permute-done.13.refs_0_.g_last, f32[8,46,8,128]{3,2,1,0:T(8,128)S(1)} %copy-done.1), custom_call_target="tpu_custom_call" | custom-call | tf_op jit(solution)/shard_map/pallas_call | solution.py:31
  107.5 7.4 %collective-permute-done.14.refs_0_.g_last = f32[2,42,8,128]{3,2,1,0:T(8,128)S(1)} collective-permute-done((f32[2,42,8,128]{3,2,1,0:T(8,128)S(1)}, f32[2,42,8,128]{3,2,1,0:T(8,128)S(1)}, u32[]{:S(2)}, u32[]{:S(2)}) %collective-permute-start.14) | collective-permute-done | bytes 344096 | tf_op jit(solution)/shard_map/ppermute | solution.py:392
  114.9 3.3 %shard_map.57 = (f32[5,40,8,128]{3,2,1,0:T(8,128)S(1)}, f32[2,38,8,128]{3,2,1,0:T(8,128)S(1)}) custom-call(s32[1]{0:T(128)} %bitcast.5.flag, f32[46,8,128]{2,1,0:T(8,128)S(1)} %get-tuple-element.66.d_ref, f32[2,42,8,128]{3,2,1,0:T(8,128)S(1)} %collective-permute-done.14.refs_0_.g_last, f32[4,42,8,128]{3,2,1,0:T(8,128)S(1)} %get-tuple-element.70.refs_1_.g_own), custom_call_target="tpu_custom_call" | custom-call | tf_op jit(solution)/shard_map/pallas_call | solution.py:31
  118.3 7.8 %collective-permute-done.15.refs_0_.g_last = f32[2,38,8,128]{3,2,1,0:T(8,128)S(1)} collective-permute-done((f32[2,38,8,128]{3,2,1,0:T(8,128)S(1)}, f32[2,38,8,128]{3,2,1,0:T(8,128)S(1)}, u32[]{:S(2)}, u32[]{:S(2)}) %collective-permute-start.15) | collective-permute-done | bytes 311328 | tf_op jit(solution)/shard_map/ppermute | solution.py:392
  132.7 5.9 %collective-permute-done.16.refs_0_ = f32[1,34,8,128]{3,2,1,0:T(8,128)S(1)} collective-permute-done((f32[1,34,8,128]{3,2,1,0:T(8,128)S(1)}, f32[1,34,8,128]{3,2,1,0:T(8,128)S(1)}, u32[]{:S(2)}, u32[]{:S(2)}) %collective-permute-start.16) | collective-permute-done | bytes 139296 | tf_op jit(solution)/shard_map/ppermute | solution.py:392
  138.6 6.2 %collective-permute-done.17.refs_1_ = f32[1,34,8,128]{3,2,1,0:T(8,128)S(1)} collective-permute-done((f32[1,34,8,128]{3,2,1,0:T(8,128)S(1)}, f32[1,34,8,128]{3,2,1,0:T(8,128)S(1)}, u32[]{:S(2)}, u32[]{:S(2)}) %collective-permute-start.17) | collective-permute-done | bytes 139296 | tf_op jit(solution)/shard_map/ppermute | solution.py:392
  150.9 5.8 %collective-permute-done.19.v_last = f32[2,28,8,128]{3,2,1,0:T(8,128)S(1)} collective-permute-done((f32[2,28,8,128]{3,2,1,0:T(8,128)S(1)}, f32[2,28,8,128]{3,2,1,0:T(8,128)S(1)}, u32[]{:S(2)}, u32[]{:S(2)}) %collective-permute-start.19) | collective-permute-done | bytes 229408 | tf_op jit(solution)/shard_map/ppermute | solution.py:392
  159.6 5.5 %collective-permute-done.20.v_last = f32[2,24,8,128]{3,2,1,0:T(8,128)S(1)} collective-permute-done((f32[2,24,8,128]{3,2,1,0:T(8,128)S(1)}, f32[2,24,8,128]{3,2,1,0:T(8,128)S(1)}, u32[]{:S(2)}, u32[]{:S(2)}) %collective-permute-start.20) | collective-permute-done | bytes 196640 | tf_op jit(solution)/shard_map/ppermute | solution.py:392
  167.3 5.1 %collective-permute-done.21.v_last = f32[2,20,8,128]{3,2,1,0:T(8,128)S(1)} collective-permute-done((f32[2,20,8,128]{3,2,1,0:T(8,128)S(1)}, f32[2,20,8,128]{3,2,1,0:T(8,128)S(1)}, u32[]{:S(2)}, u32[]{:S(2)}) %collective-permute-start.21) | collective-permute-done | bytes 163872 | tf_op jit(solution)/shard_map/ppermute | solution.py:392
  175.2 10.5 %all_to_all.11 = f32[8,16,8,128]{3,2,1,0:T(8,128)S(1)} all-to-all(f32[8,16,8,128]{3,2,1,0:T(8,128)S(1)} %shard_map.62), channel_id=1, replica_groups={{0,4,8,12,16,20,24,28},{32,36,40,44,48,52,56,60},{64,68,72,76,80,84,88,..., dimensions={0} | all-to-all | bytes 1048576 | tf_op jit(solution)/shard_map/all_to_all | solution.py:503
  185.7 3.4 %collective-permute-start.24 = (f32[1,128,8,128]{3,2,1,0:T(8,128)S(1)}, f32[1,128,8,128]{3,2,1,0:T(8,128)}, u32[]{:S(2)}, u32[]{:S(2)}) collective-permute-start(f32[1,128,8,128]{3,2,1,0:T(8,128)S(1)} %bitcast.11), channel_id=1, source_target_pairs={{0,4},{4,8},{8,12},{12,16},{16,20},{20,24},{24,28},{28,32},{32,36}... | collective-permute-start | bytes 1572872 | tf_op jit(solution)/shard_map/ppermute | solution.py:387
  189.1 4.0 %collective-permute-start.22 = (f32[1,1,8,128]{3,2,1,0:T(8,128)S(1)}, f32[1,1,8,128]{3,2,1,0:T(8,128)S(1)}, u32[]{:S(2)}, u32[]{:S(2)}) collective-permute-start(f32[1,1,8,128]{3,2,1,0:T(8,128)S(1)} %get-tuple-element.97), channel_id=1, source_target_pairs={{0,1},{1,0},{2,3},{3,2},{4,5},{5,4},{6,7},{7,6},{8,9},{9,8},{10,11... | collective-permute-start | bytes 12296 | tf_op jit(solution)/shard_map/ppermute | solution.py:408
  193.2 9.5 %collective-permute-start.23 = (f32[1,1,8,128]{3,2,1,0:T(8,128)S(1)}, f32[1,1,8,128]{3,2,1,0:T(8,128)S(1)}, u32[]{:S(2)}, u32[]{:S(2)}) collective-permute-start(f32[1,1,8,128]{3,2,1,0:T(8,128)S(1)} %get-tuple-element.96), channel_id=1, source_target_pairs={{1,2},{2,1},{5,6},{6,5},{9,10},{10,9},{13,14},{14,13},{17,18},{18,... | collective-permute-start | bytes 12296 | tf_op jit(solution)/shard_map/ppermute | solution.py:409
  202.7 4.8 %collective-permute-done.23.e_b = f32[1,1,8,128]{3,2,1,0:T(8,128)S(1)} collective-permute-done((f32[1,1,8,128]{3,2,1,0:T(8,128)S(1)}, f32[1,1,8,128]{3,2,1,0:T(8,128)S(1)}, u32[]{:S(2)}, u32[]{:S(2)}) %collective-permute-start.23) | collective-permute-done | bytes 4128 | tf_op jit(solution)/shard_map/ppermute | solution.py:409
  215.7 10.5 %collective-permute-done.26.y1_b = f32[1,1,8,128]{3,2,1,0:T(8,128)S(1)} collective-permute-done((f32[1,1,8,128]{3,2,1,0:T(8,128)S(1)}, f32[1,1,8,128]{3,2,1,0:T(8,128)S(1)}, u32[]{:S(2)}, u32[]{:S(2)}) %collective-permute-start.26) | collective-permute-done | bytes 4128 | tf_op jit(solution)/shard_map/ppermute | solution.py:409
  226.3 3.5 %shard_map.64 = (f32[1,128,8,128]{3,2,1,0:T(8,128)S(1)}, f32[1,128,8,128]{3,2,1,0:T(8,128)S(1)}, f32[2,1,8,128]{3,2,1,0:T(8,128)S(1)}, f32[2,1,8,128]{3,2,1,0:T(8,128)S(1)}) custom-call(s32[1]{0:T(128)} %bitcast.flag, f32[4,128,8,128]{3,2,1,0:T(8,128)S(1)} %get-tuple-element.49.fixed, f32[2,128,8,128]{3,2,1,0:T(8,128)S(1)} %get-tuple-element.81.x, ...), custom_call_target="tpu_custom_call" | custom-call | tf_op jit(solution)/shard_map/pallas_call | solution.py:31
  231.9 3.8 %collective-permute-start.28 = (f32[2,1,8,128]{3,2,1,0:T(8,128)S(1)}, f32[2,1,8,128]{3,2,1,0:T(8,128)S(1)}, u32[]{:S(2)}, u32[]{:S(2)}) collective-permute-start(f32[2,1,8,128]{3,2,1,0:T(8,128)S(1)} %get-tuple-element.89), channel_id=1, source_target_pairs={{1,2},{2,1},{5,6},{6,5},{9,10},{10,9},{13,14},{14,13},{17,18},{18,... | collective-permute-start | bytes 24584 | tf_op jit(solution)/shard_map/ppermute | solution.py:409
  235.7 4.9 %collective-permute-done.28.y_b.e1b = f32[2,1,8,128]{3,2,1,0:T(8,128)S(1)} collective-permute-done((f32[2,1,8,128]{3,2,1,0:T(8,128)S(1)}, f32[2,1,8,128]{3,2,1,0:T(8,128)S(1)}, u32[]{:S(2)}, u32[]{:S(2)}) %collective-permute-start.28) | collective-permute-done | bytes 8224 | tf_op jit(solution)/shard_map/ppermute | solution.py:409
  241.9 3.2 %collective-permute-start.31 = (f32[1,1,8,128]{3,2,1,0:T(8,128)S(1)}, f32[1,1,8,128]{3,2,1,0:T(8,128)S(1)}, u32[]{:S(2)}, u32[]{:S(2)}) collective-permute-start(f32[1,1,8,128]{3,2,1,0:T(8,128)S(1)} %get-tuple-element.93), channel_id=1, source_target_pairs={{1,2},{2,1},{5,6},{6,5},{9,10},{10,9},{13,14},{14,13},{17,18},{18,... | collective-permute-start | bytes 12296 | tf_op jit(solution)/shard_map/ppermute | solution.py:409
  248.4 4.5 %shard_map.66 = (f32[2,1024,128]{2,1,0:T(8,128)}, f32[2,1024,128]{2,1,0:T(8,128)}) custom-call(s32[1]{0:T(128)} %bitcast.flag, f32[4,128,8,128]{3,2,1,0:T(8,128)S(1)} %get-tuple-element.49.fixed, f32[1,128,8,128]{3,2,1,0:T(8,128)S(1)} %get-tuple-element.90.z0, f32[1,128,8,128]{3,2,1,0:T(8,128)S(1)} %get-tuple-element.91.z1, ...), custom_call_target="tpu_custom_call" | custom-call | tf_op jit(solution)/shard_map/pallas_call | solution.py:31
  (81 shorter events, 64.1 us)
Async XLA Ops:
  2.6 29.8 %collective-permute-start.2 = (f32[1,1024,128]{2,1,0:T(8,128)}, f32[1,1024,128]{2,1,0:T(8,128)}, u32[]{:S(2)}, u32[]{:S(2)}) collective-permute-start(f32[1,1024,128]{2,1,0:T(8,128)} %bitcast.4), channel_id=1, source_target_pairs={{0,4},{4,8},{8,12},{12,16},{16,20},{20,24},{24,28},{28,32},{32,36}... | collective-permute-start | bytes 1572872 | tf_op jit(solution)/shard_map/ppermute | solution.py:387
  9.8 5.5 %collective-permute-start = (f32[2,1,8,128]{3,2,1,0:T(8,128)S(1)}, f32[2,1,8,128]{3,2,1,0:T(8,128)S(1)}, u32[]{:S(2)}, u32[]{:S(2)}) collective-permute-start(f32[2,1,8,128]{3,2,1,0:T(8,128)S(1)} %get-tuple-element.51), channel_id=1, source_target_pairs={{0,1},{1,0},{2,3},{3,2},{4,5},{5,4},{6,7},{7,6},{8,9},{9,8},{10,11... | collective-permute-start | bytes 24584 | tf_op jit(solution)/shard_map/ppermute | solution.py:408
  10.9 11.0 %collective-permute-start.1 = (f32[2,1,8,128]{3,2,1,0:T(8,128)S(1)}, f32[2,1,8,128]{3,2,1,0:T(8,128)S(1)}, u32[]{:S(2)}, u32[]{:S(2)}) collective-permute-start(f32[2,1,8,128]{3,2,1,0:T(8,128)S(1)} %get-tuple-element.52), channel_id=1, source_target_pairs={{1,2},{2,1},{5,6},{6,5},{9,10},{10,9},{13,14},{14,13},{17,18},{18,... | collective-permute-start | bytes 24584 | tf_op jit(solution)/shard_map/ppermute | solution.py:409
  23.1 24.9 %collective-permute-start.7 = (f32[1,128,8,128]{3,2,1,0:T(8,128)S(1)}, f32[1,128,8,128]{3,2,1,0:T(8,128)S(1)}, u32[]{:S(2)}, u32[]{:S(2)}) collective-permute-start(f32[1,128,8,128]{3,2,1,0:T(8,128)S(1)} %get-tuple-element.53.y1), channel_id=1, source_target_pairs={{0,4},{4,8},{8,12},{12,16},{16,20},{20,24},{24,28},{28,32},{32,36}... | collective-permute-start | bytes 1572872 | tf_op jit(solution)/shard_map/ppermute | solution.py:387
  25.1 7.2 %collective-permute-start.4 = (f32[1,1,8,128]{3,2,1,0:T(8,128)S(1)}, f32[1,1,8,128]{3,2,1,0:T(8,128)S(1)}, u32[]{:S(2)}, u32[]{:S(2)}) collective-permute-start(f32[1,1,8,128]{3,2,1,0:T(8,128)S(1)} %get-tuple-element.55), channel_id=1, source_target_pairs={{1,2},{2,1},{5,6},{6,5},{9,10},{10,9},{13,14},{14,13},{17,18},{18,... | collective-permute-start | bytes 12296 | tf_op jit(solution)/shard_map/ppermute | solution.py:409
  36.1 19.7 %collective-permute-start.10 = (f32[1,128,8,128]{3,2,1,0:T(8,128)S(1)}, f32[1,128,8,128]{3,2,1,0:T(8,128)S(1)}, u32[]{:S(2)}, u32[]{:S(2)}) collective-permute-start(f32[1,128,8,128]{3,2,1,0:T(8,128)S(1)} %get-tuple-element.60.z1), channel_id=1, source_target_pairs={{0,4},{4,8},{8,12},{12,16},{16,20},{20,24},{24,28},{28,32},{32,36}... | collective-permute-start | bytes 1572872 | tf_op jit(solution)/shard_map/ppermute | solution.py:387
  39.8 3.3 %collective-permute-start.5 = (f32[2,1,8,128]{3,2,1,0:T(8,128)S(1)}, f32[2,1,8,128]{3,2,1,0:T(8,128)S(1)}, u32[]{:S(2)}, u32[]{:S(2)}) collective-permute-start(f32[2,1,8,128]{3,2,1,0:T(8,128)S(1)} %get-tuple-element.57), channel_id=1, source_target_pairs={{0,1},{1,0},{2,3},{3,2},{4,5},{5,4},{6,7},{7,6},{8,9},{9,8},{10,11... | collective-permute-start | bytes 24584 | tf_op jit(solution)/shard_map/ppermute | solution.py:408
  39.9 8.1 %collective-permute-start.6 = (f32[2,1,8,128]{3,2,1,0:T(8,128)S(1)}, f32[2,1,8,128]{3,2,1,0:T(8,128)S(1)}, u32[]{:S(2)}, u32[]{:S(2)}) collective-permute-start(f32[2,1,8,128]{3,2,1,0:T(8,128)S(1)} %get-tuple-element.58), channel_id=1, source_target_pairs={{1,2},{2,1},{5,6},{6,5},{9,10},{10,9},{13,14},{14,13},{17,18},{18,... | collective-permute-start | bytes 24584 | tf_op jit(solution)/shard_map/ppermute | solution.py:409
  49.3 4.9 %collective-permute-start.8 = (f32[1,1,8,128]{3,2,1,0:T(8,128)S(1)}, f32[1,1,8,128]{3,2,1,0:T(8,128)S(1)}, u32[]{:S(2)}, u32[]{:S(2)}) collective-permute-start(f32[1,1,8,128]{3,2,1,0:T(8,128)S(1)} %get-tuple-element.61), channel_id=1, source_target_pairs={{0,1},{1,0},{2,3},{3,2},{4,5},{5,4},{6,7},{7,6},{8,9},{9,8},{10,11... | collective-permute-start | bytes 12296 | tf_op jit(solution)/shard_map/ppermute | solution.py:408
  49.4 6.4 %collective-permute-start.9 = (f32[1,1,8,128]{3,2,1,0:T(8,128)S(1)}, f32[1,1,8,128]{3,2,1,0:T(8,128)S(1)}, u32[]{:S(2)}, u32[]{:S(2)}) collective-permute-start(f32[1,1,8,128]{3,2,1,0:T(8,128)S(1)} %get-tuple-element.62), channel_id=1, source_target_pairs={{1,2},{2,1},{5,6},{6,5},{9,10},{10,9},{13,14},{14,13},{17,18},{18,... | collective-permute-start | bytes 12296 | tf_op jit(solution)/shard_map/ppermute | solution.py:409
  59.2 4.9 %collective-permute-start.11 = (f32[2,15,8,128]{3,2,1,0:T(8,128)S(1)}, f32[2,15,8,128]{3,2,1,0:T(8,128)S(1)}, u32[]{:S(2)}, u32[]{:S(2)}) collective-permute-start(f32[2,15,8,128]{3,2,1,0:T(8,128)S(1)} %get-tuple-element.64), channel_id=1, source_target_pairs={{0,1},{1,0},{2,3},{3,2},{4,5},{5,4},{6,7},{7,6},{8,9},{9,8},{10,11... | collective-permute-start | bytes 368648 | tf_op jit(solution)/shard_map/ppermute | solution.py:408
  59.2 7.7 %collective-permute-start.12 = (f32[2,15,8,128]{3,2,1,0:T(8,128)S(1)}, f32[2,15,8,128]{3,2,1,0:T(8,128)S(1)}, u32[]{:S(2)}, u32[]{:S(2)}) collective-permute-start(f32[2,15,8,128]{3,2,1,0:T(8,128)S(1)} %get-tuple-element.65), channel_id=1, source_target_pairs={{1,2},{2,1},{5,6},{6,5},{9,10},{10,9},{13,14},{14,13},{17,18},{18,... | collective-permute-start | bytes 368648 | tf_op jit(solution)/shard_map/ppermute | solution.py:409
  88.9 10.6 %collective-permute-start.13 = (f32[2,46,8,128]{3,2,1,0:T(8,128)}, f32[2,46,8,128]{3,2,1,0:T(8,128)S(1)}, u32[]{:S(2)}, u32[]{:S(2)}) collective-permute-start(f32[2,46,8,128]{3,2,1,0:T(8,128)} %slice.12), channel_id=1, source_target_pairs={{0,32},{4,36},{8,40},{12,44},{16,48},{20,52},{24,56},{28,60},{32,6... | collective-permute-start | bytes 1130504 | tf_op jit(solution)/shard_map/ppermute | solution.py:392
  107.4 7.5 %collective-permute-start.14 = (f32[2,42,8,128]{3,2,1,0:T(8,128)S(1)}, f32[2,42,8,128]{3,2,1,0:T(8,128)S(1)}, u32[]{:S(2)}, u32[]{:S(2)}) collective-permute-start(f32[2,42,8,128]{3,2,1,0:T(8,128)S(1)} %get-tuple-element.69), channel_id=1, source_target_pairs={{0,32},{4,36},{8,40},{12,44},{16,48},{20,52},{24,56},{28,60},{32,6... | collective-permute-start | bytes 1032200 | tf_op jit(solution)/shard_map/ppermute | solution.py:392
  118.2 7.9 %collective-permute-start.15 = (f32[2,38,8,128]{3,2,1,0:T(8,128)S(1)}, f32[2,38,8,128]{3,2,1,0:T(8,128)S(1)}, u32[]{:S(2)}, u32[]{:S(2)}) collective-permute-start(f32[2,38,8,128]{3,2,1,0:T(8,128)S(1)} %get-tuple-element.72.refs_1_.g_own), channel_id=1, source_target_pairs={{0,32},{4,36},{8,40},{12,44},{16,48},{20,52},{24,56},{28,60},{32,6... | collective-permute-start | bytes 933896 | tf_op jit(solution)/shard_map/ppermute | solution.py:392
  127.8 10.8 %collective-permute-start.16 = (f32[1,34,8,128]{3,2,1,0:T(8,128)S(1)}, f32[1,34,8,128]{3,2,1,0:T(8,128)S(1)}, u32[]{:S(2)}, u32[]{:S(2)}) collective-permute-start(f32[1,34,8,128]{3,2,1,0:T(8,128)S(1)} %get-tuple-element.74.refs_3_), channel_id=1, source_target_pairs={{0,96},{4,100},{8,104},{12,108},{16,112},{20,116},{24,120},{28,124... | collective-permute-start | bytes 417800 | tf_op jit(solution)/shard_map/ppermute | solution.py:392
  129.6 15.2 %collective-permute-start.17 = (f32[1,34,8,128]{3,2,1,0:T(8,128)S(1)}, f32[1,34,8,128]{3,2,1,0:T(8,128)S(1)}, u32[]{:S(2)}, u32[]{:S(2)}) collective-permute-start(f32[1,34,8,128]{3,2,1,0:T(8,128)S(1)} %get-tuple-element.74.refs_3_), channel_id=1, source_target_pairs={{0,64},{4,68},{8,72},{12,76},{16,80},{20,84},{24,88},{28,92},{32,9... | collective-permute-start | bytes 417800 | tf_op jit(solution)/shard_map/ppermute | solution.py:392
  131.0 15.1 %collective-permute-start.18 = (f32[1,34,8,128]{3,2,1,0:T(8,128)S(1)}, f32[1,34,8,128]{3,2,1,0:T(8,128)S(1)}, u32[]{:S(2)}, u32[]{:S(2)}) collective-permute-start(f32[1,34,8,128]{3,2,1,0:T(8,128)S(1)} %get-tuple-element.74.refs_3_), channel_id=1, source_target_pairs={{0,32},{4,36},{8,40},{12,44},{16,48},{20,52},{24,56},{28,60},{32,6... | collective-permute-start | bytes 417800 | tf_op jit(solution)/shard_map/ppermute | solution.py:392
  148.0 8.8 %collective-permute-start.19 = (f32[2,28,8,128]{3,2,1,0:T(8,128)S(1)}, f32[2,28,8,128]{3,2,1,0:T(8,128)S(1)}, u32[]{:S(2)}, u32[]{:S(2)}) collective-permute-start(f32[2,28,8,128]{3,2,1,0:T(8,128)S(1)} %get-tuple-element.75), channel_id=1, source_target_pairs={{0,32},{4,36},{8,40},{12,44},{16,48},{20,52},{24,56},{28,60},{32,6... | collective-permute-start | bytes 688136 | tf_op jit(solution)/shard_map/ppermute | solution.py:392
  157.9 7.2 %collective-permute-start.20 = (f32[2,24,8,128]{3,2,1,0:T(8,128)S(1)}, f32[2,24,8,128]{3,2,1,0:T(8,128)S(1)}, u32[]{:S(2)}, u32[]{:S(2)}) collective-permute-start(f32[2,24,8,128]{3,2,1,0:T(8,128)S(1)} %get-tuple-element.77), channel_id=1, source_target_pairs={{0,32},{4,36},{8,40},{12,44},{16,48},{20,52},{24,56},{28,60},{32,6... | collective-permute-start | bytes 589832 | tf_op jit(solution)/shard_map/ppermute | solution.py:392
  167.0 5.5 %collective-permute-start.21 = (f32[2,20,8,128]{3,2,1,0:T(8,128)S(1)}, f32[2,20,8,128]{3,2,1,0:T(8,128)S(1)}, u32[]{:S(2)}, u32[]{:S(2)}) collective-permute-start(f32[2,20,8,128]{3,2,1,0:T(8,128)S(1)} %get-tuple-element.79), channel_id=1, source_target_pairs={{0,32},{4,36},{8,40},{12,44},{16,48},{20,52},{24,56},{28,60},{32,6... | collective-permute-start | bytes 491528 | tf_op jit(solution)/shard_map/ppermute | solution.py:392
  185.7 40.6 %collective-permute-start.24 = (f32[1,128,8,128]{3,2,1,0:T(8,128)S(1)}, f32[1,128,8,128]{3,2,1,0:T(8,128)}, u32[]{:S(2)}, u32[]{:S(2)}) collective-permute-start(f32[1,128,8,128]{3,2,1,0:T(8,128)S(1)} %bitcast.11), channel_id=1, source_target_pairs={{0,4},{4,8},{8,12},{12,16},{16,20},{20,24},{24,28},{28,32},{32,36}... | collective-permute-start | bytes 1572872 | tf_op jit(solution)/shard_map/ppermute | solution.py:387
  189.1 13.6 %collective-permute-start.22 = (f32[1,1,8,128]{3,2,1,0:T(8,128)S(1)}, f32[1,1,8,128]{3,2,1,0:T(8,128)S(1)}, u32[]{:S(2)}, u32[]{:S(2)}) collective-permute-start(f32[1,1,8,128]{3,2,1,0:T(8,128)S(1)} %get-tuple-element.97), channel_id=1, source_target_pairs={{0,1},{1,0},{2,3},{3,2},{4,5},{5,4},{6,7},{7,6},{8,9},{9,8},{10,11... | collective-permute-start | bytes 12296 | tf_op jit(solution)/shard_map/ppermute | solution.py:408
  193.2 14.4 %collective-permute-start.23 = (f32[1,1,8,128]{3,2,1,0:T(8,128)S(1)}, f32[1,1,8,128]{3,2,1,0:T(8,128)S(1)}, u32[]{:S(2)}, u32[]{:S(2)}) collective-permute-start(f32[1,1,8,128]{3,2,1,0:T(8,128)S(1)} %get-tuple-element.96), channel_id=1, source_target_pairs={{1,2},{2,1},{5,6},{6,5},{9,10},{10,9},{13,14},{14,13},{17,18},{18,... | collective-permute-start | bytes 12296 | tf_op jit(solution)/shard_map/ppermute | solution.py:409
  211.0 4.7 %collective-permute-start.25 = (f32[1,1,8,128]{3,2,1,0:T(8,128)S(1)}, f32[1,1,8,128]{3,2,1,0:T(8,128)S(1)}, u32[]{:S(2)}, u32[]{:S(2)}) collective-permute-start(f32[1,1,8,128]{3,2,1,0:T(8,128)S(1)} %get-tuple-element.85), channel_id=1, source_target_pairs={{0,1},{1,0},{2,3},{3,2},{4,5},{5,4},{6,7},{7,6},{8,9},{9,8},{10,11... | collective-permute-start | bytes 12296 | tf_op jit(solution)/shard_map/ppermute | solution.py:408
  211.1 24.6 %collective-permute-start.29 = (f32[1,128,8,128]{3,2,1,0:T(8,128)S(1)}, f32[1,128,8,128]{3,2,1,0:T(8,128)S(1)}, u32[]{:S(2)}, u32[]{:S(2)}) collective-permute-start(f32[1,128,8,128]{3,2,1,0:T(8,128)S(1)} %get-tuple-element.84.y1), channel_id=1, source_target_pairs={{0,4},{4,8},{8,12},{12,16},{16,20},{20,24},{24,28},{28,32},{32,36}... | collective-permute-start | bytes 1572872 | tf_op jit(solution)/shard_map/ppermute | solution.py:387
  213.0 13.2 %collective-permute-start.26 = (f32[1,1,8,128]{3,2,1,0:T(8,128)S(1)}, f32[1,1,8,128]{3,2,1,0:T(8,128)S(1)}, u32[]{:S(2)}, u32[]{:S(2)}) collective-permute-start(f32[1,1,8,128]{3,2,1,0:T(8,128)S(1)} %get-tuple-element.86), channel_id=1, source_target_pairs={{1,2},{2,1},{5,6},{6,5},{9,10},{10,9},{13,14},{14,13},{17,18},{18,... | collective-permute-start | bytes 12296 | tf_op jit(solution)/shard_map/ppermute | solution.py:409
  229.8 18.5 %collective-permute-start.32 = (f32[1,128,8,128]{3,2,1,0:T(8,128)S(1)}, f32[1,128,8,128]{3,2,1,0:T(8,128)S(1)}, u32[]{:S(2)}, u32[]{:S(2)}) collective-permute-start(f32[1,128,8,128]{3,2,1,0:T(8,128)S(1)} %get-tuple-element.91.z1), channel_id=1, source_target_pairs={{0,4},{4,8},{8,12},{12,16},{16,20},{20,24},{24,28},{28,32},{32,36}... | collective-permute-start | bytes 1572872 | tf_op jit(solution)/shard_map/ppermute | solution.py:387
  231.8 4.0 %collective-permute-start.27 = (f32[2,1,8,128]{3,2,1,0:T(8,128)S(1)}, f32[2,1,8,128]{3,2,1,0:T(8,128)S(1)}, u32[]{:S(2)}, u32[]{:S(2)}) collective-permute-start(f32[2,1,8,128]{3,2,1,0:T(8,128)S(1)} %get-tuple-element.88), channel_id=1, source_target_pairs={{0,1},{1,0},{2,3},{3,2},{4,5},{5,4},{6,7},{7,6},{8,9},{9,8},{10,11... | collective-permute-start | bytes 24584 | tf_op jit(solution)/shard_map/ppermute | solution.py:408
  231.9 8.8 %collective-permute-start.28 = (f32[2,1,8,128]{3,2,1,0:T(8,128)S(1)}, f32[2,1,8,128]{3,2,1,0:T(8,128)S(1)}, u32[]{:S(2)}, u32[]{:S(2)}) collective-permute-start(f32[2,1,8,128]{3,2,1,0:T(8,128)S(1)} %get-tuple-element.89), channel_id=1, source_target_pairs={{1,2},{2,1},{5,6},{6,5},{9,10},{10,9},{13,14},{14,13},{17,18},{18,... | collective-permute-start | bytes 24584 | tf_op jit(solution)/shard_map/ppermute | solution.py:409
  241.8 3.3 %collective-permute-start.30 = (f32[1,1,8,128]{3,2,1,0:T(8,128)S(1)}, f32[1,1,8,128]{3,2,1,0:T(8,128)S(1)}, u32[]{:S(2)}, u32[]{:S(2)}) collective-permute-start(f32[1,1,8,128]{3,2,1,0:T(8,128)S(1)} %get-tuple-element.92), channel_id=1, source_target_pairs={{0,1},{1,0},{2,3},{3,2},{4,5},{5,4},{6,7},{7,6},{8,9},{9,8},{10,11... | collective-permute-start | bytes 12296 | tf_op jit(solution)/shard_map/ppermute | solution.py:408
  241.9 6.4 %collective-permute-start.31 = (f32[1,1,8,128]{3,2,1,0:T(8,128)S(1)}, f32[1,1,8,128]{3,2,1,0:T(8,128)S(1)}, u32[]{:S(2)}, u32[]{:S(2)}) collective-permute-start(f32[1,1,8,128]{3,2,1,0:T(8,128)S(1)} %get-tuple-element.93), channel_id=1, source_target_pairs={{1,2},{2,1},{5,6},{6,5},{9,10},{10,9},{13,14},{14,13},{17,18},{18,... | collective-permute-start | bytes 12296 | tf_op jit(solution)/shard_map/ppermute | solution.py:409
  (13 other events, 55.1 us)

commit v3 on v2

--- a/solution.py
+++ b/solution.py
@@ -192,25 +192,26 @@
     odd = flag[0]
 
     def early(z, p, near):
-        out[0:1, z] = 0.5 * left(fixed, 0, z, p, near, prev)
-        out[1:2, z] = fixed[2:3, z]
+        out[:, z] += 0.5 * left(fixed, 0, z, p, near, prev)
 
     def late(z, p, near):
-        out[0:1, z] += 0.5 * left(fixed, 1, z, p, near, z0)
-
+        out[:, z] = 0.5 * left(fixed, 1, z, p, near, z0)
+
+    step_over(odd, z1, 0, e1a, e1b, 1, late)
     step_over(odd, z0, 0, e0a, e0b, 0, early)
-    step_over(odd, z1, 0, e1a, e1b, 1, late)
-    share_edges(odd, out, out_a, out_b)
-
-
-def cut(flag, own, edge_a, edge_b, pieces, d_piece, tall):
+    share_edges(odd, out, out_a.at[0:1], out_b.at[0:1])
+    share_edges(odd, fixed.at[2:3], out_a.at[1:2], out_b.at[1:2])
+
+
+def cut(flag, own, fixed, edge_a, edge_b, pieces, d_piece, tall):
     odd = flag[0]
     end = OWN + HALO
     tall[:, pl.ds(end * (1 - odd), HALO)] = edge_a[...]
     tall[:, pl.ds(end * odd, HALO)] = edge_b[...]
 
     def copy(z):
-        tall[:, moved(z, HALO)] = own[:, z]
+        tall[0:1, moved(z, HALO)] = own[:, z]
+        tall[1:2, moved(z, HALO)] = fixed[2:3, z]
 
     planes(0, OWN, 8, copy)
     for i in range(GROUP):
@@ -243,51 +244,119 @@
     sweep_both(flag, fixed, x, x_a, x_b, total, y1, y1_a, y1_b, y0, z1, out_a, out_b)
 
 
-def finish(flag, fixed, z0, z1, e0a, e0b, e1a, e1b, prev, sol_out, res_out, res):
-    odd = flag[0]
+def finish_late(flag, fixed, z0, z1, e1a, e1b, sol_out, res):
     turn_out(z0.at[0], sol_out.at[0])
     turn_out(z1.at[0], sol_out.at[1])
 
     def late(z, p, near):
-        res[1:2, z] = left(fixed, 1, z, p, near, z0)
+        res[:, z] = left(fixed, 1, z, p, near, z0)
+
+    step_over(flag[0], z1, 0, e1a, e1b, 1, late)
+
+
+def finish_early(flag, fixed, z0, e0a, e0b, prev, late, res_out, res):
+    turn_out(late.at[0], res_out.at[1])
 
     def early(z, p, near):
-        res[0:1, z] = left(fixed, 0, z, p, near, prev)
-
-    step_over(odd, z1, 0, e1a, e1b, 1, late)
-    turn_out(res.at[1], res_out.at[1])
-    step_over(odd, z0, 0, e0a, e0b, 0, early)
+        res[:, z] = left(fixed, 0, z, p, near, prev)
+
+    step_over(flag[0], z0, 0, e0a, e0b, 0, early)
     turn_out(res.at[0], res_out.at[0])
 
 
-def step_down(flag, d_ref, *refs, counts, own, c, low, last, tail_steps):
-    history = refs[: len(counts)]
-    g_own = refs[len(counts)]
-    rest = refs[len(counts) + 1 :]
-    past = sum(counts)
-    total = past + own
+def step_alone(d_ref, g_own, v2, below, tail, s_ref, va, *, c):
+    n = g_own.shape[0]
+    m = masks()
+
+    def gather(z):
+        s = damping / (c + 6.0 * d_ref[z])
+        s_ref[z] = s
+        va[:, z] = s * g_own[:, z]
+
+    planes(0, WIDE, width(n), gather)
+
+    def sweep(z):
+        p, near = spread(va, 1, n, z, m)
+        v2[:, moved(z, -1)] = keep * p + s_ref[z] * (
+            g_own[1:n, z] + c * va[0 : n - 1, z] + d_ref[z] * near
+        )
+
+    planes(1, WIDE - 1, width(n - 1), sweep)
+
+    def left(z):
+        zz = moved(z, -1)
+        p, near = spread(v2, 1, n - 1, zz, m)
+        d = d_ref[z]
+        r = g_own[2:n, z] + c * v2[0 : n - 2, zz] + d * near - (c + 6.0 * d) * p
+        for j in range(n // 2 - 1):
+            value = 0.5 * (r[2 * j] + r[2 * j + 1])
+            below[j, moved(z, -2)] = value
+            if j >= n // 2 - 3:
+                tail[j - n // 2 + 3, moved(z, -2)] = value
+
+    planes(2, WIDE - 2, width(n - 2), left)
+
+
+def step_join(flag, d_ref, history, g_own, v2, first, below, kept, s_ref, g_ref, va, vb, *, c, keep_low):
+    known = jnp.where(flag[0] > 0, 1.0, 0.0).astype(F32)
+    m = masks()
+
+    def gather(z):
+        s = damping / (c + 6.0 * d_ref[z])
+        s_ref[z] = s
+        g = known * history[:, z]
+        g_ref[0:2, z] = g
+        va[0:2, z] = s * g
+        g = g_own[0:1, z]
+        g_ref[2:3, z] = g
+        va[2:3, z] = s * g
+
+    planes(0, WIDE, 8, gather)
+
+    def sweep(z):
+        p, near = spread(va, 1, 3, z, m)
+        value = keep * p + s_ref[z] * (g_ref[1:3, z] + c * va[0:2, z] + d_ref[z] * near)
+        vb[0:2, z] = value
+        vb[2, z] = v2[0, moved(z, -1)]
+        first[:, moved(z, -1)] = value[1:2]
+
+    planes(1, WIDE - 1, 10, sweep)
+
+    def left(z):
+        p, near = spread(vb, 1, 3, z, m)
+        d = d_ref[z]
+        r = g_own[0:2, z] + c * vb[0:2, z] + d * near - (c + 6.0 * d) * p
+        below[0, moved(z, -2)] = 0.5 * (r[0] + r[1])
+
+    planes(2, WIDE - 2, 10, left)
+    kept[0:1] = g_ref[1:2, keep_low : WIDE - keep_low]
+    kept[1:] = g_own[:, keep_low : WIDE - keep_low]
+
+
+def step_down(flag, d_ref, *refs, parts, c, low, last, keep_low):
+    arrays = refs[: len(parts)]
+    rest = refs[len(parts) :]
+    past = sum(n for n, need in parts if need)
+    total = sum(n for n, need in parts)
+    own = total - past
     high = WIDE - low
     q = flag[0]
     if last:
         v_above, e_ref, tail, s_ref, g_ref, va, vb = rest
-    elif tail_steps:
-        v2, below, tail, s_ref, g_ref, va = rest
     else:
-        v2, below, s_ref, g_ref, va = rest
+        v2, below, kept, s_ref, g_ref, va = rest
 
     def gather(z):
         s = damping / (c + 6.0 * d_ref[z])
         s_ref[z] = s
         at = 0
-        for i, (ref, n) in enumerate(zip(history, counts)):
-            known = jnp.where(q > len(counts) - 1 - i, 1.0, 0.0).astype(F32)
-            g = known * ref[:, moved(z, -low)]
+        for ref, (n, need) in zip(arrays, parts):
+            g = ref[:, moved(z, -low)]
+            if need:
+                g = jnp.where(q >= need, 1.0, 0.0).astype(F32) * g
             g_ref[at : at + n, z] = g
             va[at : at + n, z] = s * g
             at += n
-        g = g_own[:, moved(z, -low)]
-        g_ref[at:, z] = g
-        va[at:, z] = s * g
 
     planes(low, high, width(total), gather)
     m = masks()
@@ -330,50 +399,44 @@
         d = d_ref[z]
         r = g_ref[past:total, z] + c * v2[past - 2 : total - 2, zz] + d * near - (c + 6.0 * d) * p
         for j in range(own // 2):
-            value = 0.5 * (r[2 * j] + r[2 * j + 1])
-            below[j, moved(z, -low - 2)] = value
-            if tail_steps and j >= own // 2 - tail_steps:
-                tail[j - own // 2 + tail_steps, moved(z, -low - 2)] = value
+            below[j, moved(z, -low - 2)] = 0.5 * (r[2 * j] + r[2 * j + 1])
 
     planes(low + 2, high - 2, width(own), left)
-
-
-def step_up(flag, d_ref, v2, g_last, g_own, v_last, e_own, *rest, own, c, low, e_low, top):
+    kept[...] = g_ref[past - 1 :, keep_low : WIDE - keep_low]
+
+
+def step_up(flag, d_ref, kept, v_last, e_own, *refs, firsts, own, c, low, e_low, top):
+    values = refs[: len(firsts)]
     if top:
-        out, s_ref, va, vb = rest
+        out, s_ref, va, vb = refs[len(firsts) :]
     else:
-        v_above, out, tail, s_ref, va, vb = rest
-    q = flag[0]
-    known = jnp.where(q > 0, 1.0, 0.0).astype(F32)
+        v_above, out, tail, s_ref, va, vb = refs[len(firsts) :]
+    known = jnp.where(flag[0] > 0, 1.0, 0.0).astype(F32)
     n = own + 2
-    last = g_last.shape[0] - 1
 
     def correct(z):
         s_ref[z] = damping / (c + 6.0 * d_ref[z])
         zz = moved(z, -low - 1)
         here = moved(z, -e_low)
         va[0:2, z] = known * v_last[:, here]
-        for j in range(own // 2):
-            e = e_own[j, here]
-            va[2 + 2 * j, z] = v2[1 + 2 * j, zz] + e
-            va[3 + 2 * j, z] = v2[2 + 2 * j, zz] + e
+        for step in range(own):
+            ref, first = [(r, f) for r, f in zip(values, firsts) if f <= step][-1]
+            va[2 + step, z] = ref[step - first, zz] + e_own[step // 2, here]
 
     planes(e_low, WIDE - e_low, width(n), correct)
     m = masks()
 
     def sweep1(z):
         p, near = spread(va, 1, n, z, m)
-        g0 = known * g_last[last : last + 1, moved(z, -low)]
-        g = jnp.concatenate([g0, g_own[:, moved(z, -low)]], axis=0)
+        g = kept[:, moved(z, -e_low - 1)]
         vb[:, z] = keep * p + s_ref[z] * (g + c * va[0 : n - 1, z] + d_ref[z] * near)
 
     planes(e_low + 1, WIDE - e_low - 1, width(n - 1), sweep1)
 
     def sweep2(z):
         p, near = spread(vb, 1, n - 1, z, m)
-        value = keep * p + s_ref[z] * (
-            g_own[:, moved(z, -low)] + c * vb[0 : n - 2, z] + d_ref[z] * near
-        )
+        g = kept[1:, moved(z, -e_low - 1)]
+        value = keep * p + s_ref[z] * (g + c * vb[0 : n - 2, z] + d_ref[z] * near)
         here = moved(z, -e_low - 2)
         out[:, here] = value
         if not top:
@@ -435,70 +498,78 @@
     z0, *ends = run(sweep_early, [plane] + edge, (odd, fixed, y0, *late_ends, y1_prev))
     v2 = (z0, z1, *swapped(*ends), *late_ends)
     g1, *ends = run(
-        restrict_left, [(2, OWN) + T] + [(2, HALO) + T] * 2, (odd, fixed, *v2, v2_prev)
+        restrict_left, [plane] + [(2, HALO) + T] * 2, (odd, fixed, *v2, v2_prev)
     )
     pieces, d = call(
         cut,
         [(GROUP, WIDE) + T, (WIDE,) + T],
-        (piece, g1, *swapped(*ends)),
+        (piece, g1, fixed, *swapped(*ends)),
         scratch=[(2, OWN + 2 * HALO) + T],
         n_scalar=1,
     )
     groups = [list(range(a, a + GROUP)) for a in range(0, count, GROUP)]
     g = lax.all_to_all(pieces, "tm", 0, 0, axis_index_groups=groups, tiled=True)
 
-    saved = []
-    own_steps = GROUP
     c = base_coef / 2.0
-    low = 0
-    g_tail = g[-2:]
-    for level in range(1, 4):
-        history = around(g_tail, GROUP)
-        total = own_steps + 2
+    history = around(g[-2:], GROUP)
+    n = GROUP
+    v, g_rest, g_tail = call(
+        functools.partial(step_alone, c=c),
+        [(n - 1, WIDE - 2) + T, (n // 2 - 1, WIDE - 4) + T, (2, WIDE - 4) + T],
+        (d, g),
+        scratch=[(WIDE,) + T, (n, WIDE) + T],
+    )
+    next_history = around(g_tail, GROUP)
+    first, g_first, kept = run(
+        functools.partial(step_join, c=c, keep_low=14),
+        [(1, WIDE - 2) + T, (1, WIDE - 4) + T, (n + 1, WIDE - 28) + T],
+        (q, d, history, g, v),
+        scratch=[(WIDE,) + T] + [(3, WIDE) + T] * 3,
+    )
+    saved = [((first, v), (0, 1), kept, n, c, 0)]
+    parts = [(2, 1), (1, 0), (3, 0)]
+    arrays = [next_history, g_first, g_rest]
+    for level in (2, 3):
+        n, c, low = n // 2, c / 2.0, 2 * level - 2
         wide = WIDE - 2 * low
-        tail_steps = 2 if own_steps > 4 else 0
-        v, g_below, *g_tail = call(
+        keep_low = 16 - 2 * level
+        v, g, kept = run(
             functools.partial(
-                step_down, counts=[2], own=own_steps, c=c, low=low, last=False, tail_steps=tail_steps
+                step_down, parts=parts, c=c, low=low, last=False, keep_low=keep_low
             ),
-            [(total - 1, wide - 2) + T, (own_steps // 2, wide - 4) + T]
-            + [(tail_steps, wide - 4) + T] * (tail_steps > 0),
-            (q, d, history, g),
-            scratch=[(WIDE,) + T, (total, WIDE) + T, (total, WIDE) + T],
-            n_scalar=1,
+            [(n + 1, wide - 2) + T, (n // 2, wide - 4) + T, (n + 1, WIDE - 2 * keep_low) + T],
+            (q, d, *arrays),
+            scratch=[(WIDE,) + T, (n + 2, WIDE) + T, (n + 2, WIDE) + T],
         )
-        g_tail = g_tail[0] if g_tail else g_below
-        saved.append((v, history, g, own_steps, c, low))
-        g = g_below
-        own_steps //= 2
-        c /= 2.0
-        low += 2
-    history = [around(g, i * GROUP) for i in (3, 2, 1)]
+        saved.append(((v,), (-1,), kept, n, c, low))
+        if level == 2:
+            parts = [(2, 1), (2, 0)]
+            arrays = [around(g, GROUP), g]
+    parts = [(1, 3), (1, 2), (1, 1), (1, 0)]
+    arrays = [around(g, i * GROUP) for i in (3, 2, 1)] + [g]
+    low = 6
     wide = WIDE - 2 * low
-    e, tail = call(
-        functools.partial(
-            step_down, counts=[1] * 3, own=1, c=c, low=low, last=True, tail_steps=0
-        ),
+    e, tail = run(
+        functools.partial(step_down, parts=parts, c=c / 2.0, low=low, last=True, keep_low=0),
         [(1, wide - 6) + T, (2, wide - 6) + T],
-        (q, d, *history, g, saved[-1][0]),
+        (q, d, *arrays, saved[-1][0][-1]),
         scratch=[(WIDE,) + T] + [(4, WIDE) + T] * 3,
-        n_scalar=1,
     )
     e_low = low + 3
     while saved:
-        v, g_last, g, own_steps, c, low = saved.pop()
+        values, firsts, kept, n, c, low = saved.pop()
         v_last = around(tail, GROUP)
         top = not saved
         narrow = WIDE - 2 * e_low - 4
-        e = call(
-            functools.partial(step_up, own=own_steps, c=c, low=low, e_low=e_low, top=top),
-            [(own_steps, narrow) + T] + [(2, narrow) + T] * (not top),
-            (q, d, v, g_last, g, v_last, e) + (() if top else (saved[-1][0],)),
-            scratch=[(WIDE,) + T, (own_steps + 2, WIDE) + T, (own_steps + 1, WIDE) + T],
-            n_scalar=1,
+        e, *tail = run(
+            functools.partial(
+                step_up, firsts=firsts, own=n, c=c, low=low, e_low=e_low, top=top
+            ),
+            [(n, narrow) + T] + [(2, narrow) + T] * (not top),
+            (q, d, kept, v_last, e, *values) + (() if top else (saved[-1][0][-1],)),
+            scratch=[(WIDE,) + T, (n + 2, WIDE) + T, (n + 1, WIDE) + T],
         )
-        tail = e[-1]
-        e = e[0]
+        tail = tail[0] if tail else None
         e_low += 2
     e0 = lax.all_to_all(e, "tm", 0, 0, axis_index_groups=groups, tiled=True)
     e0 = e0.reshape((1, OWN) + T)
@@ -522,10 +593,13 @@
     late_ends = swapped(*ends)
     z0, *ends = run(sweep_early, [plane] + edge, (odd, fixed, y0, *late_ends, y1_prev))
     sol, res = run(
-        finish,
-        [(2, SIDE * SIDE, OWN)] * 2,
-        (odd, fixed, z0, z1, *swapped(*ends), *late_ends, prev),
-        scratch=[(2, OWN) + T],
+        finish_late, [(2, SIDE * SIDE, OWN), plane], (odd, fixed, z0, z1, *late_ends)
+    )
+    res = run(
+        finish_early,
+        (2, SIDE * SIDE, OWN),
+        (odd, fixed, z0, *swapped(*ends), prev, res),
+        scratch=[plane],
     )
     return sol.reshape(source.shape), res.reshape(source.shape)
 

time: 254 us -> 243 us (0.957)
  waiting for transfers between devices: 98 us -> 83.9 us
  Pallas kernels: 40.9 us -> 43.9 us
    ppermute x9, waiting for transfers between devices: 53.9 us -> 43.1 us  [around(): lax.ppermute(block, 'tm', [(i, (i + distance) % count) for i in range(cou...]
    ppermute x9, waiting for transfers between devices: 44.1 us -> 40.8 us  [swapped(): lax.ppermute(edge_b, 'gz', pairs)]
    pallas_call x17 -> x19, Pallas kernels: 40.9 us -> 43.9 us  [call(): pl.pallas_call(body, out_shape=[jax.ShapeDtypeStruct(s, F32) for s in sha...]
    unnamed x24 -> x38, local copies, waits for them, and re-layouts: 9.09 us -> 9.75 us
  transfers between devices with their start and end apart: 33 -> 33, of which waited for: 18 -> 17; matrix products, arithmetic and copies ran while one was open for 0% -> 0% of each run, Pallas kernels for 6% -> 10%
where the time goes in v3:
time: 243 us; the launch traced here: 240 us
  waiting for transfers between devices  83.9 us (35%)
  starting transfers between devices  69.9 us (29%)
  Pallas kernels  43.9 us (18%)
  blocking collectives  28.1 us (12%)
  local copies, waits for them, and re-layouts  12.5 us (5%)
    pallas_call x19, Pallas kernels, call(): pl.pallas_call(body, out_shape=[jax.ShapeDtypeStruct(s, F32) for s in sha...  43.9 us
    ppermute x9, waiting for transfers between devices, around(): lax.ppermute(block, 'tm', [(i, (i + distance) % count) for i in range(cou...  43.1 us
    ppermute x9, waiting for transfers between devices, swapped(): lax.ppermute(edge_b, 'gz', pairs)  40.8 us
    ppermute x9, starting transfers between devices, swapped(): lax.ppermute(edge_b, 'gz', pairs)  37.2 us
    all_to_all x1, blocking collectives, body(): g = lax.all_to_all(pieces, 'tm', 0, 0, axis_index_groups=groups, tiled=True)  18 us
    ppermute x6, starting transfers between devices, later(): lax.ppermute(block, 'tm', [(i, i + distance) for i in range(count - dista...  16 us
    ppermute x9, starting transfers between devices, around(): lax.ppermute(block, 'tm', [(i, (i + distance) % count) for i in range(cou...  10.7 us
    all_to_all x1, blocking collectives, body(): e0 = lax.all_to_all(e, 'tm', 0, 0, axis_index_groups=groups, tiled=True)  10.1 us
  transfers between devices with their start and end apart: 33, of which 17 were waited for; matrix products, arithmetic and copies ran while one was open for 0% of the time, Pallas kernels for 10%

profile of v3, /device:TPU:3, one launch (start us, length us, event | category | flops | bytes accessed | tf_op | source)
XLA Modules:
  0.0 239.5 jit_solution(6229333149385645864)
XLA Ops:
  2.6 3.2 %collective-permute-start.2 = (f32[1,1024,128]{2,1,0:T(8,128)}, f32[1,1024,128]{2,1,0:T(8,128)}, u32[]{:S(2)}, u32[]{:S(2)}) collective-permute-start(f32[1,1024,128]{2,1,0:T(8,128)} %bitcast.4), channel_id=1, source_target_pairs={{0,4},{4,8},{8,12},{12,16},{16,20},{20,24},{24,28},{28,32},{32,36}... | collective-permute-start | bytes 1572872 | tf_op jit(solution)/shard_map/ppermute | solution.py:450
  10.9 4.4 %collective-permute-start.1 = (f32[2,1,8,128]{3,2,1,0:T(8,128)S(1)}, f32[2,1,8,128]{3,2,1,0:T(8,128)S(1)}, u32[]{:S(2)}, u32[]{:S(2)}) collective-permute-start(f32[2,1,8,128]{3,2,1,0:T(8,128)S(1)} %get-tuple-element.57), channel_id=1, source_target_pairs={{1,2},{2,1},{5,6},{6,5},{9,10},{10,9},{13,14},{14,13},{17,18},{18,... | collective-permute-start | bytes 24584 | tf_op jit(solution)/shard_map/ppermute | solution.py:472
  15.3 6.6 %collective-permute-done.1.x_b = f32[2,1,8,128]{3,2,1,0:T(8,128)S(1)} collective-permute-done((f32[2,1,8,128]{3,2,1,0:T(8,128)S(1)}, f32[2,1,8,128]{3,2,1,0:T(8,128)S(1)}, u32[]{:S(2)}, u32[]{:S(2)}) %collective-permute-start.1) | collective-permute-done | bytes 8224 | tf_op jit(solution)/shard_map/ppermute | solution.py:472
  27.5 4.9 %collective-permute-done.4.y1_b = f32[1,1,8,128]{3,2,1,0:T(8,128)S(1)} collective-permute-done((f32[1,1,8,128]{3,2,1,0:T(8,128)S(1)}, f32[1,1,8,128]{3,2,1,0:T(8,128)S(1)}, u32[]{:S(2)}, u32[]{:S(2)}) %collective-permute-start.4) | collective-permute-done | bytes 4128 | tf_op jit(solution)/shard_map/ppermute | solution.py:472
  32.4 3.7 %shard_map.52 = (f32[1,128,8,128]{3,2,1,0:T(8,128)S(1)}, f32[1,128,8,128]{3,2,1,0:T(8,128)S(1)}, f32[2,1,8,128]{3,2,1,0:T(8,128)S(1)}, f32[2,1,8,128]{3,2,1,0:T(8,128)S(1)}) custom-call(s32[1]{0:T(128)} %bitcast.flag, f32[4,128,8,128]{3,2,1,0:T(8,128)S(1)} %get-tuple-element.54.fixed, f32[2,128,8,128]{3,2,1,0:T(8,128)S(1)} %get-tuple-element.55.x, ...), custom_call_target="tpu_custom_call" | custom-call | tf_op jit(solution)/shard_map/pallas_call | solution.py:31
  36.1 3.7 %collective-permute-start.10 = (f32[1,128,8,128]{3,2,1,0:T(8,128)S(1)}, f32[1,128,8,128]{3,2,1,0:T(8,128)S(1)}, u32[]{:S(2)}, u32[]{:S(2)}) collective-permute-start(f32[1,128,8,128]{3,2,1,0:T(8,128)S(1)} %get-tuple-element.65.z1), channel_id=1, source_target_pairs={{0,4},{4,8},{8,12},{12,16},{16,20},{20,24},{24,28},{28,32},{32,36}... | collective-permute-start | bytes 1572872 | tf_op jit(solution)/shard_map/ppermute | solution.py:450
  39.9 3.2 %collective-permute-start.6 = (f32[2,1,8,128]{3,2,1,0:T(8,128)S(1)}, f32[2,1,8,128]{3,2,1,0:T(8,128)S(1)}, u32[]{:S(2)}, u32[]{:S(2)}) collective-permute-start(f32[2,1,8,128]{3,2,1,0:T(8,128)S(1)} %get-tuple-element.63), channel_id=1, source_target_pairs={{1,2},{2,1},{5,6},{6,5},{9,10},{10,9},{13,14},{14,13},{17,18},{18,... | collective-permute-start | bytes 24584 | tf_op jit(solution)/shard_map/ppermute | solution.py:472
  43.1 4.9 %collective-permute-done.6.y_b.e1b = f32[2,1,8,128]{3,2,1,0:T(8,128)S(1)} collective-permute-done((f32[2,1,8,128]{3,2,1,0:T(8,128)S(1)}, f32[2,1,8,128]{3,2,1,0:T(8,128)S(1)}, u32[]{:S(2)}, u32[]{:S(2)}) %collective-permute-start.6) | collective-permute-done | bytes 8224 | tf_op jit(solution)/shard_map/ppermute | solution.py:472
  49.4 4.8 %collective-permute-start.9 = (f32[1,1,8,128]{3,2,1,0:T(8,128)S(1)}, f32[1,1,8,128]{3,2,1,0:T(8,128)S(1)}, u32[]{:S(2)}, u32[]{:S(2)}) collective-permute-start(f32[1,1,8,128]{3,2,1,0:T(8,128)S(1)} %get-tuple-element.67), channel_id=1, source_target_pairs={{1,2},{2,1},{5,6},{6,5},{9,10},{10,9},{13,14},{14,13},{17,18},{18,... | collective-permute-start | bytes 12296 | tf_op jit(solution)/shard_map/ppermute | solution.py:472
  58.4 4.8 %collective-permute-start.12 = (f32[2,15,8,128]{3,2,1,0:T(8,128)S(1)}, f32[2,15,8,128]{3,2,1,0:T(8,128)S(1)}, u32[]{:S(2)}, u32[]{:S(2)}) collective-permute-start(f32[2,15,8,128]{3,2,1,0:T(8,128)S(1)} %get-tuple-element.70), channel_id=1, source_target_pairs={{1,2},{2,1},{5,6},{6,5},{9,10},{10,9},{13,14},{14,13},{17,18},{18,... | collective-permute-start | bytes 368648 | tf_op jit(solution)/shard_map/ppermute | solution.py:472
  63.3 2.8 %collective-permute-done.12.edge_b = f32[2,15,8,128]{3,2,1,0:T(8,128)S(1)} collective-permute-done((f32[2,15,8,128]{3,2,1,0:T(8,128)S(1)}, f32[2,15,8,128]{3,2,1,0:T(8,128)S(1)}, u32[]{:S(2)}, u32[]{:S(2)}) %collective-permute-start.12) | collective-permute-done | bytes 122912 | tf_op jit(solution)/shard_map/ppermute | solution.py:472
  66.9 18.0 %all_to_all.10.g_own = f32[8,46,8,128]{3,2,1,0:T(8,128)S(1)} all-to-all(f32[8,46,8,128]{3,2,1,0:T(8,128)S(1)} %get-tuple-element.72), channel_id=1, replica_groups={{0,4,8,12,16,20,24,28},{32,36,40,44,48,52,56,60},{64,68,72,76,80,84,88,..., dimensions={0} | all-to-all | bytes 3014656 | tf_op jit(solution)/shard_map/all_to_all | solution.py:511
  87.3 5.8 %shard_map.56 = (f32[7,44,8,128]{3,2,1,0:T(8,128)S(1)}, f32[3,42,8,128]{3,2,1,0:T(8,128)S(1)}, f32[2,42,8,128]{3,2,1,0:T(8,128)}) custom-call(f32[46,8,128]{2,1,0:T(8,128)S(1)} %get-tuple-element.71.d_ref, f32[8,46,8,128]{3,2,1,0:T(8,128)S(1)} %all_to_all.10.g_own), custom_call_target="tpu_custom_call" | custom-call | tf_op jit(solution)/shard_map/pallas_call | solution.py:31
  99.0 2.9 %shard_map.57 = (f32[1,44,8,128]{3,2,1,0:T(8,128)S(1)}, f32[1,42,8,128]{3,2,1,0:T(8,128)S(1)}, f32[9,18,8,128]{3,2,1,0:T(8,128)S(1)}) custom-call(s32[1]{0:T(128)} %bitcast.5.flag, f32[46,8,128]{2,1,0:T(8,128)S(1)} %get-tuple-element.71.d_ref, f32[2,46,8,128]{3,2,1,0:T(8,128)} %collective-permute-done.13.history, f32[8,46,8,128]{3,2,1,0:T(8,128)S(1)} %copy-done.1, ...), custom_call_target="tpu_custom_call" | custom-call | tf_op jit(solution)/shard_map/pallas_call | solution.py:31
  103.7 4.3 %shard_map.58 = (f32[5,40,8,128]{3,2,1,0:T(8,128)S(1)}, f32[2,38,8,128]{3,2,1,0:T(8,128)S(1)}, f32[5,22,8,128]{3,2,1,0:T(8,128)S(1)}) custom-call(s32[1]{0:T(128)} %bitcast.5.flag, f32[46,8,128]{2,1,0:T(8,128)S(1)} %get-tuple-element.71.d_ref, f32[2,42,8,128]{3,2,1,0:T(8,128)} %collective-permute-done.14.refs_0_, ...), custom_call_target="tpu_custom_call" | custom-call | tf_op jit(solution)/shard_map/pallas_call | solution.py:31
  108.5 7.4 %collective-permute-done.15.refs_0_ = f32[2,38,8,128]{3,2,1,0:T(8,128)S(1)} collective-permute-done((f32[2,38,8,128]{3,2,1,0:T(8,128)S(1)}, f32[2,38,8,128]{3,2,1,0:T(8,128)S(1)}, u32[]{:S(2)}, u32[]{:S(2)}) %collective-permute-start.15) | collective-permute-done | bytes 311328 | tf_op jit(solution)/shard_map/ppermute | solution.py:455
  122.2 8.8 %collective-permute-done.16.refs_0_ = f32[1,34,8,128]{3,2,1,0:T(8,128)S(1)} collective-permute-done((f32[1,34,8,128]{3,2,1,0:T(8,128)S(1)}, f32[1,34,8,128]{3,2,1,0:T(8,128)S(1)}, u32[]{:S(2)}, u32[]{:S(2)}) %collective-permute-start.16) | collective-permute-done | bytes 139296 | tf_op jit(solution)/shard_map/ppermute | solution.py:455
  131.0 4.0 %collective-permute-done.17.refs_1_ = f32[1,34,8,128]{3,2,1,0:T(8,128)S(1)} collective-permute-done((f32[1,34,8,128]{3,2,1,0:T(8,128)S(1)}, f32[1,34,8,128]{3,2,1,0:T(8,128)S(1)}, u32[]{:S(2)}, u32[]{:S(2)}) %collective-permute-start.17) | collective-permute-done | bytes 139296 | tf_op jit(solution)/shard_map/ppermute | solution.py:455
  140.2 6.7 %collective-permute-done.19.v_last = f32[2,28,8,128]{3,2,1,0:T(8,128)S(1)} collective-permute-done((f32[2,28,8,128]{3,2,1,0:T(8,128)S(1)}, f32[2,28,8,128]{3,2,1,0:T(8,128)S(1)}, u32[]{:S(2)}, u32[]{:S(2)}) %collective-permute-start.19) | collective-permute-done | bytes 229408 | tf_op jit(solution)/shard_map/ppermute | solution.py:455
  148.5 6.8 %collective-permute-done.20.v_last = f32[2,24,8,128]{3,2,1,0:T(8,128)S(1)} collective-permute-done((f32[2,24,8,128]{3,2,1,0:T(8,128)S(1)}, f32[2,24,8,128]{3,2,1,0:T(8,128)S(1)}, u32[]{:S(2)}, u32[]{:S(2)}) %collective-permute-start.20) | collective-permute-done | bytes 196640 | tf_op jit(solution)/shard_map/ppermute | solution.py:455
  157.3 5.4 %collective-permute-done.21.v_last = f32[2,20,8,128]{3,2,1,0:T(8,128)S(1)} collective-permute-done((f32[2,20,8,128]{3,2,1,0:T(8,128)S(1)}, f32[2,20,8,128]{3,2,1,0:T(8,128)S(1)}, u32[]{:S(2)}, u32[]{:S(2)}) %collective-permute-start.21) | collective-permute-done | bytes 163872 | tf_op jit(solution)/shard_map/ppermute | solution.py:455
  162.7 2.7 %shard_map.63 = f32[8,16,8,128]{3,2,1,0:T(8,128)S(1)} custom-call(s32[1]{0:T(128)} %bitcast.5.flag, f32[46,8,128]{2,1,0:T(8,128)S(1)} %get-tuple-element.71.d_ref, f32[9,18,8,128]{3,2,1,0:T(8,128)S(1)} %get-tuple-element.74.kept, f32[2,20,8,128]{3,2,1,0:T(8,128)S(1)} %collective-permute-done.21.v_last, f32[4,20,8,128]{3,2,1,0:T(8,128)S(1)} %get-tuple-element.89.e_own, ...), custom_call_target="tpu_custom_call" | custom-call | tf_op jit(solution)/shard_map/pallas_call | solution.py:31
  165.4 10.1 %all_to_all.11 = f32[8,16,8,128]{3,2,1,0:T(8,128)S(1)} all-to-all(f32[8,16,8,128]{3,2,1,0:T(8,128)S(1)} %shard_map.63), channel_id=1, replica_groups={{0,4,8,12,16,20,24,28},{32,36,40,44,48,52,56,60},{64,68,72,76,80,84,88,..., dimensions={0} | all-to-all | bytes 1048576 | tf_op jit(solution)/shard_map/all_to_all | solution.py:574
  175.5 3.4 %collective-permute-start.24 = (f32[1,128,8,128]{3,2,1,0:T(8,128)S(1)}, f32[1,128,8,128]{3,2,1,0:T(8,128)S(1)}, u32[]{:S(2)}, u32[]{:S(2)}) collective-permute-start(f32[1,128,8,128]{3,2,1,0:T(8,128)S(1)} %bitcast.11), channel_id=1, source_target_pairs={{0,4},{4,8},{8,12},{12,16},{16,20},{20,24},{24,28},{28,32},{32,36}... | collective-permute-start | bytes 1572872 | tf_op jit(solution)/shard_map/ppermute | solution.py:450
  178.9 4.2 %collective-permute-start.22 = (f32[1,1,8,128]{3,2,1,0:T(8,128)S(1)}, f32[1,1,8,128]{3,2,1,0:T(8,128)S(1)}, u32[]{:S(2)}, u32[]{:S(2)}) collective-permute-start(f32[1,1,8,128]{3,2,1,0:T(8,128)S(1)} %get-tuple-element.107), channel_id=1, source_target_pairs={{0,1},{1,0},{2,3},{3,2},{4,5},{5,4},{6,7},{7,6},{8,9},{9,8},{10,11... | collective-permute-start | bytes 12296 | tf_op jit(solution)/shard_map/ppermute | solution.py:471
  183.1 6.1 %collective-permute-start.23 = (f32[1,1,8,128]{3,2,1,0:T(8,128)S(1)}, f32[1,1,8,128]{3,2,1,0:T(8,128)S(1)}, u32[]{:S(2)}, u32[]{:S(2)}) collective-permute-start(f32[1,1,8,128]{3,2,1,0:T(8,128)S(1)} %get-tuple-element.106), channel_id=1, source_target_pairs={{1,2},{2,1},{5,6},{6,5},{9,10},{10,9},{13,14},{14,13},{17,18},{18,... | collective-permute-start | bytes 12296 | tf_op jit(solution)/shard_map/ppermute | solution.py:472
  189.2 4.7 %collective-permute-done.23.e_b = f32[1,1,8,128]{3,2,1,0:T(8,128)S(1)} collective-permute-done((f32[1,1,8,128]{3,2,1,0:T(8,128)S(1)}, f32[1,1,8,128]{3,2,1,0:T(8,128)S(1)}, u32[]{:S(2)}, u32[]{:S(2)}) %collective-permute-start.23) | collective-permute-done | bytes 4128 | tf_op jit(solution)/shard_map/ppermute | solution.py:472
  201.4 4.4 %collective-permute-start.26 = (f32[1,1,8,128]{3,2,1,0:T(8,128)S(1)}, f32[1,1,8,128]{3,2,1,0:T(8,128)S(1)}, u32[]{:S(2)}, u32[]{:S(2)}) collective-permute-start(f32[1,1,8,128]{3,2,1,0:T(8,128)S(1)} %get-tuple-element.96), channel_id=1, source_target_pairs={{1,2},{2,1},{5,6},{6,5},{9,10},{10,9},{13,14},{14,13},{17,18},{18,... | collective-permute-start | bytes 12296 | tf_op jit(solution)/shard_map/ppermute | solution.py:472
  205.8 10.5 %collective-permute-done.26.y1_b = f32[1,1,8,128]{3,2,1,0:T(8,128)S(1)} collective-permute-done((f32[1,1,8,128]{3,2,1,0:T(8,128)S(1)}, f32[1,1,8,128]{3,2,1,0:T(8,128)S(1)}, u32[]{:S(2)}, u32[]{:S(2)}) %collective-permute-start.26) | collective-permute-done | bytes 4128 | tf_op jit(solution)/shard_map/ppermute | solution.py:472
  223.1 4.9 %collective-permute-done.28.y_b.e1b = f32[2,1,8,128]{3,2,1,0:T(8,128)S(1)} collective-permute-done((f32[2,1,8,128]{3,2,1,0:T(8,128)S(1)}, f32[2,1,8,128]{3,2,1,0:T(8,128)S(1)}, u32[]{:S(2)}, u32[]{:S(2)}) %collective-permute-start.28) | collective-permute-done | bytes 8224 | tf_op jit(solution)/shard_map/ppermute | solution.py:472
  229.3 4.9 %collective-permute-start.31 = (f32[1,1,8,128]{3,2,1,0:T(8,128)S(1)}, f32[1,1,8,128]{3,2,1,0:T(8,128)S(1)}, u32[]{:S(2)}, u32[]{:S(2)}) collective-permute-start(f32[1,1,8,128]{3,2,1,0:T(8,128)S(1)} %get-tuple-element.104), channel_id=1, source_target_pairs={{1,2},{2,1},{5,6},{6,5},{9,10},{10,9},{13,14},{14,13},{17,18},{18,... | collective-permute-start | bytes 12296 | tf_op jit(solution)/shard_map/ppermute | solution.py:472
  236.8 2.8 %shard_map.68 = f32[2,1024,128]{2,1,0:T(8,128)} custom-call(s32[1]{0:T(128)} %bitcast.flag, f32[4,128,8,128]{3,2,1,0:T(8,128)S(1)} %get-tuple-element.54.fixed, f32[1,128,8,128]{3,2,1,0:T(8,128)S(1)} %get-tuple-element.100.z0, f32[1,1,8,128]{3,2,1,0:T(8,128)S(1)} %collective-permute-done.30.e0a, f32[1,1,8,128]{3,2,1,0:T(8,128)S(1)} %collective-permute-done.31.e0b, ...), custom_call_target="tpu_custom_call" | custom-call | tf_op jit(solution)/shard_map/pallas_call | solution.py:31
  (97 shorter events, 62.6 us)
Async XLA Ops:
  2.6 29.8 %collective-permute-start.2 = (f32[1,1024,128]{2,1,0:T(8,128)}, f32[1,1024,128]{2,1,0:T(8,128)}, u32[]{:S(2)}, u32[]{:S(2)}) collective-permute-start(f32[1,1024,128]{2,1,0:T(8,128)} %bitcast.4), channel_id=1, source_target_pairs={{0,4},{4,8},{8,12},{12,16},{16,20},{20,24},{24,28},{28,32},{32,36}... | collective-permute-start | bytes 1572872 | tf_op jit(solution)/shard_map/ppermute | solution.py:450
  9.8 5.5 %collective-permute-start = (f32[2,1,8,128]{3,2,1,0:T(8,128)S(1)}, f32[2,1,8,128]{3,2,1,0:T(8,128)S(1)}, u32[]{:S(2)}, u32[]{:S(2)}) collective-permute-start(f32[2,1,8,128]{3,2,1,0:T(8,128)S(1)} %get-tuple-element.56), channel_id=1, source_target_pairs={{0,1},{1,0},{2,3},{3,2},{4,5},{5,4},{6,7},{7,6},{8,9},{9,8},{10,11... | collective-permute-start | bytes 24584 | tf_op jit(solution)/shard_map/ppermute | solution.py:471
  10.9 11.0 %collective-permute-start.1 = (f32[2,1,8,128]{3,2,1,0:T(8,128)S(1)}, f32[2,1,8,128]{3,2,1,0:T(8,128)S(1)}, u32[]{:S(2)}, u32[]{:S(2)}) collective-permute-start(f32[2,1,8,128]{3,2,1,0:T(8,128)S(1)} %get-tuple-element.57), channel_id=1, source_target_pairs={{1,2},{2,1},{5,6},{6,5},{9,10},{10,9},{13,14},{14,13},{17,18},{18,... | collective-permute-start | bytes 24584 | tf_op jit(solution)/shard_map/ppermute | solution.py:472
  23.1 24.9 %collective-permute-start.7 = (f32[1,128,8,128]{3,2,1,0:T(8,128)S(1)}, f32[1,128,8,128]{3,2,1,0:T(8,128)S(1)}, u32[]{:S(2)}, u32[]{:S(2)}) collective-permute-start(f32[1,128,8,128]{3,2,1,0:T(8,128)S(1)} %get-tuple-element.58.y1), channel_id=1, source_target_pairs={{0,4},{4,8},{8,12},{12,16},{16,20},{20,24},{24,28},{28,32},{32,36}... | collective-permute-start | bytes 1572872 | tf_op jit(solution)/shard_map/ppermute | solution.py:450
  25.0 2.5 %collective-permute-start.3 = (f32[1,1,8,128]{3,2,1,0:T(8,128)S(1)}, f32[1,1,8,128]{3,2,1,0:T(8,128)S(1)}, u32[]{:S(2)}, u32[]{:S(2)}) collective-permute-start(f32[1,1,8,128]{3,2,1,0:T(8,128)S(1)} %get-tuple-element.59), channel_id=1, source_target_pairs={{0,1},{1,0},{2,3},{3,2},{4,5},{5,4},{6,7},{7,6},{8,9},{9,8},{10,11... | collective-permute-start | bytes 12296 | tf_op jit(solution)/shard_map/ppermute | solution.py:471
  25.1 7.2 %collective-permute-start.4 = (f32[1,1,8,128]{3,2,1,0:T(8,128)S(1)}, f32[1,1,8,128]{3,2,1,0:T(8,128)S(1)}, u32[]{:S(2)}, u32[]{:S(2)}) collective-permute-start(f32[1,1,8,128]{3,2,1,0:T(8,128)S(1)} %get-tuple-element.60), channel_id=1, source_target_pairs={{1,2},{2,1},{5,6},{6,5},{9,10},{10,9},{13,14},{14,13},{17,18},{18,... | collective-permute-start | bytes 12296 | tf_op jit(solution)/shard_map/ppermute | solution.py:472
  36.1 19.7 %collective-permute-start.10 = (f32[1,128,8,128]{3,2,1,0:T(8,128)S(1)}, f32[1,128,8,128]{3,2,1,0:T(8,128)S(1)}, u32[]{:S(2)}, u32[]{:S(2)}) collective-permute-start(f32[1,128,8,128]{3,2,1,0:T(8,128)S(1)} %get-tuple-element.65.z1), channel_id=1, source_target_pairs={{0,4},{4,8},{8,12},{12,16},{16,20},{20,24},{24,28},{28,32},{32,36}... | collective-permute-start | bytes 1572872 | tf_op jit(solution)/shard_map/ppermute | solution.py:450
  39.8 3.3 %collective-permute-start.5 = (f32[2,1,8,128]{3,2,1,0:T(8,128)S(1)}, f32[2,1,8,128]{3,2,1,0:T(8,128)S(1)}, u32[]{:S(2)}, u32[]{:S(2)}) collective-permute-start(f32[2,1,8,128]{3,2,1,0:T(8,128)S(1)} %get-tuple-element.62), channel_id=1, source_target_pairs={{0,1},{1,0},{2,3},{3,2},{4,5},{5,4},{6,7},{7,6},{8,9},{9,8},{10,11... | collective-permute-start | bytes 24584 | tf_op jit(solution)/shard_map/ppermute | solution.py:471
  39.9 8.1 %collective-permute-start.6 = (f32[2,1,8,128]{3,2,1,0:T(8,128)S(1)}, f32[2,1,8,128]{3,2,1,0:T(8,128)S(1)}, u32[]{:S(2)}, u32[]{:S(2)}) collective-permute-start(f32[2,1,8,128]{3,2,1,0:T(8,128)S(1)} %get-tuple-element.63), channel_id=1, source_target_pairs={{1,2},{2,1},{5,6},{6,5},{9,10},{10,9},{13,14},{14,13},{17,18},{18,... | collective-permute-start | bytes 24584 | tf_op jit(solution)/shard_map/ppermute | solution.py:472
  49.3 4.9 %collective-permute-start.8 = (f32[1,1,8,128]{3,2,1,0:T(8,128)S(1)}, f32[1,1,8,128]{3,2,1,0:T(8,128)S(1)}, u32[]{:S(2)}, u32[]{:S(2)}) collective-permute-start(f32[1,1,8,128]{3,2,1,0:T(8,128)S(1)} %get-tuple-element.66), channel_id=1, source_target_pairs={{0,1},{1,0},{2,3},{3,2},{4,5},{5,4},{6,7},{7,6},{8,9},{9,8},{10,11... | collective-permute-start | bytes 12296 | tf_op jit(solution)/shard_map/ppermute | solution.py:471
  49.4 6.4 %collective-permute-start.9 = (f32[1,1,8,128]{3,2,1,0:T(8,128)S(1)}, f32[1,1,8,128]{3,2,1,0:T(8,128)S(1)}, u32[]{:S(2)}, u32[]{:S(2)}) collective-permute-start(f32[1,1,8,128]{3,2,1,0:T(8,128)S(1)} %get-tuple-element.67), channel_id=1, source_target_pairs={{1,2},{2,1},{5,6},{6,5},{9,10},{10,9},{13,14},{14,13},{17,18},{18,... | collective-permute-start | bytes 12296 | tf_op jit(solution)/shard_map/ppermute | solution.py:472
  58.3 5.0 %collective-permute-start.11 = (f32[2,15,8,128]{3,2,1,0:T(8,128)S(1)}, f32[2,15,8,128]{3,2,1,0:T(8,128)S(1)}, u32[]{:S(2)}, u32[]{:S(2)}) collective-permute-start(f32[2,15,8,128]{3,2,1,0:T(8,128)S(1)} %get-tuple-element.69), channel_id=1, source_target_pairs={{0,1},{1,0},{2,3},{3,2},{4,5},{5,4},{6,7},{7,6},{8,9},{9,8},{10,11... | collective-permute-start | bytes 368648 | tf_op jit(solution)/shard_map/ppermute | solution.py:471
  58.4 7.7 %collective-permute-start.12 = (f32[2,15,8,128]{3,2,1,0:T(8,128)S(1)}, f32[2,15,8,128]{3,2,1,0:T(8,128)S(1)}, u32[]{:S(2)}, u32[]{:S(2)}) collective-permute-start(f32[2,15,8,128]{3,2,1,0:T(8,128)S(1)} %get-tuple-element.70), channel_id=1, source_target_pairs={{1,2},{2,1},{5,6},{6,5},{9,10},{10,9},{13,14},{14,13},{17,18},{18,... | collective-permute-start | bytes 368648 | tf_op jit(solution)/shard_map/ppermute | solution.py:472
  85.7 12.0 %collective-permute-start.13 = (f32[2,46,8,128]{3,2,1,0:T(8,128)}, f32[2,46,8,128]{3,2,1,0:T(8,128)}, u32[]{:S(2)}, u32[]{:S(2)}) collective-permute-start(f32[2,46,8,128]{3,2,1,0:T(8,128)} %slice.12), channel_id=1, source_target_pairs={{0,32},{4,36},{8,40},{12,44},{16,48},{20,52},{24,56},{28,60},{32,6... | collective-permute-start | bytes 1130504 | tf_op jit(solution)/shard_map/ppermute | solution.py:455
  95.0 8.7 %collective-permute-start.14 = (f32[2,42,8,128]{3,2,1,0:T(8,128)}, f32[2,42,8,128]{3,2,1,0:T(8,128)}, u32[]{:S(2)}, u32[]{:S(2)}) collective-permute-start(f32[2,42,8,128]{3,2,1,0:T(8,128)} %get-tuple-element.75), channel_id=1, source_target_pairs={{0,32},{4,36},{8,40},{12,44},{16,48},{20,52},{24,56},{28,60},{32,6... | collective-permute-start | bytes 1032200 | tf_op jit(solution)/shard_map/ppermute | solution.py:455
  108.0 7.8 %collective-permute-start.15 = (f32[2,38,8,128]{3,2,1,0:T(8,128)S(1)}, f32[2,38,8,128]{3,2,1,0:T(8,128)S(1)}, u32[]{:S(2)}, u32[]{:S(2)}) collective-permute-start(f32[2,38,8,128]{3,2,1,0:T(8,128)S(1)} %get-tuple-element.79.refs_1_), channel_id=1, source_target_pairs={{0,32},{4,36},{8,40},{12,44},{16,48},{20,52},{24,56},{28,60},{32,6... | collective-permute-start | bytes 933896 | tf_op jit(solution)/shard_map/ppermute | solution.py:455
  117.6 13.4 %collective-permute-start.16 = (f32[1,34,8,128]{3,2,1,0:T(8,128)S(1)}, f32[1,34,8,128]{3,2,1,0:T(8,128)S(1)}, u32[]{:S(2)}, u32[]{:S(2)}) collective-permute-start(f32[1,34,8,128]{3,2,1,0:T(8,128)S(1)} %get-tuple-element.81.refs_3_), channel_id=1, source_target_pairs={{0,96},{4,100},{8,104},{12,108},{16,112},{20,116},{24,120},{28,124... | collective-permute-start | bytes 417800 | tf_op jit(solution)/shard_map/ppermute | solution.py:455
  119.0 15.9 %collective-permute-start.17 = (f32[1,34,8,128]{3,2,1,0:T(8,128)S(1)}, f32[1,34,8,128]{3,2,1,0:T(8,128)S(1)}, u32[]{:S(2)}, u32[]{:S(2)}) collective-permute-start(f32[1,34,8,128]{3,2,1,0:T(8,128)S(1)} %get-tuple-element.81.refs_3_), channel_id=1, source_target_pairs={{0,64},{4,68},{8,72},{12,76},{16,80},{20,84},{24,88},{28,92},{32,9... | collective-permute-start | bytes 417800 | tf_op jit(solution)/shard_map/ppermute | solution.py:455
  120.4 15.9 %collective-permute-start.18 = (f32[1,34,8,128]{3,2,1,0:T(8,128)S(1)}, f32[1,34,8,128]{3,2,1,0:T(8,128)S(1)}, u32[]{:S(2)}, u32[]{:S(2)}) collective-permute-start(f32[1,34,8,128]{3,2,1,0:T(8,128)S(1)} %get-tuple-element.81.refs_3_), channel_id=1, source_target_pairs={{0,32},{4,36},{8,40},{12,44},{16,48},{20,52},{24,56},{28,60},{32,6... | collective-permute-start | bytes 417800 | tf_op jit(solution)/shard_map/ppermute | solution.py:455
  138.2 8.7 %collective-permute-start.19 = (f32[2,28,8,128]{3,2,1,0:T(8,128)S(1)}, f32[2,28,8,128]{3,2,1,0:T(8,128)S(1)}, u32[]{:S(2)}, u32[]{:S(2)}) collective-permute-start(f32[2,28,8,128]{3,2,1,0:T(8,128)S(1)} %get-tuple-element.83), channel_id=1, source_target_pairs={{0,32},{4,36},{8,40},{12,44},{16,48},{20,52},{24,56},{28,60},{32,6... | collective-permute-start | bytes 688136 | tf_op jit(solution)/shard_map/ppermute | solution.py:455
  148.2 7.2 %collective-permute-start.20 = (f32[2,24,8,128]{3,2,1,0:T(8,128)S(1)}, f32[2,24,8,128]{3,2,1,0:T(8,128)S(1)}, u32[]{:S(2)}, u32[]{:S(2)}) collective-permute-start(f32[2,24,8,128]{3,2,1,0:T(8,128)S(1)} %get-tuple-element.86), channel_id=1, source_target_pairs={{0,32},{4,36},{8,40},{12,44},{16,48},{20,52},{24,56},{28,60},{32,6... | collective-permute-start | bytes 589832 | tf_op jit(solution)/shard_map/ppermute | solution.py:455
  157.2 5.5 %collective-permute-start.21 = (f32[2,20,8,128]{3,2,1,0:T(8,128)S(1)}, f32[2,20,8,128]{3,2,1,0:T(8,128)S(1)}, u32[]{:S(2)}, u32[]{:S(2)}) collective-permute-start(f32[2,20,8,128]{3,2,1,0:T(8,128)S(1)} %get-tuple-element.88), channel_id=1, source_target_pairs={{0,32},{4,36},{8,40},{12,44},{16,48},{20,52},{24,56},{28,60},{32,6... | collective-permute-start | bytes 491528 | tf_op jit(solution)/shard_map/ppermute | solution.py:455
  175.5 40.9 %collective-permute-start.24 = (f32[1,128,8,128]{3,2,1,0:T(8,128)S(1)}, f32[1,128,8,128]{3,2,1,0:T(8,128)S(1)}, u32[]{:S(2)}, u32[]{:S(2)}) collective-permute-start(f32[1,128,8,128]{3,2,1,0:T(8,128)S(1)} %bitcast.11), channel_id=1, source_target_pairs={{0,4},{4,8},{8,12},{12,16},{16,20},{20,24},{24,28},{28,32},{32,36}... | collective-permute-start | bytes 1572872 | tf_op jit(solution)/shard_map/ppermute | solution.py:450
  178.9 10.3 %collective-permute-start.22 = (f32[1,1,8,128]{3,2,1,0:T(8,128)S(1)}, f32[1,1,8,128]{3,2,1,0:T(8,128)S(1)}, u32[]{:S(2)}, u32[]{:S(2)}) collective-permute-start(f32[1,1,8,128]{3,2,1,0:T(8,128)S(1)} %get-tuple-element.107), channel_id=1, source_target_pairs={{0,1},{1,0},{2,3},{3,2},{4,5},{5,4},{6,7},{7,6},{8,9},{9,8},{10,11... | collective-permute-start | bytes 12296 | tf_op jit(solution)/shard_map/ppermute | solution.py:471
  183.1 10.8 %collective-permute-start.23 = (f32[1,1,8,128]{3,2,1,0:T(8,128)S(1)}, f32[1,1,8,128]{3,2,1,0:T(8,128)S(1)}, u32[]{:S(2)}, u32[]{:S(2)}) collective-permute-start(f32[1,1,8,128]{3,2,1,0:T(8,128)S(1)} %get-tuple-element.106), channel_id=1, source_target_pairs={{1,2},{2,1},{5,6},{6,5},{9,10},{10,9},{13,14},{14,13},{17,18},{18,... | collective-permute-start | bytes 12296 | tf_op jit(solution)/shard_map/ppermute | solution.py:472
  199.4 6.4 %collective-permute-start.25 = (f32[1,1,8,128]{3,2,1,0:T(8,128)S(1)}, f32[1,1,8,128]{3,2,1,0:T(8,128)S(1)}, u32[]{:S(2)}, u32[]{:S(2)}) collective-permute-start(f32[1,1,8,128]{3,2,1,0:T(8,128)S(1)} %get-tuple-element.95), channel_id=1, source_target_pairs={{0,1},{1,0},{2,3},{3,2},{4,5},{5,4},{6,7},{7,6},{8,9},{9,8},{10,11... | collective-permute-start | bytes 12296 | tf_op jit(solution)/shard_map/ppermute | solution.py:471
  199.5 23.6 %collective-permute-start.29 = (f32[1,128,8,128]{3,2,1,0:T(8,128)S(1)}, f32[1,128,8,128]{3,2,1,0:T(8,128)S(1)}, u32[]{:S(2)}, u32[]{:S(2)}) collective-permute-start(f32[1,128,8,128]{3,2,1,0:T(8,128)S(1)} %get-tuple-element.94.y1), channel_id=1, source_target_pairs={{0,4},{4,8},{8,12},{12,16},{16,20},{20,24},{24,28},{28,32},{32,36}... | collective-permute-start | bytes 1572872 | tf_op jit(solution)/shard_map/ppermute | solution.py:450
  201.4 14.9 %collective-permute-start.26 = (f32[1,1,8,128]{3,2,1,0:T(8,128)S(1)}, f32[1,1,8,128]{3,2,1,0:T(8,128)S(1)}, u32[]{:S(2)}, u32[]{:S(2)}) collective-permute-start(f32[1,1,8,128]{3,2,1,0:T(8,128)S(1)} %get-tuple-element.96), channel_id=1, source_target_pairs={{1,2},{2,1},{5,6},{6,5},{9,10},{10,9},{13,14},{14,13},{17,18},{18,... | collective-permute-start | bytes 12296 | tf_op jit(solution)/shard_map/ppermute | solution.py:472
  218.9 17.9 %collective-permute-start.32 = (f32[1,128,8,128]{3,2,1,0:T(8,128)S(1)}, f32[1,128,8,128]{3,2,1,0:T(8,128)S(1)}, u32[]{:S(2)}, u32[]{:S(2)}) collective-permute-start(f32[1,128,8,128]{3,2,1,0:T(8,128)S(1)} %get-tuple-element.101.z1), channel_id=1, source_target_pairs={{0,4},{4,8},{8,12},{12,16},{16,20},{20,24},{24,28},{28,32},{32,36}... | collective-permute-start | bytes 1572872 | tf_op jit(solution)/shard_map/ppermute | solution.py:450
  220.9 7.1 %collective-permute-start.28 = (f32[2,1,8,128]{3,2,1,0:T(8,128)S(1)}, f32[2,1,8,128]{3,2,1,0:T(8,128)S(1)}, u32[]{:S(2)}, u32[]{:S(2)}) collective-permute-start(f32[2,1,8,128]{3,2,1,0:T(8,128)S(1)} %get-tuple-element.99), channel_id=1, source_target_pairs={{1,2},{2,1},{5,6},{6,5},{9,10},{10,9},{13,14},{14,13},{17,18},{18,... | collective-permute-start | bytes 24584 | tf_op jit(solution)/shard_map/ppermute | solution.py:472
  229.2 7.6 %collective-permute-start.30 = (f32[1,1,8,128]{3,2,1,0:T(8,128)S(1)}, f32[1,1,8,128]{3,2,1,0:T(8,128)S(1)}, u32[]{:S(2)}, u32[]{:S(2)}) collective-permute-start(f32[1,1,8,128]{3,2,1,0:T(8,128)S(1)} %get-tuple-element.103), channel_id=1, source_target_pairs={{0,1},{1,0},{2,3},{3,2},{4,5},{5,4},{6,7},{7,6},{8,9},{9,8},{10,11... | collective-permute-start | bytes 12296 | tf_op jit(solution)/shard_map/ppermute | solution.py:471
  229.3 7.5 %collective-permute-start.31 = (f32[1,1,8,128]{3,2,1,0:T(8,128)S(1)}, f32[1,1,8,128]{3,2,1,0:T(8,128)S(1)}, u32[]{:S(2)}, u32[]{:S(2)}) collective-permute-start(f32[1,1,8,128]{3,2,1,0:T(8,128)S(1)} %get-tuple-element.104), channel_id=1, source_target_pairs={{1,2},{2,1},{5,6},{6,5},{9,10},{10,9},{13,14},{14,13},{17,18},{18,... | collective-permute-start | bytes 12296 | tf_op jit(solution)/shard_map/ppermute | solution.py:472
  (20 other events, 100.5 us)

commit v4 on v3

--- a/solution.py
+++ b/solution.py
@@ -188,7 +188,7 @@
     planes(0, OWN, 8, scale)
 
 
-def restrict_left(flag, fixed, z0, z1, e0a, e0b, e1a, e1b, prev, out, out_a, out_b):
+def restrict_left(flag, fixed, z0, z1, e0a, e0b, e1a, e1b, prev, out, out_a, out_b, held):
     odd = flag[0]
 
     def early(z, p, near):
@@ -201,6 +201,16 @@
     step_over(odd, z0, 0, e0a, e0b, 0, early)
     share_edges(odd, out, out_a.at[0:1], out_b.at[0:1])
     share_edges(odd, fixed.at[2:3], out_a.at[1:2], out_b.at[1:2])
+    held[0:1, 0:1] = e0a[...]
+    held[1:2, 0:1] = e1a[1:2]
+    held[0:1, OWN + 1 :] = e0b[...]
+    held[1:2, OWN + 1 :] = e1b[1:2]
+
+    def hold(z):
+        held[0:1, moved(z, 1)] = z0[:, z]
+        held[1:2, moved(z, 1)] = z1[:, z]
+
+    planes(0, OWN, 8, hold)
 
 
 def cut(flag, own, fixed, edge_a, edge_b, pieces, d_piece, tall):
@@ -219,18 +229,13 @@
     d_piece[...] = tall[1, pl.ds(flag[1], WIDE)]
 
 
-def corrected_late(
-    flag, fixed, z0, z1, e0a, e0b, e1a, e1b, e, e_a, e_b, x, x_a, x_b, y1, out_a, out_b
-):
+def corrected_late(flag, fixed, held, e, e_a, e_b, x, x_a, x_b, y1, out_a, out_b):
     def add(z):
-        x[0:1, z] = z0[:, z] + e[:, z]
-        x[1:2, z] = z1[:, z] + e[:, z]
+        x[:, z] = held[:, moved(z, 1)] + e[:, z]
 
     planes(0, OWN, 8, add)
-    x_a[0:1] = e0a[...] + e_a[...]
-    x_b[0:1] = e0b[...] + e_b[...]
-    x_a[1:2] = e1a[1:2] + e_a[...]
-    x_b[1:2] = e1b[1:2] + e_b[...]
+    x_a[...] = held[:, 0:1] + e_a[...]
+    x_b[...] = held[:, OWN + 1 :] + e_b[...]
     sweep_late(flag, fixed, x, x_a, x_b, y1, out_a, out_b)
 
 
@@ -496,9 +501,10 @@
     v2_prev = later(z1, 1)
     late_ends = swapped(*ends)
     z0, *ends = run(sweep_early, [plane] + edge, (odd, fixed, y0, *late_ends, y1_prev))
-    v2 = (z0, z1, *swapped(*ends), *late_ends)
-    g1, *ends = run(
-        restrict_left, [plane] + [(2, HALO) + T] * 2, (odd, fixed, *v2, v2_prev)
+    g1, *ends, held = run(
+        restrict_left,
+        [plane] + [(2, HALO) + T] * 2 + [(2, OWN + 2) + T],
+        (odd, fixed, z0, z1, *swapped(*ends), *late_ends, v2_prev),
     )
     pieces, d = call(
         cut,
@@ -580,7 +586,7 @@
     *x, y1, out_a, out_b = run(
         corrected_late,
         [(2, OWN) + T] + edges + [plane] + edge,
-        (odd, fixed, *v2, e0, *swapped(e_a, e_b)),
+        (odd, fixed, held, e0, *swapped(e_a, e_b)),
     )
     y1_prev = later(y1, 1)
     y0, z1, *ends = run(

time: 243 us -> 241 us (level)
    unnamed x38 -> x22, local copies, waits for them, and re-layouts: 9.75 us -> 7.81 us
where the time goes in v4:
time: 241 us; the launch traced here: 238 us
  waiting for transfers between devices  84.2 us (35%)
  starting transfers between devices  70.2 us (29%)
  Pallas kernels  44 us (18%)
  blocking collectives  28 us (12%)
  local copies, waits for them, and re-layouts  10.5 us (4%)
    pallas_call x19, Pallas kernels, call(): pl.pallas_call(body, out_shape=[jax.ShapeDtypeStruct(s, F32) for s in sha...  44 us
    ppermute x9, waiting for transfers between devices, around(): lax.ppermute(block, 'tm', [(i, (i + distance) % count) for i in range(cou...  43.3 us
    ppermute x9, waiting for transfers between devices, swapped(): lax.ppermute(edge_b, 'gz', pairs)  40.9 us
    ppermute x9, starting transfers between devices, swapped(): lax.ppermute(edge_b, 'gz', pairs)  37.6 us
    all_to_all x1, blocking collectives, body(): g = lax.all_to_all(pieces, 'tm', 0, 0, axis_index_groups=groups, tiled=True)  18.1 us
    ppermute x6, starting transfers between devices, later(): lax.ppermute(block, 'tm', [(i, i + distance) for i in range(count - dista...  16 us
    ppermute x9, starting transfers between devices, around(): lax.ppermute(block, 'tm', [(i, (i + distance) % count) for i in range(cou...  10.7 us
    all_to_all x1, blocking collectives, body(): e0 = lax.all_to_all(e, 'tm', 0, 0, axis_index_groups=groups, tiled=True)  10 us
  transfers between devices with their start and end apart: 33, of which 17 were waited for; matrix products, arithmetic and copies ran while one was open for 0% of the time, Pallas kernels for 10%

profile of v4, /device:TPU:3, one launch (start us, length us, event | category | flops | bytes accessed | tf_op | source)
XLA Modules:
  0.0 238.1 jit_solution(12831075746945825718)
XLA Ops:
  2.6 3.2 %collective-permute-start.2 = (f32[1,1024,128]{2,1,0:T(8,128)}, f32[1,1024,128]{2,1,0:T(8,128)}, u32[]{:S(2)}, u32[]{:S(2)}) collective-permute-start(f32[1,1024,128]{2,1,0:T(8,128)} %bitcast.4), channel_id=1, source_target_pairs={{0,4},{4,8},{8,12},{12,16},{16,20},{20,24},{24,28},{28,32},{32,36}... | collective-permute-start | bytes 1572872 | tf_op jit(solution)/shard_map/ppermute | solution.py:455
  10.9 4.4 %collective-permute-start.1 = (f32[2,1,8,128]{3,2,1,0:T(8,128)S(1)}, f32[2,1,8,128]{3,2,1,0:T(8,128)S(1)}, u32[]{:S(2)}, u32[]{:S(2)}) collective-permute-start(f32[2,1,8,128]{3,2,1,0:T(8,128)S(1)} %get-tuple-element.58), channel_id=1, source_target_pairs={{1,2},{2,1},{5,6},{6,5},{9,10},{10,9},{13,14},{14,13},{17,18},{18,... | collective-permute-start | bytes 24584 | tf_op jit(solution)/shard_map/ppermute | solution.py:477
  15.3 6.6 %collective-permute-done.1.x_b = f32[2,1,8,128]{3,2,1,0:T(8,128)S(1)} collective-permute-done((f32[2,1,8,128]{3,2,1,0:T(8,128)S(1)}, f32[2,1,8,128]{3,2,1,0:T(8,128)S(1)}, u32[]{:S(2)}, u32[]{:S(2)}) %collective-permute-start.1) | collective-permute-done | bytes 8224 | tf_op jit(solution)/shard_map/ppermute | solution.py:477
  27.5 4.9 %collective-permute-done.4.y1_b = f32[1,1,8,128]{3,2,1,0:T(8,128)S(1)} collective-permute-done((f32[1,1,8,128]{3,2,1,0:T(8,128)S(1)}, f32[1,1,8,128]{3,2,1,0:T(8,128)S(1)}, u32[]{:S(2)}, u32[]{:S(2)}) %collective-permute-start.4) | collective-permute-done | bytes 4128 | tf_op jit(solution)/shard_map/ppermute | solution.py:477
  32.4 3.7 %shard_map.52 = (f32[1,128,8,128]{3,2,1,0:T(8,128)S(1)}, f32[1,128,8,128]{3,2,1,0:T(8,128)S(1)}, f32[2,1,8,128]{3,2,1,0:T(8,128)S(1)}, f32[2,1,8,128]{3,2,1,0:T(8,128)S(1)}) custom-call(s32[1]{0:T(128)} %bitcast.flag, f32[4,128,8,128]{3,2,1,0:T(8,128)S(1)} %get-tuple-element.55.fixed, f32[2,128,8,128]{3,2,1,0:T(8,128)S(1)} %get-tuple-element.56.x, ...), custom_call_target="tpu_custom_call" | custom-call | tf_op jit(solution)/shard_map/pallas_call | solution.py:31
  36.1 3.7 %collective-permute-start.10 = (f32[1,128,8,128]{3,2,1,0:T(8,128)S(1)}, f32[1,128,8,128]{3,2,1,0:T(8,128)S(1)}, u32[]{:S(2)}, u32[]{:S(2)}) collective-permute-start(f32[1,128,8,128]{3,2,1,0:T(8,128)S(1)} %get-tuple-element.66.z1), channel_id=1, source_target_pairs={{0,4},{4,8},{8,12},{12,16},{16,20},{20,24},{24,28},{28,32},{32,36}... | collective-permute-start | bytes 1572872 | tf_op jit(solution)/shard_map/ppermute | solution.py:455
  39.9 3.2 %collective-permute-start.6 = (f32[2,1,8,128]{3,2,1,0:T(8,128)S(1)}, f32[2,1,8,128]{3,2,1,0:T(8,128)S(1)}, u32[]{:S(2)}, u32[]{:S(2)}) collective-permute-start(f32[2,1,8,128]{3,2,1,0:T(8,128)S(1)} %get-tuple-element.64), channel_id=1, source_target_pairs={{1,2},{2,1},{5,6},{6,5},{9,10},{10,9},{13,14},{14,13},{17,18},{18,... | collective-permute-start | bytes 24584 | tf_op jit(solution)/shard_map/ppermute | solution.py:477
  43.1 4.9 %collective-permute-done.6.y_b.e1b = f32[2,1,8,128]{3,2,1,0:T(8,128)S(1)} collective-permute-done((f32[2,1,8,128]{3,2,1,0:T(8,128)S(1)}, f32[2,1,8,128]{3,2,1,0:T(8,128)S(1)}, u32[]{:S(2)}, u32[]{:S(2)}) %collective-permute-start.6) | collective-permute-done | bytes 8224 | tf_op jit(solution)/shard_map/ppermute | solution.py:477
  49.3 4.8 %collective-permute-start.9 = (f32[1,1,8,128]{3,2,1,0:T(8,128)S(1)}, f32[1,1,8,128]{3,2,1,0:T(8,128)S(1)}, u32[]{:S(2)}, u32[]{:S(2)}) collective-permute-start(f32[1,1,8,128]{3,2,1,0:T(8,128)S(1)} %get-tuple-element.68), channel_id=1, source_target_pairs={{1,2},{2,1},{5,6},{6,5},{9,10},{10,9},{13,14},{14,13},{17,18},{18,... | collective-permute-start | bytes 12296 | tf_op jit(solution)/shard_map/ppermute | solution.py:477
  59.3 4.8 %collective-permute-start.12 = (f32[2,15,8,128]{3,2,1,0:T(8,128)S(1)}, f32[2,15,8,128]{3,2,1,0:T(8,128)S(1)}, u32[]{:S(2)}, u32[]{:S(2)}) collective-permute-start(f32[2,15,8,128]{3,2,1,0:T(8,128)S(1)} %get-tuple-element.72), channel_id=1, source_target_pairs={{1,2},{2,1},{5,6},{6,5},{9,10},{10,9},{13,14},{14,13},{17,18},{18,... | collective-permute-start | bytes 368648 | tf_op jit(solution)/shard_map/ppermute | solution.py:477
  64.2 2.8 %collective-permute-done.12.edge_b = f32[2,15,8,128]{3,2,1,0:T(8,128)S(1)} collective-permute-done((f32[2,15,8,128]{3,2,1,0:T(8,128)S(1)}, f32[2,15,8,128]{3,2,1,0:T(8,128)S(1)}, u32[]{:S(2)}, u32[]{:S(2)}) %collective-permute-start.12) | collective-permute-done | bytes 122912 | tf_op jit(solution)/shard_map/ppermute | solution.py:477
  67.8 18.1 %all_to_all.10.g_own = f32[8,46,8,128]{3,2,1,0:T(8,128)S(1)} all-to-all(f32[8,46,8,128]{3,2,1,0:T(8,128)S(1)} %get-tuple-element.74), channel_id=1, replica_groups={{0,4,8,12,16,20,24,28},{32,36,40,44,48,52,56,60},{64,68,72,76,80,84,88,..., dimensions={0} | all-to-all | bytes 3014656 | tf_op jit(solution)/shard_map/all_to_all | solution.py:517
  88.3 5.7 %shard_map.56 = (f32[7,44,8,128]{3,2,1,0:T(8,128)S(1)}, f32[3,42,8,128]{3,2,1,0:T(8,128)S(1)}, f32[2,42,8,128]{3,2,1,0:T(8,128)}) custom-call(f32[46,8,128]{2,1,0:T(8,128)S(1)} %get-tuple-element.73.d_ref, f32[8,46,8,128]{3,2,1,0:T(8,128)S(1)} %all_to_all.10.g_own), custom_call_target="tpu_custom_call" | custom-call | tf_op jit(solution)/shard_map/pallas_call | solution.py:31
  100.0 2.9 %shard_map.57 = (f32[1,44,8,128]{3,2,1,0:T(8,128)S(1)}, f32[1,42,8,128]{3,2,1,0:T(8,128)S(1)}, f32[9,18,8,128]{3,2,1,0:T(8,128)S(1)}) custom-call(s32[1]{0:T(128)} %bitcast.5.flag, f32[46,8,128]{2,1,0:T(8,128)S(1)} %get-tuple-element.73.d_ref, f32[2,46,8,128]{3,2,1,0:T(8,128)} %collective-permute-done.13.history, f32[8,46,8,128]{3,2,1,0:T(8,128)S(1)} %copy-done.1, ...), custom_call_target="tpu_custom_call" | custom-call | tf_op jit(solution)/shard_map/pallas_call | solution.py:31
  104.7 4.3 %shard_map.58 = (f32[5,40,8,128]{3,2,1,0:T(8,128)S(1)}, f32[2,38,8,128]{3,2,1,0:T(8,128)S(1)}, f32[5,22,8,128]{3,2,1,0:T(8,128)S(1)}) custom-call(s32[1]{0:T(128)} %bitcast.5.flag, f32[46,8,128]{2,1,0:T(8,128)S(1)} %get-tuple-element.73.d_ref, f32[2,42,8,128]{3,2,1,0:T(8,128)} %collective-permute-done.14.refs_0_, ...), custom_call_target="tpu_custom_call" | custom-call | tf_op jit(solution)/shard_map/pallas_call | solution.py:31
  109.4 7.4 %collective-permute-done.15.refs_0_ = f32[2,38,8,128]{3,2,1,0:T(8,128)S(1)} collective-permute-done((f32[2,38,8,128]{3,2,1,0:T(8,128)S(1)}, f32[2,38,8,128]{3,2,1,0:T(8,128)S(1)}, u32[]{:S(2)}, u32[]{:S(2)}) %collective-permute-start.15) | collective-permute-done | bytes 311328 | tf_op jit(solution)/shard_map/ppermute | solution.py:460
  123.1 8.9 %collective-permute-done.16.refs_0_ = f32[1,34,8,128]{3,2,1,0:T(8,128)S(1)} collective-permute-done((f32[1,34,8,128]{3,2,1,0:T(8,128)S(1)}, f32[1,34,8,128]{3,2,1,0:T(8,128)S(1)}, u32[]{:S(2)}, u32[]{:S(2)}) %collective-permute-start.16) | collective-permute-done | bytes 139296 | tf_op jit(solution)/shard_map/ppermute | solution.py:460
  132.0 3.9 %collective-permute-done.17.refs_1_ = f32[1,34,8,128]{3,2,1,0:T(8,128)S(1)} collective-permute-done((f32[1,34,8,128]{3,2,1,0:T(8,128)S(1)}, f32[1,34,8,128]{3,2,1,0:T(8,128)S(1)}, u32[]{:S(2)}, u32[]{:S(2)}) %collective-permute-start.17) | collective-permute-done | bytes 139296 | tf_op jit(solution)/shard_map/ppermute | solution.py:460
  141.1 6.8 %collective-permute-done.19.v_last = f32[2,28,8,128]{3,2,1,0:T(8,128)S(1)} collective-permute-done((f32[2,28,8,128]{3,2,1,0:T(8,128)S(1)}, f32[2,28,8,128]{3,2,1,0:T(8,128)S(1)}, u32[]{:S(2)}, u32[]{:S(2)}) %collective-permute-start.19) | collective-permute-done | bytes 229408 | tf_op jit(solution)/shard_map/ppermute | solution.py:460
  149.5 6.8 %collective-permute-done.20.v_last = f32[2,24,8,128]{3,2,1,0:T(8,128)S(1)} collective-permute-done((f32[2,24,8,128]{3,2,1,0:T(8,128)S(1)}, f32[2,24,8,128]{3,2,1,0:T(8,128)S(1)}, u32[]{:S(2)}, u32[]{:S(2)}) %collective-permute-start.20) | collective-permute-done | bytes 196640 | tf_op jit(solution)/shard_map/ppermute | solution.py:460
  158.3 5.4 %collective-permute-done.21.v_last = f32[2,20,8,128]{3,2,1,0:T(8,128)S(1)} collective-permute-done((f32[2,20,8,128]{3,2,1,0:T(8,128)S(1)}, f32[2,20,8,128]{3,2,1,0:T(8,128)S(1)}, u32[]{:S(2)}, u32[]{:S(2)}) %collective-permute-start.21) | collective-permute-done | bytes 163872 | tf_op jit(solution)/shard_map/ppermute | solution.py:460
  163.7 2.7 %shard_map.63 = f32[8,16,8,128]{3,2,1,0:T(8,128)S(1)} custom-call(s32[1]{0:T(128)} %bitcast.5.flag, f32[46,8,128]{2,1,0:T(8,128)S(1)} %get-tuple-element.73.d_ref, f32[9,18,8,128]{3,2,1,0:T(8,128)S(1)} %get-tuple-element.76.kept, f32[2,20,8,128]{3,2,1,0:T(8,128)S(1)} %collective-permute-done.21.v_last, f32[4,20,8,128]{3,2,1,0:T(8,128)S(1)} %get-tuple-element.91.e_own, ...), custom_call_target="tpu_custom_call" | custom-call | tf_op jit(solution)/shard_map/pallas_call | solution.py:31
  166.4 10.0 %all_to_all.11 = f32[8,16,8,128]{3,2,1,0:T(8,128)S(1)} all-to-all(f32[8,16,8,128]{3,2,1,0:T(8,128)S(1)} %shard_map.63), channel_id=1, replica_groups={{0,4,8,12,16,20,24,28},{32,36,40,44,48,52,56,60},{64,68,72,76,80,84,88,..., dimensions={0} | all-to-all | bytes 1048576 | tf_op jit(solution)/shard_map/all_to_all | solution.py:580
  176.4 3.4 %collective-permute-start.24 = (f32[1,128,8,128]{3,2,1,0:T(8,128)S(1)}, f32[1,128,8,128]{3,2,1,0:T(8,128)S(1)}, u32[]{:S(2)}, u32[]{:S(2)}) collective-permute-start(f32[1,128,8,128]{3,2,1,0:T(8,128)S(1)} %bitcast.11), channel_id=1, source_target_pairs={{0,4},{4,8},{8,12},{12,16},{16,20},{20,24},{24,28},{28,32},{32,36}... | collective-permute-start | bytes 1572872 | tf_op jit(solution)/shard_map/ppermute | solution.py:455
  179.8 4.2 %collective-permute-start.22 = (f32[1,1,8,128]{3,2,1,0:T(8,128)S(1)}, f32[1,1,8,128]{3,2,1,0:T(8,128)S(1)}, u32[]{:S(2)}, u32[]{:S(2)}) collective-permute-start(f32[1,1,8,128]{3,2,1,0:T(8,128)S(1)} %get-tuple-element.109), channel_id=1, source_target_pairs={{0,1},{1,0},{2,3},{3,2},{4,5},{5,4},{6,7},{7,6},{8,9},{9,8},{10,11... | collective-permute-start | bytes 12296 | tf_op jit(solution)/shard_map/ppermute | solution.py:476
  184.0 6.4 %collective-permute-start.23 = (f32[1,1,8,128]{3,2,1,0:T(8,128)S(1)}, f32[1,1,8,128]{3,2,1,0:T(8,128)S(1)}, u32[]{:S(2)}, u32[]{:S(2)}) collective-permute-start(f32[1,1,8,128]{3,2,1,0:T(8,128)S(1)} %get-tuple-element.108), channel_id=1, source_target_pairs={{1,2},{2,1},{5,6},{6,5},{9,10},{10,9},{13,14},{14,13},{17,18},{18,... | collective-permute-start | bytes 12296 | tf_op jit(solution)/shard_map/ppermute | solution.py:477
  190.5 4.8 %collective-permute-done.23.e_b = f32[1,1,8,128]{3,2,1,0:T(8,128)S(1)} collective-permute-done((f32[1,1,8,128]{3,2,1,0:T(8,128)S(1)}, f32[1,1,8,128]{3,2,1,0:T(8,128)S(1)}, u32[]{:S(2)}, u32[]{:S(2)}) %collective-permute-start.23) | collective-permute-done | bytes 4128 | tf_op jit(solution)/shard_map/ppermute | solution.py:477
  199.9 4.5 %collective-permute-start.26 = (f32[1,1,8,128]{3,2,1,0:T(8,128)S(1)}, f32[1,1,8,128]{3,2,1,0:T(8,128)S(1)}, u32[]{:S(2)}, u32[]{:S(2)}) collective-permute-start(f32[1,1,8,128]{3,2,1,0:T(8,128)S(1)} %get-tuple-element.98), channel_id=1, source_target_pairs={{1,2},{2,1},{5,6},{6,5},{9,10},{10,9},{13,14},{14,13},{17,18},{18,... | collective-permute-start | bytes 12296 | tf_op jit(solution)/shard_map/ppermute | solution.py:477
  204.4 10.5 %collective-permute-done.26.y1_b = f32[1,1,8,128]{3,2,1,0:T(8,128)S(1)} collective-permute-done((f32[1,1,8,128]{3,2,1,0:T(8,128)S(1)}, f32[1,1,8,128]{3,2,1,0:T(8,128)S(1)}, u32[]{:S(2)}, u32[]{:S(2)}) %collective-permute-start.26) | collective-permute-done | bytes 4128 | tf_op jit(solution)/shard_map/ppermute | solution.py:477
  221.6 4.9 %collective-permute-done.28.y_b.e1b = f32[2,1,8,128]{3,2,1,0:T(8,128)S(1)} collective-permute-done((f32[2,1,8,128]{3,2,1,0:T(8,128)S(1)}, f32[2,1,8,128]{3,2,1,0:T(8,128)S(1)}, u32[]{:S(2)}, u32[]{:S(2)}) %collective-permute-start.28) | collective-permute-done | bytes 8224 | tf_op jit(solution)/shard_map/ppermute | solution.py:477
  227.8 5.0 %collective-permute-start.31 = (f32[1,1,8,128]{3,2,1,0:T(8,128)S(1)}, f32[1,1,8,128]{3,2,1,0:T(8,128)S(1)}, u32[]{:S(2)}, u32[]{:S(2)}) collective-permute-start(f32[1,1,8,128]{3,2,1,0:T(8,128)S(1)} %get-tuple-element.106), channel_id=1, source_target_pairs={{1,2},{2,1},{5,6},{6,5},{9,10},{10,9},{13,14},{14,13},{17,18},{18,... | collective-permute-start | bytes 12296 | tf_op jit(solution)/shard_map/ppermute | solution.py:477
  235.4 2.8 %shard_map.68 = f32[2,1024,128]{2,1,0:T(8,128)} custom-call(s32[1]{0:T(128)} %bitcast.flag, f32[4,128,8,128]{3,2,1,0:T(8,128)S(1)} %get-tuple-element.55.fixed, f32[1,128,8,128]{3,2,1,0:T(8,128)S(1)} %get-tuple-element.102.z0, f32[1,1,8,128]{3,2,1,0:T(8,128)S(1)} %collective-permute-done.30.e0a, f32[1,1,8,128]{3,2,1,0:T(8,128)S(1)} %collective-permute-done.31.e0b, ...), custom_call_target="tpu_custom_call" | custom-call | tf_op jit(solution)/shard_map/pallas_call | solution.py:31
  (81 shorter events, 60.7 us)
Async XLA Ops:
  2.6 29.8 %collective-permute-start.2 = (f32[1,1024,128]{2,1,0:T(8,128)}, f32[1,1024,128]{2,1,0:T(8,128)}, u32[]{:S(2)}, u32[]{:S(2)}) collective-permute-start(f32[1,1024,128]{2,1,0:T(8,128)} %bitcast.4), channel_id=1, source_target_pairs={{0,4},{4,8},{8,12},{12,16},{16,20},{20,24},{24,28},{28,32},{32,36}... | collective-permute-start | bytes 1572872 | tf_op jit(solution)/shard_map/ppermute | solution.py:455
  9.8 5.5 %collective-permute-start = (f32[2,1,8,128]{3,2,1,0:T(8,128)S(1)}, f32[2,1,8,128]{3,2,1,0:T(8,128)S(1)}, u32[]{:S(2)}, u32[]{:S(2)}) collective-permute-start(f32[2,1,8,128]{3,2,1,0:T(8,128)S(1)} %get-tuple-element.57), channel_id=1, source_target_pairs={{0,1},{1,0},{2,3},{3,2},{4,5},{5,4},{6,7},{7,6},{8,9},{9,8},{10,11... | collective-permute-start | bytes 24584 | tf_op jit(solution)/shard_map/ppermute | solution.py:476
  10.9 11.0 %collective-permute-start.1 = (f32[2,1,8,128]{3,2,1,0:T(8,128)S(1)}, f32[2,1,8,128]{3,2,1,0:T(8,128)S(1)}, u32[]{:S(2)}, u32[]{:S(2)}) collective-permute-start(f32[2,1,8,128]{3,2,1,0:T(8,128)S(1)} %get-tuple-element.58), channel_id=1, source_target_pairs={{1,2},{2,1},{5,6},{6,5},{9,10},{10,9},{13,14},{14,13},{17,18},{18,... | collective-permute-start | bytes 24584 | tf_op jit(solution)/shard_map/ppermute | solution.py:477
  23.1 24.9 %collective-permute-start.7 = (f32[1,128,8,128]{3,2,1,0:T(8,128)S(1)}, f32[1,128,8,128]{3,2,1,0:T(8,128)S(1)}, u32[]{:S(2)}, u32[]{:S(2)}) collective-permute-start(f32[1,128,8,128]{3,2,1,0:T(8,128)S(1)} %get-tuple-element.59.y1), channel_id=1, source_target_pairs={{0,4},{4,8},{8,12},{12,16},{16,20},{20,24},{24,28},{28,32},{32,36}... | collective-permute-start | bytes 1572872 | tf_op jit(solution)/shard_map/ppermute | solution.py:455
  25.0 2.5 %collective-permute-start.3 = (f32[1,1,8,128]{3,2,1,0:T(8,128)S(1)}, f32[1,1,8,128]{3,2,1,0:T(8,128)S(1)}, u32[]{:S(2)}, u32[]{:S(2)}) collective-permute-start(f32[1,1,8,128]{3,2,1,0:T(8,128)S(1)} %get-tuple-element.60), channel_id=1, source_target_pairs={{0,1},{1,0},{2,3},{3,2},{4,5},{5,4},{6,7},{7,6},{8,9},{9,8},{10,11... | collective-permute-start | bytes 12296 | tf_op jit(solution)/shard_map/ppermute | solution.py:476
  25.1 7.2 %collective-permute-start.4 = (f32[1,1,8,128]{3,2,1,0:T(8,128)S(1)}, f32[1,1,8,128]{3,2,1,0:T(8,128)S(1)}, u32[]{:S(2)}, u32[]{:S(2)}) collective-permute-start(f32[1,1,8,128]{3,2,1,0:T(8,128)S(1)} %get-tuple-element.61), channel_id=1, source_target_pairs={{1,2},{2,1},{5,6},{6,5},{9,10},{10,9},{13,14},{14,13},{17,18},{18,... | collective-permute-start | bytes 12296 | tf_op jit(solution)/shard_map/ppermute | solution.py:477
  36.1 19.7 %collective-permute-start.10 = (f32[1,128,8,128]{3,2,1,0:T(8,128)S(1)}, f32[1,128,8,128]{3,2,1,0:T(8,128)S(1)}, u32[]{:S(2)}, u32[]{:S(2)}) collective-permute-start(f32[1,128,8,128]{3,2,1,0:T(8,128)S(1)} %get-tuple-element.66.z1), channel_id=1, source_target_pairs={{0,4},{4,8},{8,12},{12,16},{16,20},{20,24},{24,28},{28,32},{32,36}... | collective-permute-start | bytes 1572872 | tf_op jit(solution)/shard_map/ppermute | solution.py:455
  39.8 3.3 %collective-permute-start.5 = (f32[2,1,8,128]{3,2,1,0:T(8,128)S(1)}, f32[2,1,8,128]{3,2,1,0:T(8,128)S(1)}, u32[]{:S(2)}, u32[]{:S(2)}) collective-permute-start(f32[2,1,8,128]{3,2,1,0:T(8,128)S(1)} %get-tuple-element.63), channel_id=1, source_target_pairs={{0,1},{1,0},{2,3},{3,2},{4,5},{5,4},{6,7},{7,6},{8,9},{9,8},{10,11... | collective-permute-start | bytes 24584 | tf_op jit(solution)/shard_map/ppermute | solution.py:476
  39.9 8.1 %collective-permute-start.6 = (f32[2,1,8,128]{3,2,1,0:T(8,128)S(1)}, f32[2,1,8,128]{3,2,1,0:T(8,128)S(1)}, u32[]{:S(2)}, u32[]{:S(2)}) collective-permute-start(f32[2,1,8,128]{3,2,1,0:T(8,128)S(1)} %get-tuple-element.64), channel_id=1, source_target_pairs={{1,2},{2,1},{5,6},{6,5},{9,10},{10,9},{13,14},{14,13},{17,18},{18,... | collective-permute-start | bytes 24584 | tf_op jit(solution)/shard_map/ppermute | solution.py:477
  49.2 4.9 %collective-permute-start.8 = (f32[1,1,8,128]{3,2,1,0:T(8,128)S(1)}, f32[1,1,8,128]{3,2,1,0:T(8,128)S(1)}, u32[]{:S(2)}, u32[]{:S(2)}) collective-permute-start(f32[1,1,8,128]{3,2,1,0:T(8,128)S(1)} %get-tuple-element.67), channel_id=1, source_target_pairs={{0,1},{1,0},{2,3},{3,2},{4,5},{5,4},{6,7},{7,6},{8,9},{9,8},{10,11... | collective-permute-start | bytes 12296 | tf_op jit(solution)/shard_map/ppermute | solution.py:476
  49.3 6.4 %collective-permute-start.9 = (f32[1,1,8,128]{3,2,1,0:T(8,128)S(1)}, f32[1,1,8,128]{3,2,1,0:T(8,128)S(1)}, u32[]{:S(2)}, u32[]{:S(2)}) collective-permute-start(f32[1,1,8,128]{3,2,1,0:T(8,128)S(1)} %get-tuple-element.68), channel_id=1, source_target_pairs={{1,2},{2,1},{5,6},{6,5},{9,10},{10,9},{13,14},{14,13},{17,18},{18,... | collective-permute-start | bytes 12296 | tf_op jit(solution)/shard_map/ppermute | solution.py:477
  59.3 4.9 %collective-permute-start.11 = (f32[2,15,8,128]{3,2,1,0:T(8,128)S(1)}, f32[2,15,8,128]{3,2,1,0:T(8,128)S(1)}, u32[]{:S(2)}, u32[]{:S(2)}) collective-permute-start(f32[2,15,8,128]{3,2,1,0:T(8,128)S(1)} %get-tuple-element.71), channel_id=1, source_target_pairs={{0,1},{1,0},{2,3},{3,2},{4,5},{5,4},{6,7},{7,6},{8,9},{9,8},{10,11... | collective-permute-start | bytes 368648 | tf_op jit(solution)/shard_map/ppermute | solution.py:476
  59.3 7.7 %collective-permute-start.12 = (f32[2,15,8,128]{3,2,1,0:T(8,128)S(1)}, f32[2,15,8,128]{3,2,1,0:T(8,128)S(1)}, u32[]{:S(2)}, u32[]{:S(2)}) collective-permute-start(f32[2,15,8,128]{3,2,1,0:T(8,128)S(1)} %get-tuple-element.72), channel_id=1, source_target_pairs={{1,2},{2,1},{5,6},{6,5},{9,10},{10,9},{13,14},{14,13},{17,18},{18,... | collective-permute-start | bytes 368648 | tf_op jit(solution)/shard_map/ppermute | solution.py:477
  86.6 12.0 %collective-permute-start.13 = (f32[2,46,8,128]{3,2,1,0:T(8,128)}, f32[2,46,8,128]{3,2,1,0:T(8,128)}, u32[]{:S(2)}, u32[]{:S(2)}) collective-permute-start(f32[2,46,8,128]{3,2,1,0:T(8,128)} %slice.12), channel_id=1, source_target_pairs={{0,32},{4,36},{8,40},{12,44},{16,48},{20,52},{24,56},{28,60},{32,6... | collective-permute-start | bytes 1130504 | tf_op jit(solution)/shard_map/ppermute | solution.py:460
  95.9 8.7 %collective-permute-start.14 = (f32[2,42,8,128]{3,2,1,0:T(8,128)}, f32[2,42,8,128]{3,2,1,0:T(8,128)}, u32[]{:S(2)}, u32[]{:S(2)}) collective-permute-start(f32[2,42,8,128]{3,2,1,0:T(8,128)} %get-tuple-element.77), channel_id=1, source_target_pairs={{0,32},{4,36},{8,40},{12,44},{16,48},{20,52},{24,56},{28,60},{32,6... | collective-permute-start | bytes 1032200 | tf_op jit(solution)/shard_map/ppermute | solution.py:460
  109.0 7.8 %collective-permute-start.15 = (f32[2,38,8,128]{3,2,1,0:T(8,128)S(1)}, f32[2,38,8,128]{3,2,1,0:T(8,128)S(1)}, u32[]{:S(2)}, u32[]{:S(2)}) collective-permute-start(f32[2,38,8,128]{3,2,1,0:T(8,128)S(1)} %get-tuple-element.81.refs_1_), channel_id=1, source_target_pairs={{0,32},{4,36},{8,40},{12,44},{16,48},{20,52},{24,56},{28,60},{32,6... | collective-permute-start | bytes 933896 | tf_op jit(solution)/shard_map/ppermute | solution.py:460
  118.5 13.5 %collective-permute-start.16 = (f32[1,34,8,128]{3,2,1,0:T(8,128)S(1)}, f32[1,34,8,128]{3,2,1,0:T(8,128)S(1)}, u32[]{:S(2)}, u32[]{:S(2)}) collective-permute-start(f32[1,34,8,128]{3,2,1,0:T(8,128)S(1)} %get-tuple-element.83.refs_3_), channel_id=1, source_target_pairs={{0,96},{4,100},{8,104},{12,108},{16,112},{20,116},{24,120},{28,124... | collective-permute-start | bytes 417800 | tf_op jit(solution)/shard_map/ppermute | solution.py:460
  120.0 15.9 %collective-permute-start.17 = (f32[1,34,8,128]{3,2,1,0:T(8,128)S(1)}, f32[1,34,8,128]{3,2,1,0:T(8,128)S(1)}, u32[]{:S(2)}, u32[]{:S(2)}) collective-permute-start(f32[1,34,8,128]{3,2,1,0:T(8,128)S(1)} %get-tuple-element.83.refs_3_), channel_id=1, source_target_pairs={{0,64},{4,68},{8,72},{12,76},{16,80},{20,84},{24,88},{28,92},{32,9... | collective-permute-start | bytes 417800 | tf_op jit(solution)/shard_map/ppermute | solution.py:460
  121.3 15.9 %collective-permute-start.18 = (f32[1,34,8,128]{3,2,1,0:T(8,128)S(1)}, f32[1,34,8,128]{3,2,1,0:T(8,128)S(1)}, u32[]{:S(2)}, u32[]{:S(2)}) collective-permute-start(f32[1,34,8,128]{3,2,1,0:T(8,128)S(1)} %get-tuple-element.83.refs_3_), channel_id=1, source_target_pairs={{0,32},{4,36},{8,40},{12,44},{16,48},{20,52},{24,56},{28,60},{32,6... | collective-permute-start | bytes 417800 | tf_op jit(solution)/shard_map/ppermute | solution.py:460
  139.2 8.7 %collective-permute-start.19 = (f32[2,28,8,128]{3,2,1,0:T(8,128)S(1)}, f32[2,28,8,128]{3,2,1,0:T(8,128)S(1)}, u32[]{:S(2)}, u32[]{:S(2)}) collective-permute-start(f32[2,28,8,128]{3,2,1,0:T(8,128)S(1)} %get-tuple-element.85), channel_id=1, source_target_pairs={{0,32},{4,36},{8,40},{12,44},{16,48},{20,52},{24,56},{28,60},{32,6... | collective-permute-start | bytes 688136 | tf_op jit(solution)/shard_map/ppermute | solution.py:460
  149.2 7.2 %collective-permute-start.20 = (f32[2,24,8,128]{3,2,1,0:T(8,128)S(1)}, f32[2,24,8,128]{3,2,1,0:T(8,128)S(1)}, u32[]{:S(2)}, u32[]{:S(2)}) collective-permute-start(f32[2,24,8,128]{3,2,1,0:T(8,128)S(1)} %get-tuple-element.88), channel_id=1, source_target_pairs={{0,32},{4,36},{8,40},{12,44},{16,48},{20,52},{24,56},{28,60},{32,6... | collective-permute-start | bytes 589832 | tf_op jit(solution)/shard_map/ppermute | solution.py:460
  158.2 5.5 %collective-permute-start.21 = (f32[2,20,8,128]{3,2,1,0:T(8,128)S(1)}, f32[2,20,8,128]{3,2,1,0:T(8,128)S(1)}, u32[]{:S(2)}, u32[]{:S(2)}) collective-permute-start(f32[2,20,8,128]{3,2,1,0:T(8,128)S(1)} %get-tuple-element.90), channel_id=1, source_target_pairs={{0,32},{4,36},{8,40},{12,44},{16,48},{20,52},{24,56},{28,60},{32,6... | collective-permute-start | bytes 491528 | tf_op jit(solution)/shard_map/ppermute | solution.py:460
  176.4 38.6 %collective-permute-start.24 = (f32[1,128,8,128]{3,2,1,0:T(8,128)S(1)}, f32[1,128,8,128]{3,2,1,0:T(8,128)S(1)}, u32[]{:S(2)}, u32[]{:S(2)}) collective-permute-start(f32[1,128,8,128]{3,2,1,0:T(8,128)S(1)} %bitcast.11), channel_id=1, source_target_pairs={{0,4},{4,8},{8,12},{12,16},{16,20},{20,24},{24,28},{28,32},{32,36}... | collective-permute-start | bytes 1572872 | tf_op jit(solution)/shard_map/ppermute | solution.py:455
  179.8 10.6 %collective-permute-start.22 = (f32[1,1,8,128]{3,2,1,0:T(8,128)S(1)}, f32[1,1,8,128]{3,2,1,0:T(8,128)S(1)}, u32[]{:S(2)}, u32[]{:S(2)}) collective-permute-start(f32[1,1,8,128]{3,2,1,0:T(8,128)S(1)} %get-tuple-element.109), channel_id=1, source_target_pairs={{0,1},{1,0},{2,3},{3,2},{4,5},{5,4},{6,7},{7,6},{8,9},{9,8},{10,11... | collective-permute-start | bytes 12296 | tf_op jit(solution)/shard_map/ppermute | solution.py:476
  184.0 11.3 %collective-permute-start.23 = (f32[1,1,8,128]{3,2,1,0:T(8,128)S(1)}, f32[1,1,8,128]{3,2,1,0:T(8,128)S(1)}, u32[]{:S(2)}, u32[]{:S(2)}) collective-permute-start(f32[1,1,8,128]{3,2,1,0:T(8,128)S(1)} %get-tuple-element.108), channel_id=1, source_target_pairs={{1,2},{2,1},{5,6},{6,5},{9,10},{10,9},{13,14},{14,13},{17,18},{18,... | collective-permute-start | bytes 12296 | tf_op jit(solution)/shard_map/ppermute | solution.py:477
  197.9 6.5 %collective-permute-start.25 = (f32[1,1,8,128]{3,2,1,0:T(8,128)S(1)}, f32[1,1,8,128]{3,2,1,0:T(8,128)S(1)}, u32[]{:S(2)}, u32[]{:S(2)}) collective-permute-start(f32[1,1,8,128]{3,2,1,0:T(8,128)S(1)} %get-tuple-element.97), channel_id=1, source_target_pairs={{0,1},{1,0},{2,3},{3,2},{4,5},{5,4},{6,7},{7,6},{8,9},{9,8},{10,11... | collective-permute-start | bytes 12296 | tf_op jit(solution)/shard_map/ppermute | solution.py:476
  198.0 23.6 %collective-permute-start.29 = (f32[1,128,8,128]{3,2,1,0:T(8,128)S(1)}, f32[1,128,8,128]{3,2,1,0:T(8,128)S(1)}, u32[]{:S(2)}, u32[]{:S(2)}) collective-permute-start(f32[1,128,8,128]{3,2,1,0:T(8,128)S(1)} %get-tuple-element.96.y1), channel_id=1, source_target_pairs={{0,4},{4,8},{8,12},{12,16},{16,20},{20,24},{24,28},{28,32},{32,36}... | collective-permute-start | bytes 1572872 | tf_op jit(solution)/shard_map/ppermute | solution.py:455
  199.9 15.0 %collective-permute-start.26 = (f32[1,1,8,128]{3,2,1,0:T(8,128)S(1)}, f32[1,1,8,128]{3,2,1,0:T(8,128)S(1)}, u32[]{:S(2)}, u32[]{:S(2)}) collective-permute-start(f32[1,1,8,128]{3,2,1,0:T(8,128)S(1)} %get-tuple-element.98), channel_id=1, source_target_pairs={{1,2},{2,1},{5,6},{6,5},{9,10},{10,9},{13,14},{14,13},{17,18},{18,... | collective-permute-start | bytes 12296 | tf_op jit(solution)/shard_map/ppermute | solution.py:477
  217.5 17.9 %collective-permute-start.32 = (f32[1,128,8,128]{3,2,1,0:T(8,128)S(1)}, f32[1,128,8,128]{3,2,1,0:T(8,128)S(1)}, u32[]{:S(2)}, u32[]{:S(2)}) collective-permute-start(f32[1,128,8,128]{3,2,1,0:T(8,128)S(1)} %get-tuple-element.103.z1), channel_id=1, source_target_pairs={{0,4},{4,8},{8,12},{12,16},{16,20},{20,24},{24,28},{28,32},{32,36}... | collective-permute-start | bytes 1572872 | tf_op jit(solution)/shard_map/ppermute | solution.py:455
  219.5 7.0 %collective-permute-start.28 = (f32[2,1,8,128]{3,2,1,0:T(8,128)S(1)}, f32[2,1,8,128]{3,2,1,0:T(8,128)S(1)}, u32[]{:S(2)}, u32[]{:S(2)}) collective-permute-start(f32[2,1,8,128]{3,2,1,0:T(8,128)S(1)} %get-tuple-element.101), channel_id=1, source_target_pairs={{1,2},{2,1},{5,6},{6,5},{9,10},{10,9},{13,14},{14,13},{17,18},{18,... | collective-permute-start | bytes 24584 | tf_op jit(solution)/shard_map/ppermute | solution.py:477
  227.7 7.7 %collective-permute-start.30 = (f32[1,1,8,128]{3,2,1,0:T(8,128)S(1)}, f32[1,1,8,128]{3,2,1,0:T(8,128)S(1)}, u32[]{:S(2)}, u32[]{:S(2)}) collective-permute-start(f32[1,1,8,128]{3,2,1,0:T(8,128)S(1)} %get-tuple-element.105), channel_id=1, source_target_pairs={{0,1},{1,0},{2,3},{3,2},{4,5},{5,4},{6,7},{7,6},{8,9},{9,8},{10,11... | collective-permute-start | bytes 12296 | tf_op jit(solution)/shard_map/ppermute | solution.py:476
  227.8 7.6 %collective-permute-start.31 = (f32[1,1,8,128]{3,2,1,0:T(8,128)S(1)}, f32[1,1,8,128]{3,2,1,0:T(8,128)S(1)}, u32[]{:S(2)}, u32[]{:S(2)}) collective-permute-start(f32[1,1,8,128]{3,2,1,0:T(8,128)S(1)} %get-tuple-element.106), channel_id=1, source_target_pairs={{1,2},{2,1},{5,6},{6,5},{9,10},{10,9},{13,14},{14,13},{17,18},{18,... | collective-permute-start | bytes 12296 | tf_op jit(solution)/shard_map/ppermute | solution.py:477
  (12 other events, 40.8 us)
